TPU v7x, 32 devices: a whole 2x2x4 slice. The times are simulated.
32 devices in a mesh: wide: 8 (over y, x, core), narrow: 4 (over z).
Axes of the slice: x: 2, y: 2, z: 4, core: 2. Of those that a mesh axis runs over, the one named last changes fastest.
Arguments:
- inputs: bfloat16 [8192, 1024], P(('wide', 'narrow')), may hold values from -6 to 6
- memory: bfloat16 [64, 1024, 1024], P(('wide', 'narrow')), may hold values from -6 to 6
- mem_lengths: int32 [64], P(('wide', 'narrow')), may hold values from 1 to 1024, 40960 in all
- self_qkv: bfloat16 [3, 1024, 1024], P(None, ('wide', 'narrow')), may hold values from -0.1875 to 0.1875
- self_out: bfloat16 [1024, 1024], P(('wide', 'narrow')), may hold values from -0.5 to 0.5
- self_bias: bfloat16 [4, 1024], P(None, ('wide', 'narrow')), may hold values from -3 to 3
- self_gain: bfloat16 [1024], P(('wide', 'narrow')), may hold values from 0.25 to 1.75
- cross_qkv: bfloat16 [3, 1024, 1024], P(None, ('wide', 'narrow')), may hold values from -0.1875 to 0.1875
- cross_out: bfloat16 [1024, 1024], P(('wide', 'narrow')), may hold values from -1 to 1
- cross_bias: bfloat16 [4, 1024], P(None, ('wide', 'narrow')), may hold values from -3 to 3
- cross_gain: bfloat16 [1024], P(('wide', 'narrow')), may hold values from 0.25 to 1.75
- ffn_in: bfloat16 [1024, 4096], P(('wide', 'narrow')), may hold values from -0.1875 to 0.1875
- ffn_out: bfloat16 [4096, 1024], P(('wide', 'narrow')), may hold values from -0.09375 to 0.09375
- ffn_bias_in: bfloat16 [4096], P(('wide', 'narrow')), may hold values from -3 to 3
- ffn_bias_out: bfloat16 [2, 1024], P(None, ('wide', 'narrow')), may hold values from -3 to 3
- ffn_gain: bfloat16 [1024], P(('wide', 'narrow')), may hold values from 0.25 to 1.75
- out_grad: bfloat16 [8192, 1024], P(('wide', 'narrow')), may hold values from -6 to 6
Outputs:
- layer_out: bfloat16 [8192, 1024], P(('wide', 'narrow'))
- input_grad: float32 [8192, 1024], P(('wide', 'narrow'))
- memory_grad: float32 [64, 1024, 1024], P(('wide', 'narrow'))
- self_qkv_grad: float32 [3, 1024, 1024], P(None, ('wide', 'narrow'))
- self_out_grad: float32 [1024, 1024], P(('wide', 'narrow'))
- self_bias_grad: float32 [4, 1024], P(None, ('wide', 'narrow'))
- self_gain_grad: float32 [1024], P(('wide', 'narrow'))
- cross_qkv_grad: float32 [3, 1024, 1024], P(None, ('wide', 'narrow'))
- cross_out_grad: float32 [1024, 1024], P(('wide', 'narrow'))
- cross_bias_grad: float32 [4, 1024], P(None, ('wide', 'narrow'))
- cross_gain_grad: float32 [1024], P(('wide', 'narrow'))
- ffn_in_grad: float32 [1024, 4096], P(('wide', 'narrow'))
- ffn_out_grad: float32 [4096, 1024], P(('wide', 'narrow'))
- ffn_bias_in_grad: float32 [4096], P(('wide', 'narrow'))
- ffn_bias_out_grad: float32 [2, 1024], P(None, ('wide', 'narrow'))
- ffn_gain_grad: float32 [1024], P(('wide', 'narrow'))
Inputs may be any that keep to these rules, and one draw needn't show every extreme that they name: Item b's first mem_lengths[b] memory slots are live, the rest padding; the longest item has exactly 1024.
All inputs are finite; a program needn't handle non-finite values. No bound on the sum of `mem_lengths` on one device may be relied on, other than what follows from the above.
Results may differ from a plain program's by a relative error of at most 0.02.
The roundings to bfloat16 on the way count: a program that leaves them out, or rounds other values in their place, can miss the bound.
Values may be sent and summed in bfloat16 or wider, within the bound.
No kernel may reach another device: no remote copies, remote signals or barrier semaphores. Data moves between devices by JAX's collectives and lax.ppermute only.
A program may use at most 256 MiB of HBM per device.

v0:
```python
import jax
import jax.numpy as jnp
from jax import lax
from jax.sharding import PartitionSpec as P

HD = 64


EPSILON = 1e-05
MASKED = -1e30


def project(left_rows, weight):
    return jnp.dot(left_rows, weight, preferred_element_type=jnp.float32)


def project_back(gradient, weight):
    return lax.dot_general(
        gradient, weight, (((1,), (1,)), ((), ())), preferred_element_type=jnp.float32
    )


def weight_grad(left_rows, gradient):
    return lax.dot_general(
        left_rows, gradient, (((0,), (0,)), ((), ())), preferred_element_type=jnp.float32
    )


def column_sums(gradient):
    return jnp.sum(gradient.astype(jnp.float32), axis=0)


def layer_norm(hidden, gain_row, shift_row):
    average = jnp.mean(hidden, axis=-1, keepdims=True)
    centred = hidden - average
    variance = jnp.mean(centred * centred, axis=-1, keepdims=True)
    return centred * lax.rsqrt(variance + EPSILON) * gain_row + shift_row


def gelu_exact(pre_gelu):
    return jax.nn.gelu(pre_gelu, approximate=False)


def to_flat(grad_array, dim):
    return jnp.moveaxis(grad_array, dim, 0).reshape(-1, 128)


def from_flat(piece, full_shape, dim, share_count):
    moved = list(full_shape)
    moved.insert(0, moved.pop(dim))
    moved[0] = moved[0] // share_count
    return jnp.moveaxis(piece.reshape(tuple(moved)), 0, dim)


def attend(queries, key_rows, values, allowed):
    scores = jnp.einsum("thd,shd->hts", queries, key_rows, preferred_element_type=jnp.float32)
    scores = jnp.where(allowed, scores, MASKED)
    log_total = jax.nn.logsumexp(scores, axis=-1, keepdims=True)
    chances = jnp.exp(scores - log_total).astype(jnp.bfloat16)
    context = jnp.einsum("hts,shd->thd", chances, values, preferred_element_type=jnp.float32)
    return (context.astype(jnp.bfloat16), log_total)


def attend_back(queries, key_rows, values, log_total, d_context, allowed):
    scores = jnp.einsum("thd,shd->hts", queries, key_rows, preferred_element_type=jnp.float32)
    scores = jnp.where(allowed, scores, MASKED)
    chances = jnp.exp(scores - log_total)
    d_chances = jnp.einsum("thd,shd->hts", d_context, values, preferred_element_type=jnp.float32)
    d_scores = (
        chances * (d_chances - jnp.sum(d_chances * chances, axis=-1, keepdims=True))
    ).astype(jnp.bfloat16)
    d_queries = jnp.einsum("hts,shd->thd", d_scores, key_rows, preferred_element_type=jnp.float32)
    d_keys = jnp.einsum("hts,thd->shd", d_scores, queries, preferred_element_type=jnp.float32)
    d_values = jnp.einsum(
        "hts,thd->shd", chances.astype(jnp.bfloat16), d_context, preferred_element_type=jnp.float32
    )
    return (
        d_queries.astype(jnp.bfloat16),
        d_keys.astype(jnp.bfloat16),
        d_values.astype(jnp.bfloat16),
    )


def local(
    inputs,
    memory,
    mem_lengths,
    self_qkv,
    self_out,
    self_bias,
    self_gain,
    cross_qkv,
    cross_out,
    cross_bias,
    cross_gain,
    ffn_in,
    ffn_out,
    ffn_bias_in,
    ffn_bias_out,
    ffn_gain,
    out_grad,
):
    scaling = HD ** (-0.5)
    item_count = memory.shape[0]
    mem_slots = memory.shape[1]
    model_width = inputs.shape[1]
    row_count = inputs.shape[0]
    seq_len = row_count // item_count
    head_count = model_width // HD
    head_split = (item_count, seq_len, head_count, HD)
    mem_split = (item_count, mem_slots, head_count, HD)
    causal = lax.broadcasted_iota(jnp.int32, (seq_len, seq_len), 0) >= lax.broadcasted_iota(
        jnp.int32, (seq_len, seq_len), 1
    )
    key_slots = lax.broadcasted_iota(jnp.int32, (1, mem_slots), 1)
    inputs_f = inputs.astype(jnp.float32)
    wide_count = lax.axis_size("wide")
    narrow_count = lax.axis_size("narrow")
    share_count = wide_count * narrow_count
    sqkv, sout, sbias, sgain = (
        lax.all_gather(self_qkv, ("wide", "narrow"), axis=1, tiled=True),
        lax.all_gather(self_out, ("wide", "narrow"), axis=0, tiled=True),
        lax.all_gather(self_bias, ("wide", "narrow"), axis=1, tiled=True),
        lax.all_gather(self_gain, ("wide", "narrow"), axis=0, tiled=True),
    )
    sbias_f = sbias.astype(jnp.float32)
    queries = (
        ((project(inputs, sqkv[0]) + sbias_f[0]) * scaling).astype(jnp.bfloat16).reshape(head_split)
    )
    key_rows = project(inputs, sqkv[1]).astype(jnp.bfloat16).reshape(head_split)
    values = (project(inputs, sqkv[2]) + sbias_f[1]).astype(jnp.bfloat16).reshape(head_split)
    self_ctx, self_lse = jax.vmap(attend, in_axes=(0, 0, 0, None))(
        queries, key_rows, values, causal
    )
    self_flat = self_ctx.reshape(row_count, model_width)
    first_pre = inputs_f + (project(self_flat, sout) + sbias_f[2])
    first = layer_norm(first_pre, sgain.astype(jnp.float32), sbias_f[3])
    first_low = first.astype(jnp.bfloat16)
    cqkv, cout, cbias, cgain = (
        lax.all_gather(cross_qkv, ("wide", "narrow"), axis=1, tiled=True),
        lax.all_gather(cross_out, ("wide", "narrow"), axis=0, tiled=True),
        lax.all_gather(cross_bias, ("wide", "narrow"), axis=1, tiled=True),
        lax.all_gather(cross_gain, ("wide", "narrow"), axis=0, tiled=True),
    )
    cbias_f = cbias.astype(jnp.float32)
    queries_two = (
        ((project(first_low, cqkv[0]) + cbias_f[0]) * scaling)
        .astype(jnp.bfloat16)
        .reshape(head_split)
    )
    mem_flat = memory.reshape(item_count * mem_slots, model_width)
    mem_keys = project(mem_flat, cqkv[1]).astype(jnp.bfloat16).reshape(mem_split)
    mem_values = (project(mem_flat, cqkv[2]) + cbias_f[1]).astype(jnp.bfloat16).reshape(mem_split)

    def cross_item(packed):
        item_q, item_k, item_v, item_len = packed
        return attend(item_q, item_k, item_v, key_slots < item_len)

    cross_ctx, cross_lse = lax.map(cross_item, (queries_two, mem_keys, mem_values, mem_lengths))
    cross_flat = cross_ctx.reshape(row_count, model_width)
    second_pre = first + (project(cross_flat, cout) + cbias_f[2])
    second = layer_norm(second_pre, cgain.astype(jnp.float32), cbias_f[3])
    second_low = second.astype(jnp.bfloat16)
    fin, fout, fbin, fbout, fgain = (
        lax.all_gather(ffn_in, ("wide", "narrow"), axis=0, tiled=True),
        lax.all_gather(ffn_out, ("wide", "narrow"), axis=0, tiled=True),
        lax.all_gather(ffn_bias_in, ("wide", "narrow"), axis=0, tiled=True),
        lax.all_gather(ffn_bias_out, ("wide", "narrow"), axis=1, tiled=True),
        lax.all_gather(ffn_gain, ("wide", "narrow"), axis=0, tiled=True),
    )
    hidden_low = gelu_exact(project(second_low, fin) + fbin.astype(jnp.float32)).astype(
        jnp.bfloat16
    )
    third_pre = second + (project(hidden_low, fout) + fbout.astype(jnp.float32)[0])
    layer_out = layer_norm(third_pre, fgain.astype(jnp.float32), fbout.astype(jnp.float32)[1])
    fin_b, fout_b, fbin_b, fbout_b, fgain_b = (
        lax.all_gather(ffn_in, ("wide", "narrow"), axis=0, tiled=True),
        lax.all_gather(ffn_out, ("wide", "narrow"), axis=0, tiled=True),
        lax.all_gather(ffn_bias_in, ("wide", "narrow"), axis=0, tiled=True),
        lax.all_gather(ffn_bias_out, ("wide", "narrow"), axis=1, tiled=True),
        lax.all_gather(ffn_gain, ("wide", "narrow"), axis=0, tiled=True),
    )
    _, norm_pull = jax.vjp(
        layer_norm, third_pre, fgain_b.astype(jnp.float32), fbout_b.astype(jnp.float32)[1]
    )
    d_third, g_fgain, g_fshift = norm_pull(out_grad.astype(jnp.float32))
    e_three = d_third.astype(jnp.bfloat16)
    hidden_again, gelu_pull = jax.vjp(
        gelu_exact, project(second_low, fin_b) + fbin_b.astype(jnp.float32)
    )
    g_fout = weight_grad(hidden_again.astype(jnp.bfloat16), e_three)
    g_fbout = jnp.stack([column_sums(e_three), g_fshift])
    d_pre = gelu_pull(project_back(e_three, fout_b))[0].astype(jnp.bfloat16)
    g_fin = weight_grad(second_low, d_pre)
    g_fbin = column_sums(d_pre)
    d_second = d_third + project_back(d_pre, fin_b)
    fin_shape = g_fin.shape
    fout_shape = g_fout.shape
    ffn_parts = (
        lax.psum_scatter(to_flat(g_fin, 0), ("wide", "narrow"), scatter_dimension=0, tiled=True),
        lax.psum_scatter(to_flat(g_fout, 0), ("wide", "narrow"), scatter_dimension=0, tiled=True),
        lax.psum_scatter(g_fbin, ("wide", "narrow"), scatter_dimension=0, tiled=True),
        lax.psum_scatter(g_fbout, ("wide", "narrow"), scatter_dimension=1, tiled=True),
        lax.psum_scatter(g_fgain, ("wide", "narrow"), scatter_dimension=0, tiled=True),
    )
    ffn_sums = (
        from_flat(ffn_parts[0], fin_shape, 0, share_count),
        from_flat(ffn_parts[1], fout_shape, 0, share_count),
        ffn_parts[2],
        ffn_parts[3],
        ffn_parts[4],
    )
    cqkv_b, cout_b, cbias_b, cgain_b = (
        lax.all_gather(cross_qkv, ("wide", "narrow"), axis=1, tiled=True),
        lax.all_gather(cross_out, ("wide", "narrow"), axis=0, tiled=True),
        lax.all_gather(cross_bias, ("wide", "narrow"), axis=1, tiled=True),
        lax.all_gather(cross_gain, ("wide", "narrow"), axis=0, tiled=True),
    )
    _, norm_pull_two = jax.vjp(
        layer_norm, second_pre, cgain_b.astype(jnp.float32), cbias_b.astype(jnp.float32)[3]
    )
    d_second_pre, g_cgain, g_cshift = norm_pull_two(d_second)
    e_two = d_second_pre.astype(jnp.bfloat16)
    g_cout = weight_grad(cross_flat, e_two)
    d_cross_ctx = project_back(e_two, cout_b).astype(jnp.bfloat16).reshape(head_split)

    def cross_back(packed):
        item_q, item_k, item_v, item_lse, item_d, item_len = packed
        return attend_back(item_q, item_k, item_v, item_lse, item_d, key_slots < item_len)

    dq_two, dk_two, dv_two = lax.map(
        cross_back, (queries_two, mem_keys, mem_values, cross_lse, d_cross_ctx, mem_lengths)
    )
    dq_scaled = dq_two.reshape(row_count, model_width) * scaling
    dk_flat = dk_two.reshape(item_count * mem_slots, model_width)
    dv_flat = dv_two.reshape(item_count * mem_slots, model_width)
    g_cqkv = jnp.stack(
        [
            weight_grad(first_low, dq_scaled),
            weight_grad(mem_flat, dk_flat),
            weight_grad(mem_flat, dv_flat),
        ]
    )
    g_cbias = jnp.stack(
        [column_sums(dq_scaled), column_sums(dv_flat), column_sums(e_two), g_cshift]
    )
    memory_grad = (project_back(dk_flat, cqkv_b[1]) + project_back(dv_flat, cqkv_b[2])).reshape(
        item_count, mem_slots, model_width
    )
    d_first = d_second_pre + project_back(dq_scaled, cqkv_b[0])
    qkv_shape = g_cqkv.shape
    square_shape = g_cout.shape
    cross_parts = (
        lax.psum_scatter(to_flat(g_cqkv, 1), ("wide", "narrow"), scatter_dimension=0, tiled=True),
        lax.psum_scatter(to_flat(g_cout, 0), ("wide", "narrow"), scatter_dimension=0, tiled=True),
        lax.psum_scatter(g_cbias, ("wide", "narrow"), scatter_dimension=1, tiled=True),
        lax.psum_scatter(g_cgain, ("wide", "narrow"), scatter_dimension=0, tiled=True),
    )
    cross_sums = (
        from_flat(cross_parts[0], qkv_shape, 1, share_count),
        from_flat(cross_parts[1], square_shape, 0, share_count),
        cross_parts[2],
        cross_parts[3],
    )
    sqkv_b, sout_b, sbias_b, sgain_b = (
        lax.all_gather(self_qkv, ("wide", "narrow"), axis=1, tiled=True),
        lax.all_gather(self_out, ("wide", "narrow"), axis=0, tiled=True),
        lax.all_gather(self_bias, ("wide", "narrow"), axis=1, tiled=True),
        lax.all_gather(self_gain, ("wide", "narrow"), axis=0, tiled=True),
    )
    _, norm_pull_one = jax.vjp(
        layer_norm, first_pre, sgain_b.astype(jnp.float32), sbias_b.astype(jnp.float32)[3]
    )
    d_first_pre, g_sgain, g_sshift = norm_pull_one(d_first)
    e_one = d_first_pre.astype(jnp.bfloat16)
    g_sout = weight_grad(self_flat, e_one)
    d_self_ctx = project_back(e_one, sout_b).astype(jnp.bfloat16).reshape(head_split)
    dq_one, dk_one, dv_one = jax.vmap(attend_back, in_axes=(0, 0, 0, 0, 0, None))(
        queries, key_rows, values, self_lse, d_self_ctx, causal
    )
    dq_self = dq_one.reshape(row_count, model_width) * scaling
    dk_self = dk_one.reshape(row_count, model_width)
    dv_self = dv_one.reshape(row_count, model_width)
    g_sqkv = jnp.stack(
        [weight_grad(inputs, dq_self), weight_grad(inputs, dk_self), weight_grad(inputs, dv_self)]
    )
    g_sbias = jnp.stack([column_sums(dq_self), column_sums(dv_self), column_sums(e_one), g_sshift])
    input_grad = (
        d_first_pre
        + project_back(dq_self, sqkv_b[0])
        + project_back(dk_self, sqkv_b[1])
        + project_back(dv_self, sqkv_b[2])
    )
    self_parts = (
        lax.psum_scatter(to_flat(g_sqkv, 1), ("wide", "narrow"), scatter_dimension=0, tiled=True),
        lax.psum_scatter(to_flat(g_sout, 0), ("wide", "narrow"), scatter_dimension=0, tiled=True),
        lax.psum_scatter(g_sbias, ("wide", "narrow"), scatter_dimension=1, tiled=True),
        lax.psum_scatter(g_sgain, ("wide", "narrow"), scatter_dimension=0, tiled=True),
    )
    self_sums = (
        from_flat(self_parts[0], qkv_shape, 1, share_count),
        from_flat(self_parts[1], square_shape, 0, share_count),
        self_parts[2],
        self_parts[3],
    )
    return (
        layer_out.astype(jnp.bfloat16),
        input_grad,
        memory_grad,
        self_sums[0],
        self_sums[1],
        self_sums[2],
        self_sums[3],
        cross_sums[0],
        cross_sums[1],
        cross_sums[2],
        cross_sums[3],
        ffn_sums[0],
        ffn_sums[1],
        ffn_sums[2],
        ffn_sums[3],
        ffn_sums[4],
    )


def solution(mesh):
    placed = (
        P(("wide", "narrow"), None),
        P(("wide", "narrow"), None, None),
        P(("wide", "narrow")),
        P(None, ("wide", "narrow"), None),
        P(("wide", "narrow"), None),
        P(None, ("wide", "narrow")),
        P(("wide", "narrow")),
        P(None, ("wide", "narrow"), None),
        P(("wide", "narrow"), None),
        P(None, ("wide", "narrow")),
        P(("wide", "narrow")),
        P(("wide", "narrow"), None),
        P(("wide", "narrow"), None),
        P(("wide", "narrow")),
        P(None, ("wide", "narrow")),
        P(("wide", "narrow")),
        P(("wide", "narrow"), None),
    )
    return jax.shard_map(
        local,
        mesh=mesh,
        in_specs=placed,
        out_specs=(
            P(("wide", "narrow"), None),
            P(("wide", "narrow"), None),
            P(("wide", "narrow"), None, None),
            P(None, ("wide", "narrow"), None),
            P(("wide", "narrow"), None),
            P(None, ("wide", "narrow")),
            P(("wide", "narrow")),
            P(None, ("wide", "narrow"), None),
            P(("wide", "narrow"), None),
            P(None, ("wide", "narrow")),
            P(("wide", "narrow")),
            P(("wide", "narrow"), None),
            P(("wide", "narrow"), None),
            P(("wide", "narrow")),
            P(None, ("wide", "narrow")),
            P(("wide", "narrow")),
        ),
        check_vma=False,
    )
```

profile of v0, /device:TPU:0, one launch (start us, length us, event | category | flops | bytes accessed | tf_op | source)
XLA Modules:
  0.0 2287.6 jit_solution(9036056696846999073)
XLA Ops:
  11.2 70.9 %all-gather = bf16[32,32,4]{1,2,0:T(4,128)(2,1)S(1)} all-gather(bf16[1,32,4]{1,2,0:T(4,128)(2,1)} %bitcast.413), channel_id=1, replica_groups=mesh['wide'=8,'narrow'=4] {'wide','narrow'}, dimensions={0}, use_global_device_ids=true | all-gather | bytes 8448 | tf_op jit(solution)/shard_map/all_gather | solution.py:123
  84.8 37.1 %all-reduce.8 = (bf16[1024]{0:T(1024)(128)(2,1)S(1)}, bf16[1024]{0:T(1024)(128)(2,1)S(1)}, bf16[1024]{0:T(1024)(128)(2,1)S(1)}) all-reduce(bf16[1024]{0:T(1024)(128)(2,1)S(1)} %dynamic-update-slice, bf16[1024]{0:T(1024)(128)(2,1)S(1)} %dynamic-update-slice.1, ...), channel_id=1, replica_groups=mesh['wide'=8,'narrow'=4] {'wide','narrow'}, use_global_device_ids=true, to_apply=%add | all-reduce | flops 3072 | bytes 12288
  121.9 66.5 %all-gather.1 = bf16[32,32,4]{1,2,0:T(4,128)(2,1)S(1)} all-gather(bf16[1,32,4]{1,2,0:T(4,128)(2,1)} %bitcast.414), channel_id=1, replica_groups=mesh['wide'=8,'narrow'=4] {'wide','narrow'}, dimensions={0}, use_global_device_ids=true | all-gather | bytes 8448 | tf_op jit(solution)/shard_map/all_gather | solution.py:142
  188.6 64.3 %all-gather.2 = bf16[32,1,128]{2,1,0:T(2,128)(2,1)S(1)} all-gather(bf16[1,1,128]{2,1,0:T(2,128)(2,1)} %bitcast.415), channel_id=1, replica_groups=mesh['wide'=8,'narrow'=4] {'wide','narrow'}, dimensions={0}, use_global_device_ids=true | all-gather | bytes 8448 | tf_op jit(solution)/shard_map/all_gather | solution.py:167
  252.9 66.2 %all-gather.3 = bf16[32,32,2]{1,2,0:T(2,128)(2,1)S(1)} all-gather(bf16[1,32,2]{1,2,0:T(2,128)(2,1)} %bitcast.416), channel_id=1, replica_groups=mesh['wide'=8,'narrow'=4] {'wide','narrow'}, dimensions={0}, use_global_device_ids=true | all-gather | bytes 4224 | tf_op jit(solution)/shard_map/all_gather | solution.py:168
  352.2 11.6 reshape.363
  404.7 17.0 while.28
  425.3 16.3 multiply_convert_fusion.1
  451.0 12.7 convert_reduce_fusion.1
  471.5 33.6 %while.29 = (s32[]{:T(128)}, bf16[2,128,16,64]{1,3,2,0:T(8,128)(2,1)S(1)}, bf16[2,1024,16,64]{1,3,2,0:T(8,128)(2,1)}, bf16[2,1024,16,64]{1,3,2,0:T(8,128)(2,1)},...) while((s32[]{:T(128)}, ...), condition=%wide.region_18.19_spmd.clone, body=%wide.region_16.18_spmd.clone.sunk | while | flops 1369570304 | bytes 141886736 | solution.py:231
  585.2 21.8 copy.183
  607.0 20.1 reshape.325
  639.0 18.4 copy.180
  657.5 20.1 reshape.320
  688.7 18.0 reshape.330
  717.4 18.0 reshape.332
  736.1 38.6 %all-reduce.7 = (f32[1024]{0:T(1024)S(1)}, f32[1024]{0:T(1024)S(1)}, f32[4096]{0:T(1024)S(1)}, f32[1024]{0:T(1024)S(1)}) all-reduce(f32[1024]{0:T(1024)S(1)} %get-tuple-element.279, f32[1024]{0:T(1024)S(1)} %copy-done.71, f32[4096]{0:T(1024)S(1)} %copy-done.68, ...), channel_id=5, replica_groups=mesh['wide'=8,'narrow'=4] {'wide','narrow'}, use_global_device_ids=true, to_apply=%region_30.31.clone | all-reduce | flops 7168 | bytes 57344
  803.1 132.1 %reduce-scatter.28.cloned.1.call-done = f32[32,4]{1,0:T(8,128)} async-done(((f32[1024,4]{1,0:T(8,128)}), f32[32,4]{1,0:T(8,128)}) %reduce-scatter.28.cloned.1.call-update) | async-done | bytes 528
  936.6 146.4 %reduce-scatter.22.cloned.1.call-done = f32[256,128]{1,0:T(8,128)} async-done(((f32[8192,128]{1,0:T(8,128)}), f32[256,128]{1,0:T(8,128)}) %reduce-scatter.22.cloned.1.call-update) | async-done | bytes 131088 | tf_op jit(solution)/shard_map/reduce_scatter | solution.py:255
  1084.6 149.3 %reduce-scatter.18.cloned.1.call-done = f32[256,128]{1,0:T(8,128)} async-done(((f32[8192,128]{1,0:T(8,128)}), f32[256,128]{1,0:T(8,128)}) %reduce-scatter.18.cloned.1.call-update) | async-done | bytes 131088 | tf_op jit(solution)/shard_map/reduce_scatter | solution.py:296
  1235.5 157.8 %reduce-scatter.20.cloned.1.call-done = f32[768,128]{1,0:T(8,128)} async-done(((f32[24576,128]{1,0:T(8,128)}), f32[768,128]{1,0:T(8,128)}) %reduce-scatter.20.cloned.1.call-update) | async-done | bytes 393232 | tf_op jit(solution)/shard_map/reduce_scatter | solution.py:254
  1395.4 157.8 %reduce-scatter.16.cloned.1.call-done = f32[768,128]{1,0:T(8,128)} async-done(((f32[24576,128]{1,0:T(8,128)}), f32[768,128]{1,0:T(8,128)}) %reduce-scatter.16.cloned.1.call-update) | async-done | bytes 393232 | tf_op jit(solution)/shard_map/reduce_scatter | solution.py:295
  1555.2 359.5 %reduce-scatter.24.cloned.1.call-done = f32[1024,128]{1,0:T(8,128)} async-done(((f32[32768,128]{1,0:T(8,128)}), f32[1024,128]{1,0:T(8,128)}) %reduce-scatter.24.cloned.1.call-update) | async-done | bytes 524304 | tf_op jit(solution)/shard_map/reduce_scatter | solution.py:200
  1916.7 362.2 %reduce-scatter.26.cloned.1.call-done = f32[1024,128]{1,0:T(8,128)} async-done(((f32[32768,128]{1,0:T(8,128)}), f32[1024,128]{1,0:T(8,128)}) %reduce-scatter.26.cloned.1.call-update) | async-done | bytes 524304 | tf_op jit(solution)/shard_map/reduce_scatter | solution.py:201
  (377 shorter events, 306.0 us)
Async XLA Ops:
  7.2 312.1 %all-gather.11.cloned.1.call-start = ((), (), s32[]{:S(2)}) async-start(), calls=%async_computation.9 | async-start | bytes 6488064 | tf_op jit(solution)/shard_map/all_gather | solution.py:121
  7.9 327.4 %all-gather.13.cloned.1.call-start = ((), (), s32[]{:S(2)}) async-start(), calls=%async_computation.10 | async-start | bytes 2162688 | tf_op jit(solution)/shard_map/all_gather | solution.py:122
  8.7 329.6 %all-gather.15.cloned.1.call-start = ((), (), s32[]{:S(2)}) async-start(), calls=%async_computation.11 | async-start | bytes 6488064 | tf_op jit(solution)/shard_map/all_gather | solution.py:140
  9.4 412.9 %all-gather.17.cloned.1.call-start = ((), (), s32[]{:S(2)}) async-start(), calls=%async_computation.12 | async-start | bytes 2162688 | tf_op jit(solution)/shard_map/all_gather | solution.py:141
  10.0 415.3 %all-gather.19.cloned.1.call-start = ((), (), s32[]{:S(2)}) async-start(), calls=%async_computation.13 | async-start | bytes 8650752 | tf_op jit(solution)/shard_map/all_gather | solution.py:165
  10.6 431.1 %all-gather.21.cloned.1.call-start = ((), (), s32[]{:S(2)}) async-start(), calls=%async_computation.14 | async-start | bytes 8650752 | tf_op jit(solution)/shard_map/all_gather | solution.py:166
  11.1 789.2 %reduce-scatter.32.cloned.1.call-start = ((), (), s32[]{:S(2)}) async-start(), calls=%async_computation.23 | async-start | bytes 540672
  83.1 240.6 %copy-start.11 = (bf16[256,1024]{1,0:T(8,128)(2,1)S(1)}, bf16[256,1024]{1,0:T(8,128)(2,1)}, u32[]{:S(2)}) copy-start(bf16[256,1024]{1,0:T(8,128)(2,1)} %param.21) | copy-start | bytes 1572868
  121.9 300.4 %copy-start.55 = (f32[1024]{0:T(1024)}, f32[1024]{0:T(1024)S(1)}, u32[]{:S(2)}) copy-start(f32[1024]{0:T(1024)S(1)} %convert_element_type.179) | copy-start | bytes 12292
  188.6 278.5 %copy-start.51 = (f32[1024]{0:T(1024)}, f32[1024]{0:T(1024)S(1)}, u32[]{:S(2)}) copy-start(f32[1024]{0:T(1024)S(1)} %convert_element_type.185) | copy-start | bytes 12292
  319.2 103.1 %copy-start.57 = (f32[1,1024]{1,0:T(1,128)}, f32[1,1024]{1,0:T(1,128)S(1)}, u32[]{:S(2)}) copy-start(f32[1,1024]{1,0:T(1,128)S(1)} %get-tuple-element.352) | copy-start | bytes 12292
  319.3 122.4 %copy-start.53 = (f32[1,1024]{1,0:T(1,128)}, f32[1,1024]{1,0:T(1,128)S(1)}, u32[]{:S(2)}) copy-start(f32[1,1024]{1,0:T(1,128)S(1)} %get-tuple-element.348) | copy-start | bytes 12292
  337.9 84.4 %copy-start.5 = (f32[256,1024]{1,0:T(8,128)}, f32[256,1024]{1,0:T(8,128)S(1)}, u32[]{:S(2)}) copy-start(f32[256,1024]{1,0:T(8,128)S(1)} %get-tuple-element.361) | copy-start | bytes 3145732
  338.0 84.4 %copy-start.59 = (f32[256]{0:T(256)}, f32[256]{0:T(256)S(1)}, u32[]{:S(2)}) copy-start(f32[256]{0:T(256)S(1)} %broadcast_multiply_fusion.3) | copy-start | bytes 3076
  338.2 84.1 %copy-start.61 = (f32[256]{0:T(256)}, f32[256]{0:T(256)S(1)}, u32[]{:S(2)}) copy-start(f32[256]{0:T(256)S(1)} %fusion.141) | copy-start | bytes 3076
  531.9 269.8 %reduce-scatter.30.cloned.1.call-start = ((), (), s32[]{:S(2)}) async-start(), calls=%async_computation.22 | async-start | bytes 540672
  533.2 402.0 %reduce-scatter.28.cloned.1.call-start = ((), (), s32[]{:S(2)}) async-start(), calls=%async_computation.21 | async-start | bytes 540672
  534.3 548.6 %reduce-scatter.22.cloned.1.call-start = ((), (), s32[]{:S(2)}) async-start(), calls=%async_computation.18 | async-start | bytes 4325376 | tf_op jit(solution)/shard_map/reduce_scatter | solution.py:255
  542.1 691.8 %reduce-scatter.18.cloned.1.call-start = ((), (), s32[]{:S(2)}) async-start(), calls=%async_computation.16 | async-start | bytes 4325376 | tf_op jit(solution)/shard_map/reduce_scatter | solution.py:296
  550.9 842.3 %reduce-scatter.20.cloned.1.call-start = ((), (), s32[]{:S(2)}) async-start(), calls=%async_computation.17 | async-start | bytes 12976128 | tf_op jit(solution)/shard_map/reduce_scatter | solution.py:254
  627.2 925.9 %reduce-scatter.16.cloned.1.call-start = ((), (), s32[]{:S(2)}) async-start(), calls=%async_computation.15 | async-start | bytes 12976128 | tf_op jit(solution)/shard_map/reduce_scatter | solution.py:295
  677.6 1237.1 %reduce-scatter.24.cloned.1.call-start = ((), (), s32[]{:S(2)}) async-start(), calls=%async_computation.19 | async-start | bytes 17301504 | tf_op jit(solution)/shard_map/reduce_scatter | solution.py:200
  706.7 1572.2 %reduce-scatter.26.cloned.1.call-start = ((), (), s32[]{:S(2)}) async-start(), calls=%async_computation.20 | async-start | bytes 17301504 | tf_op jit(solution)/shard_map/reduce_scatter | solution.py:201
  735.4 44.1 %copy-start.24 = (f32[256,1024]{1,0:T(8,128)S(1)}, f32[256,1024]{1,0:T(8,128)}, u32[]{:S(2)}) copy-start(f32[256,1024]{1,0:T(8,128)} %copy-done.23) | copy-start | bytes 3145732
  (72 other events, 581.5 us)
Sparse Core Ops, SparseCore 0:
  11.0 72.0 all-gather.10
  86.0 55.0 all-gather.12
  144.1 68.1 all-gather.14
  215.1 55.0 all-gather.16
  272.9 75.9 all-gather.18
  351.7 75.7 all-gather.20
  532.0 133.3 reduce-scatter.31
  667.7 132.6 reduce-scatter.29
  802.6 132.5 reduce-scatter.27
  937.3 145.5 reduce-scatter.21
  1085.2 148.5 reduce-scatter.17
  1239.8 153.4 reduce-scatter.19
  1399.2 153.8 reduce-scatter.15
  1555.3 359.4 reduce-scatter.23
  1916.9 361.9 reduce-scatter.25
where the time goes:
time: 2300 us; the launch traced here: 2290 us
  waiting for transfers between devices  1470 us (64%)
  blocking collectives  344 us (15%)
  local copies, waits for them, and re-layouts  250 us (11%)
  matrix products  182 us (8%)
  other arithmetic  26.5 us (1%)
    reduce_scatter x1, waiting for transfers between devices, local(): lax.psum_scatter(to_flat(g_fout, 0), ('wide', 'narrow'), scatter_dimensio...  362 us
    reduce_scatter x1, waiting for transfers between devices, local(): lax.psum_scatter(to_flat(g_fin, 0), ('wide', 'narrow'), scatter_dimension...  360 us
    reduce_scatter x1, waiting for transfers between devices, local(): lax.psum_scatter(to_flat(g_cqkv, 1), ('wide', 'narrow'), scatter_dimensio...  158 us
    reduce_scatter x1, waiting for transfers between devices, local(): lax.psum_scatter(to_flat(g_sqkv, 1), ('wide', 'narrow'), scatter_dimensio...  158 us
    reduce_scatter x1, waiting for transfers between devices, local(): lax.psum_scatter(to_flat(g_sout, 0), ('wide', 'narrow'), scatter_dimensio...  149 us
    reduce_scatter x1, waiting for transfers between devices, local(): lax.psum_scatter(to_flat(g_cout, 0), ('wide', 'narrow'), scatter_dimensio...  146 us
    unnamed x18, waiting for transfers between devices  136 us
    reshape x6, local copies, waits for them, and re-layouts, to_flat(): return jnp.moveaxis(grad_array, dim, 0).reshape(-1, 128)  86.1 us
  transfers between devices with their start and end apart: 15, of which 7 were waited for; matrix products, arithmetic and copies ran while one was open for 16% of the time, Pallas kernels for 0%

commit v1 on v0

v1 whole, which is shorter than its diff:
```python
import jax
import jax.numpy as jnp
from jax import lax
from jax.sharding import PartitionSpec as P

HD = 64
EPSILON = 1e-05
MASKED = -1e30
AXES = ("wide", "narrow")
BF = jnp.bfloat16
F32 = jnp.float32


def project(left_rows, weight):
    return jnp.dot(left_rows, weight, preferred_element_type=F32)


def project_back(gradient, weight):
    return lax.dot_general(gradient, weight, (((1,), (1,)), ((), ())), preferred_element_type=F32)


def weight_grad(left_rows, gradient):
    return lax.dot_general(left_rows, gradient, (((0,), (0,)), ((), ())), preferred_element_type=F32)


def column_sums(gradient):
    return jnp.sum(gradient.astype(F32), axis=0)


def layer_norm(hidden, gain_row, shift_row):
    average = jnp.mean(hidden, axis=-1, keepdims=True)
    centred = hidden - average
    variance = jnp.mean(centred * centred, axis=-1, keepdims=True)
    return centred * lax.rsqrt(variance + EPSILON) * gain_row + shift_row


def gelu_exact(pre_gelu):
    return jax.nn.gelu(pre_gelu, approximate=False)


def attend(queries, key_rows, values, allowed):
    scores = jnp.einsum("thd,shd->hts", queries, key_rows, preferred_element_type=F32)
    scores = jnp.where(allowed, scores, MASKED)
    log_total = jax.nn.logsumexp(scores, axis=-1, keepdims=True)
    chances = jnp.exp(scores - log_total).astype(BF)
    context = jnp.einsum("hts,shd->thd", chances, values, preferred_element_type=F32)
    return (context.astype(BF), log_total)


def attend_back(queries, key_rows, values, log_total, d_context, allowed):
    scores = jnp.einsum("thd,shd->hts", queries, key_rows, preferred_element_type=F32)
    scores = jnp.where(allowed, scores, MASKED)
    chances = jnp.exp(scores - log_total)
    d_chances = jnp.einsum("thd,shd->hts", d_context, values, preferred_element_type=F32)
    d_scores = (
        chances * (d_chances - jnp.sum(d_chances * chances, axis=-1, keepdims=True))
    ).astype(BF)
    d_queries = jnp.einsum("hts,shd->thd", d_scores, key_rows, preferred_element_type=F32)
    d_keys = jnp.einsum("hts,thd->shd", d_scores, queries, preferred_element_type=F32)
    d_values = jnp.einsum("hts,thd->shd", chances.astype(BF), d_context, preferred_element_type=F32)
    return (d_queries.astype(BF), d_keys.astype(BF), d_values.astype(BF))


class Plan:
    def __init__(self):
        self.wide = lax.axis_size("wide")
        self.narrow = lax.axis_size("narrow")
        self.count = self.wide * self.narrow
        self.w = lax.axis_index("wide")
        self.z = lax.axis_index("narrow")
        self.me = self.w * self.narrow + self.z
        bits = self.wide.bit_length() - 1
        rest = [1 << b for b in range(1, bits)]
        half = len(rest) // 2
        self.xs, self.ys = rest[:half], rest[half:]
        self.zs = [1 << b for b in range(self.narrow.bit_length() - 1)]
        self.order = [r for r in range(self.wide) if r % 2 == 0] + [
            r for r in range(self.wide) if r % 2 == 1
        ]

    def swap(self, value, mask):
        return lax.ppermute(value, AXES, [(i, i ^ mask) for i in range(self.count)])

    def swap_wide(self, value, mask):
        return self.swap(value, mask * self.narrow)

    def bit(self, index, mask):
        return (index // mask) % 2

    def gather_z(self, part):
        k, rows, n = part.shape
        have = part.reshape(k, 1, rows, n)
        for mask in reversed(self.zs):
            other = self.swap(have, mask)
            mine_low = self.bit(self.z, mask) == 0
            low = jnp.where(mine_low, have, other)
            high = jnp.where(mine_low, other, have)
            have = jnp.stack([low, high], axis=2).reshape(k, -1, rows, n)
        return have.reshape(k, -1, n)

    def gather_wide(self, part, route):
        first, second = (self.xs, self.ys) if route == 0 else (self.ys, self.xs)
        pieces = {0: part}
        for mask in [*first, *second, 1]:
            pieces.update({r ^ mask: self.swap_wide(a, mask) for r, a in list(pieces.items())})
        return jnp.concatenate([pieces[r] for r in self.order], axis=1)

    def relative(self, rows):
        size = rows.shape[1] // self.wide
        return jnp.concatenate(
            [
                lax.dynamic_slice_in_dim(rows, (jnp.int32(r) ^ self.w) * size, size, axis=1)
                for r in self.order
            ],
            axis=1,
        )

    def natural(self, rows):
        size = rows.shape[1] // self.wide
        pieces = []
        for i in range(self.wide):
            r = jnp.int32(i) ^ self.w
            place = (r % 2) * (self.wide // 2) + r // 2
            pieces.append(lax.dynamic_slice_in_dim(rows, place * size, size, axis=1))
        return jnp.concatenate(pieces, axis=1)

    def scatter(self, left_rel, right, route):
        half = left_rel.shape[1] // 2
        keep = weight_grad(left_rel[:, :half], right).astype(BF)
        send = weight_grad(left_rel[:, half:], right).astype(BF)
        n = right.shape[1]
        blocks = self.wide // 2
        rows = half // blocks
        first, second = (self.xs, self.ys) if route == 0 else (self.ys, self.xs)
        acc = keep.astype(F32) + self.swap_wide(send, 1).astype(F32)
        bits = len(self.xs) + len(self.ys)
        acc = acc.reshape((2,) * bits + (rows, n))
        left = sorted((m for m in [*self.xs, *self.ys]), reverse=True)
        for mask in reversed([*first, *second]):
            axis = left.index(mask)
            left.pop(axis)
            keep = lax.index_in_dim(acc, 0, axis, keepdims=False)
            send = lax.index_in_dim(acc, 1, axis, keepdims=False).astype(BF)
            acc = keep + self.swap_wide(send, mask).astype(F32)
        own = rows // self.narrow
        acc = acc.reshape((2,) * len(self.zs) + (own, n))
        for mask in self.zs:
            axis = len(acc.shape) - 3
            place = self.bit(self.z, mask)
            keep = lax.dynamic_index_in_dim(acc, place, axis, keepdims=False)
            send = lax.dynamic_index_in_dim(acc, 1 - place, axis, keepdims=False).astype(BF)
            acc = keep + self.swap(send, mask).astype(F32)
        return acc

    def gather_small(self, vector):
        n = vector.shape[0]
        have = vector.reshape(1, n // 128, 128)
        masks = [1 << b for b in range(self.count.bit_length() - 1)]
        for mask in masks:
            other = self.swap(have, mask)
            low = self.bit(self.me, mask) == 0
            have = jnp.concatenate(
                [jnp.where(low, have, other), jnp.where(low, other, have)], axis=0
            )
        return have.reshape(self.count, n)

    def scatter_small(self, table):
        n = table.shape[1]
        have = table.reshape(self.count, n // 128, 128)
        masks = [1 << b for b in range(self.count.bit_length() - 1)]
        for mask in reversed(masks):
            size = mask
            place = self.bit(self.me, mask)
            keep = lax.dynamic_slice_in_dim(have, place * size, size, axis=0)
            send = lax.dynamic_slice_in_dim(have, (1 - place) * size, size, axis=0)
            have = keep + self.swap(send, mask)
        return have.reshape(n)


def pack(vectors, parts):
    rows = []
    for v in vectors:
        lead = v.reshape(-1, parts, v.shape[-1] // parts)
        rows.append(jnp.moveaxis(lead, 1, 0).reshape(parts, -1))
    table = jnp.concatenate(rows, axis=1)
    return jnp.pad(table, ((0, 0), (0, -table.shape[1] % 1024)))


def unpack(table, shapes):
    parts, at, found = table.shape[0], 0, []
    for shape in shapes:
        size = 1
        for d in shape:
            size *= d
        piece = table[:, at : at + size].reshape((parts,) + shape)
        piece = jnp.moveaxis(piece, 0, -2)
        found.append(piece.reshape(shape[:-1] + (parts * shape[-1],)))
        at += size
    return found


def local(
    inputs,
    memory,
    mem_lengths,
    self_qkv,
    self_out,
    self_bias,
    self_gain,
    cross_qkv,
    cross_out,
    cross_bias,
    cross_gain,
    ffn_in,
    ffn_out,
    ffn_bias_in,
    ffn_bias_out,
    ffn_gain,
    out_grad,
):
    plan = Plan()
    scaling = HD ** (-0.5)
    item_count, mem_slots, model_width = memory.shape
    row_count = inputs.shape[0]
    seq_len = row_count // item_count
    head_count = model_width // HD
    head_split = (item_count, seq_len, head_count, HD)
    mem_split = (item_count, mem_slots, head_count, HD)
    causal = lax.broadcasted_iota(jnp.int32, (seq_len, seq_len), 0) >= lax.broadcasted_iota(
        jnp.int32, (seq_len, seq_len), 1
    )
    key_slots = lax.broadcasted_iota(jnp.int32, (1, mem_slots), 1)
    inputs_f = inputs.astype(F32)

    vectors = [self_bias, self_gain, cross_bias, cross_gain, ffn_bias_in, ffn_bias_out, ffn_gain]
    small = pack([v for v in vectors], 1)[0]
    table = plan.gather_small(small)
    sbias, sgain, cbias, cgain, fbin, fbout, fgain = unpack(
        table.astype(F32), [v.shape for v in vectors]
    )
    self_z = plan.gather_z(jnp.concatenate([self_qkv, self_out[None]], axis=0))
    sqk = plan.gather_wide(self_z[:2], 0)
    svo = plan.gather_wide(self_z[2:], 1)
    cross_z = plan.gather_z(jnp.concatenate([cross_qkv, cross_out[None]], axis=0))
    cqk = plan.gather_wide(cross_z[:2], 0)
    cvo = plan.gather_wide(cross_z[2:], 1)
    fin = plan.gather_wide(plan.gather_z(ffn_in[None]), 0)[0]
    fout = plan.gather_wide(plan.gather_z(ffn_out[None]), 1)[0]

    x_rel = plan.relative(inputs)
    queries = (((project(x_rel, sqk[0]) + sbias[0]) * scaling).astype(BF)).reshape(head_split)
    key_rows = project(x_rel, sqk[1]).astype(BF).reshape(head_split)
    values = (project(x_rel, svo[0]) + sbias[1]).astype(BF).reshape(head_split)
    self_ctx, self_lse = jax.vmap(attend, in_axes=(0, 0, 0, None))(
        queries, key_rows, values, causal
    )
    self_rel = plan.relative(self_ctx.reshape(row_count, model_width))
    first_pre = inputs_f + (project(self_rel, svo[1]) + sbias[2])
    first = layer_norm(first_pre, sgain, sbias[3])
    first_rel = plan.relative(first.astype(BF))

    queries_two = (
        ((project(first_rel, cqk[0]) + cbias[0]) * scaling).astype(BF).reshape(head_split)
    )
    mem_rel = plan.relative(memory.reshape(item_count * mem_slots, model_width))
    mem_keys = project(mem_rel, cqk[1]).astype(BF).reshape(mem_split)
    mem_values = (project(mem_rel, cvo[0]) + cbias[1]).astype(BF).reshape(mem_split)

    def cross_item(packed):
        item_q, item_k, item_v, item_len = packed
        return attend(item_q, item_k, item_v, key_slots < item_len)

    cross_ctx, cross_lse = lax.map(cross_item, (queries_two, mem_keys, mem_values, mem_lengths))
    cross_rel = plan.relative(cross_ctx.reshape(row_count, model_width))
    second_pre = first + (project(cross_rel, cvo[1]) + cbias[2])
    second = layer_norm(second_pre, cgain, cbias[3])
    second_rel = plan.relative(second.astype(BF))

    pre_gelu = project(second_rel, fin) + fbin
    hidden, gelu_pull = jax.vjp(gelu_exact, pre_gelu)
    hidden_rel = plan.relative(hidden.astype(BF))
    third_pre = second + (project(hidden_rel, fout) + fbout[0])
    layer_out, norm_pull = jax.vjp(layer_norm, third_pre, fgain, fbout[1])

    d_third, g_fgain, g_fshift = norm_pull(out_grad.astype(F32))
    e_three = d_third.astype(BF)
    g_fout = plan.scatter(hidden_rel, e_three, 1)
    d_pre = gelu_pull(plan.natural(project_back(e_three, fout)))[0].astype(BF)
    g_fin = plan.scatter(second_rel, d_pre, 0)
    g_fbin = column_sums(d_pre)
    g_fbout = jnp.stack([column_sums(e_three), g_fshift])
    d_second = d_third + plan.natural(project_back(d_pre, fin))

    _, norm_pull_two = jax.vjp(layer_norm, second_pre, cgain, cbias[3])
    d_second_pre, g_cgain, g_cshift = norm_pull_two(d_second)
    e_two = d_second_pre.astype(BF)
    g_cout = plan.scatter(cross_rel, e_two, 1)
    d_cross_ctx = plan.natural(project_back(e_two, cvo[1]).astype(BF)).reshape(head_split)

    def cross_back(packed):
        item_q, item_k, item_v, item_lse, item_d, item_len = packed
        return attend_back(item_q, item_k, item_v, item_lse, item_d, key_slots < item_len)

    dq_two, dk_two, dv_two = lax.map(
        cross_back, (queries_two, mem_keys, mem_values, cross_lse, d_cross_ctx, mem_lengths)
    )
    dq_scaled = dq_two.reshape(row_count, model_width) * scaling
    dk_flat = dk_two.reshape(item_count * mem_slots, model_width)
    dv_flat = dv_two.reshape(item_count * mem_slots, model_width)
    g_cv = plan.scatter(mem_rel, dv_flat, 1)
    g_ck = plan.scatter(mem_rel, dk_flat, 0)
    g_cq = plan.scatter(first_rel, dq_scaled, 0)
    g_cbias = jnp.stack(
        [column_sums(dq_scaled), column_sums(dv_flat), column_sums(e_two), g_cshift]
    )
    memory_grad = plan.natural(
        project_back(dk_flat, cqk[1]) + project_back(dv_flat, cvo[0])
    ).reshape(item_count, mem_slots, model_width)
    d_first = d_second_pre + plan.natural(project_back(dq_scaled, cqk[0]))

    _, norm_pull_one = jax.vjp(layer_norm, first_pre, sgain, sbias[3])
    d_first_pre, g_sgain, g_sshift = norm_pull_one(d_first)
    e_one = d_first_pre.astype(BF)
    g_sout = plan.scatter(self_rel, e_one, 1)
    d_self_ctx = plan.natural(project_back(e_one, svo[1]).astype(BF)).reshape(head_split)
    dq_one, dk_one, dv_one = jax.vmap(attend_back, in_axes=(0, 0, 0, 0, 0, None))(
        queries, key_rows, values, self_lse, d_self_ctx, causal
    )
    dq_self = dq_one.reshape(row_count, model_width) * scaling
    dk_self = dk_one.reshape(row_count, model_width)
    dv_self = dv_one.reshape(row_count, model_width)
    g_sv = plan.scatter(x_rel, dv_self, 1)
    g_sk = plan.scatter(x_rel, dk_self, 0)
    g_sq = plan.scatter(x_rel, dq_self, 0)
    g_sbias = jnp.stack([column_sums(dq_self), column_sums(dv_self), column_sums(e_one), g_sshift])
    input_grad = d_first_pre + plan.natural(
        project_back(dq_self, sqk[0])
        + project_back(dk_self, sqk[1])
        + project_back(dv_self, svo[0])
    )

    grads = [g_sbias, g_sgain, g_cbias, g_cgain, g_fbin, g_fbout, g_fgain]
    sums = plan.scatter_small(pack(grads, plan.count))
    found = unpack(sums[None], [v.shape for v in vectors])
    return (
        layer_out.astype(BF),
        input_grad,
        memory_grad,
        jnp.stack([g_sq, g_sk, g_sv]),
        g_sout,
        found[0],
        found[1],
        jnp.stack([g_cq, g_ck, g_cv]),
        g_cout,
        found[2],
        found[3],
        g_fin,
        g_fout,
        found[4],
        found[5],
        found[6],
    )


def solution(mesh):
    both = ("wide", "narrow")
    placed = (
        P(both, None),
        P(both, None, None),
        P(both),
        P(None, both, None),
        P(both, None),
        P(None, both),
        P(both),
        P(None, both, None),
        P(both, None),
        P(None, both),
        P(both),
        P(both, None),
        P(both, None),
        P(both),
        P(None, both),
        P(both),
        P(both, None),
    )
    return jax.shard_map(
        local,
        mesh=mesh,
        in_specs=placed,
        out_specs=(
            P(both, None),
            P(both, None),
            P(both, None, None),
            P(None, both, None),
            P(both, None),
            P(None, both),
            P(both),
            P(None, both, None),
            P(both, None),
            P(None, both),
            P(both),
            P(both, None),
            P(both, None),
            P(both),
            P(None, both),
            P(both),
        ),
        check_vma=False,
    )
```

time: 2300 us -> 830 us (0.36)
  waiting for transfers between devices: 1470 us -> 294 us
  blocking collectives: 344 us -> 0 us
  starting transfers between devices: 0.77 us -> 95.6 us
  local copies, waits for them, and re-layouts: 250 us -> 220 us
    reduce_scatter x6 -> x0, waiting for transfers between devices: 1330 us -> none  [the longest x1 362 us: local(): lax.psum_scatter(to_flat(g_fout, 0), ('wide', 'narrow'), scatter_dimensio...]
    ppermute x0 -> x110, waiting for transfers between devices: none -> 294 us  [swap(): return lax.ppermute(value, AXES, [(i, i ^ mask) for i in range(self.count)])]
    all_gather x4 -> x0, blocking collectives: 268 us -> none  [the longest x1 70.9 us: local(): lax.all_gather(self_bias, ('wide', 'narrow'), axis=1, tiled=True)]
    unnamed x18 -> x0, waiting for transfers between devices: 136 us -> none
    ppermute x0 -> x110, starting transfers between devices: none -> 95.6 us  [swap(): return lax.ppermute(value, AXES, [(i, i ^ mask) for i in range(self.count)])]
    reshape x24 -> x19, local copies, waits for them, and re-layouts: 130 us -> 40.1 us  [the longest x1 11.8 us: local(): mem_keys = project(mem_rel, cqk[1]).astype(BF).reshape(mem_split)]
    unnamed x2 -> x0, blocking collectives: 75.7 us -> none
    unnamed x166 -> x466, local copies, waits for them, and re-layouts: 54.6 us -> 126 us
  transfers between devices with their start and end apart: 15 -> 110, of which waited for: 7 -> 50; matrix products, arithmetic and copies ran while one was open for 16% -> 36% of each run, Pallas kernels for 0% -> 0%
where the time goes in v1:
time: 830 us; the launch traced here: 819 us
  waiting for transfers between devices  294 us (35%)
  local copies, waits for them, and re-layouts  220 us (27%)
  matrix products  162 us (20%)
  starting transfers between devices  95.6 us (12%)
  other arithmetic  41 us (5%)
    ppermute x110, waiting for transfers between devices, swap(): return lax.ppermute(value, AXES, [(i, i ^ mask) for i in range(self.count)])  294 us
    unnamed x466, local copies, waits for them, and re-layouts  126 us
    ppermute x110, starting transfers between devices, swap(): return lax.ppermute(value, AXES, [(i, i ^ mask) for i in range(self.count)])  95.6 us
    dot_general x10, matrix products, project(): return jnp.dot(left_rows, weight, preferred_element_type=F32)  47 us
    dot_general x20, matrix products, weight_grad(): lax.dot_general(left_rows, gradient, (((0,), (0,)), ((), ())), preferred_...  41.6 us
    dot_general x10, matrix products, project_back(): lax.dot_general(gradient, weight, (((1,), (1,)), ((), ())), preferred_ele...  35.5 us
  transfers between devices with their start and end apart: 110, of which 50 were waited for; matrix products, arithmetic and copies ran while one was open for 36% of the time, Pallas kernels for 0%

profile of v1, /device:TPU:0, one launch (start us, length us, event | category | flops | bytes accessed | tf_op | source)
XLA Modules:
  0.0 818.6 jit_solution(7979867877882168670)
XLA Ops:
  39.9 11.7 %collective-permute-done.10 = bf16[2,8,128]{2,1,0:T(8,128)(2,1)S(1)} collective-permute-done((bf16[2,8,128]{2,1,0:T(8,128)(2,1)S(1)}, bf16[2,8,128]{2,1,0:T(8,128)(2,1)S(1)}, u32[]{:S(2)}, u32[]{:S(2)}) %collective-permute-start.10) | collective-permute-done | bytes 4128 | tf_op jit(solution)/shard_map/ppermute | solution.py:82
  69.2 10.2 %collective-permute-done.22 = bf16[4,2,32,1024]{3,2,1,0:T(8,128)(2,1)S(1)} collective-permute-done((bf16[4,2,32,1024]{3,2,1,0:T(8,128)(2,1)S(1)}, bf16[4,2,32,1024]{3,2,1,0:T(8,128)(2,1)S(1)}, u32[]{:S(2)}, u32[]{:S(2)}) %collective-permute-start.22) | collective-permute-done | bytes 524320 | tf_op jit(solution)/shard_map/ppermute | solution.py:82
  82.8 7.9 collective-permute-done.1
  91.1 10.9 %collective-permute-done.38 = bf16[1,2,32,4096]{3,2,1,0:T(8,128)(2,1)S(1)} collective-permute-done((bf16[1,2,32,4096]{3,2,1,0:T(8,128)(2,1)S(1)}, bf16[1,2,32,4096]{3,2,1,0:T(8,128)(2,1)S(1)}, u32[]{:S(2)}, u32[]{:S(2)}) %collective-permute-start.38) | collective-permute-done | bytes 524320 | tf_op jit(solution)/shard_map/ppermute | solution.py:82
  148.2 8.7 %collective-permute-done.32 = bf16[2,128,1024]{2,1,0:T(8,128)(2,1)S(1)} collective-permute-done((bf16[2,128,1024]{2,1,0:T(8,128)(2,1)S(1)}, bf16[2,128,1024]{2,1,0:T(8,128)(2,1)S(1)}, u32[]{:S(2)}, u32[]{:S(2)}) %collective-permute-start.32) | collective-permute-done | bytes 524320 | tf_op jit(solution)/shard_map/ppermute | solution.py:82
  176.3 30.2 %collective-permute-done.25 = bf16[2,128,1024]{2,1,0:T(8,128)(2,1)} collective-permute-done((bf16[2,128,1024]{2,1,0:T(8,128)(2,1)S(1)}, bf16[2,128,1024]{2,1,0:T(8,128)(2,1)}, u32[]{:S(2)}, u32[]{:S(2)}) %collective-permute-start.25) | collective-permute-done | bytes 524320 | tf_op jit(solution)/shard_map/ppermute | solution.py:82
  212.6 15.8 %collective-permute-done.39 = bf16[1,128,4096]{2,1,0:T(8,128)(2,1)} collective-permute-done((bf16[1,128,4096]{2,1,0:T(8,128)(2,1)}, bf16[1,128,4096]{2,1,0:T(8,128)(2,1)}, u32[]{:S(2)}, u32[]{:S(2)}) %collective-permute-start.39) | collective-permute-done | bytes 1048608 | tf_op jit(solution)/shard_map/ppermute | solution.py:82
  249.6 9.4 %convolution_convert_fusion.3 = bf16[2048,1024]{1,0:T(8,128)(2,1)} fusion(bf16[2048,1024]{1,0:T(8,128)(2,1)} %get-tuple-element.396, bf16[2,1024,1024]{2,1,0:T(8,128)(2,1)} %constant_dynamic-update-slice_fusion.56), kind=kOutput, calls=%fused_computation.107 | convolution fusion | flops 4297064448 | bytes 10485760 | tf_op jit(solution)/shard_map/dot_general | solution.py:15
  259.6 11.8 %reshape.534 = bf16[2,1024,16,64]{3,2,1,0:T(8,128)(2,1)} reshape(bf16[2048,1024]{1,0:T(8,128)(2,1)} %convolution_convert_fusion.3) | data formatting | bytes 8388608 | tf_op jit(solution)/shard_map/reshape | solution.py:266
  271.4 10.0 %copy.76 = bf16[2,1024,16,64]{1,3,2,0:T(8,128)(2,1)} copy(bf16[2,1024,16,64]{3,2,1,0:T(8,128)(2,1)} %reshape.534) | data formatting | bytes 8388608
  308.8 9.3 %add_convert_fusion = bf16[2048,1024]{1,0:T(8,128)(2,1)} fusion(f32[1024]{0:T(1024)S(1)} %add.878, bf16[2048,1024]{1,0:T(8,128)(2,1)} %get-tuple-element.396, bf16[2,1024,1024]{2,1,0:T(8,128)(2,1)} %constant_dynamic-update-slice_fusion.40), kind=kOutput, calls=%fused_computation.78 | convolution fusion | flops 4299161600 | bytes 10489856 | tf_op jit(solution)/shard_map/dot_general | solution.py:15
  318.1 11.7 %reshape.532 = bf16[2,1024,16,64]{3,2,1,0:T(8,128)(2,1)} reshape(bf16[2048,1024]{1,0:T(8,128)(2,1)} %add_convert_fusion) | data formatting | bytes 8388608 | tf_op jit(solution)/shard_map/reshape | solution.py:267
  329.9 9.8 %copy.74 = bf16[2,1024,16,64]{1,3,2,0:T(8,128)(2,1)} copy(bf16[2,1024,16,64]{3,2,1,0:T(8,128)(2,1)} %reshape.532) | data formatting | bytes 8388608
  339.8 17.0 %while.28 = (s32[]{:T(128)}, bf16[2,128,16,64]{1,3,2,0:T(8,128)(2,1)S(1)}, f32[2,16,128,1]{2,1,3,0:T(8,128)S(1)}, bf16[2,1024,16,64]{1,3,2,0:T(8,128)(2,1)}, s32...) while((s32[]{:T(128)}, ...), condition=%wide.region_7.8_spmd.clone, body=%wide.region_4.7_spmd.clone.sunk | while | flops 553796608 | bytes 46766212 | solution.py:273
  381.9 12.7 %multiply_convert_fusion.1 = (bf16[256,4096]{1,0:T(8,128)(2,1)S(1)}, f32[256,4096]{1,0:T(8,128)S(1)}, f32[256,4096]{1,0:T(8,128)S(1)}) fusion(f32[4096]{0:T(1024)S(1)} %get-tuple-element.440, bf16[256,1024]{1,0:T(8,128)(2,1)S(1)} %get-tuple-element.316, bf16[1,1024,4096]{2,1,0:T(8,128)(2,1)S(1)} %constant_dynamic-update-slice_fusion.80), kind=kOutput, calls=%fused_computation.91 | convolution fusion | flops 2216689664 | bytes 19415040 | tf_op jit(solution)/shard_map/dot_general | solution.py:15
  437.8 33.8 %while.29 = (s32[]{:T(128)}, bf16[2,128,16,64]{1,3,2,0:T(8,128)(2,1)S(1)}, bf16[2,1024,16,64]{1,3,2,0:T(8,128)(2,1)}, bf16[2,1024,16,64]{1,3,2,0:T(8,128)(2,1)},...) while((s32[]{:T(128)}, ...), condition=%wide.region_18.19_spmd.clone, body=%wide.region_16.18_spmd.clone.sunk | while | flops 1369570304 | bytes 141886736 | solution.py:304
  471.9 8.5 %copy.99 = bf16[2,1024,16,64]{1,0,3,2:T(2,128)(2,1)} copy(bf16[2,1024,16,64]{1,3,2,0:T(8,128)(2,1)} %get-tuple-element.122) | data formatting | bytes 8388608 | tf_op jit(solution)/shard_map/while | solution.py:304
  548.4 9.8 %convolution_add_fusion = f32[2048,1024]{0,1:T(8,128)S(1)} fusion(f32[2048,1024]{0,1:T(8,128)} %fusion.99, bf16[2048,1024]{0,1:T(8,128)(2,1)} %bitcast.719, bf16[2,1024,1024]{2,1,0:T(8,128)(2,1)} %constant_dynamic-update-slice_fusion.56), kind=kOutput, calls=%fused_computation.105 | convolution fusion | flops 4297064448 | bytes 23068672 | tf_op jit(solution)/shard_map/dot_general | solution.py:19
  584.2 9.3 %copy.121 = f32[2048,1024]{1,0:T(8,128)} copy(f32[2048,1024]{0,1:T(8,128)} %dynamic-slice_dynamic-update-slice_fusion) | data formatting | bytes 16777216
  631.1 9.7 %collective-permute-done.86 = bf16[2,128,1024]{2,1,0:T(8,128)(2,1)S(1)} collective-permute-done((bf16[2,128,1024]{2,1,0:T(8,128)(2,1)S(1)}, bf16[2,128,1024]{2,1,0:T(8,128)(2,1)S(1)}, u32[]{:S(2)}, u32[]{:S(2)}) %collective-permute-start.86) | collective-permute-done | bytes 524320 | tf_op jit(solution)/shard_map/ppermute | solution.py:82
  728.2 29.7 %collective-permute-done.106 = bf16[2,512,1024]{2,1,0:T(8,128)(2,1)S(1)} collective-permute-done((bf16[2,512,1024]{2,1,0:T(8,128)(2,1)S(1)}, bf16[2,512,1024]{2,1,0:T(8,128)(2,1)S(1)}, u32[]{:S(2)}, u32[]{:S(2)}) %collective-permute-start.106) | collective-permute-done | bytes 2097184 | tf_op jit(solution)/shard_map/ppermute | solution.py:82
  766.8 15.4 %collective-permute-done.107 = bf16[512,1024]{1,0:T(8,128)(2,1)S(1)} collective-permute-done((bf16[512,1024]{1,0:T(8,128)(2,1)S(1)}, bf16[512,1024]{1,0:T(8,128)(2,1)S(1)}, u32[]{:S(2)}, u32[]{:S(2)}) %collective-permute-start.107) | collective-permute-done | bytes 1048608 | tf_op jit(solution)/shard_map/ppermute | solution.py:82
  785.9 12.2 %collective-permute-done.108 = bf16[2,128,1024]{2,1,0:T(8,128)(2,1)S(1)} collective-permute-done((bf16[2,128,1024]{2,1,0:T(8,128)(2,1)S(1)}, bf16[2,128,1024]{2,1,0:T(8,128)(2,1)S(1)}, u32[]{:S(2)}, u32[]{:S(2)}) %collective-permute-start.108) | collective-permute-done | bytes 524320 | tf_op jit(solution)/shard_map/ppermute | solution.py:82
  798.4 9.9 %collective-permute-done.103 = bf16[2,32,4096]{2,1,0:T(8,128)(2,1)S(1)} collective-permute-done((bf16[2,32,4096]{2,1,0:T(8,128)(2,1)S(1)}, bf16[2,32,4096]{2,1,0:T(8,128)(2,1)S(1)}, u32[]{:S(2)}, u32[]{:S(2)}) %collective-permute-start.103) | collective-permute-done | bytes 524320 | tf_op jit(solution)/shard_map/ppermute | solution.py:82
  (1030 shorter events, 538.3 us)
Async XLA Ops:
  1.7 62.8 %collective-permute-start.21 = (bf16[4,1,32,1024]{3,2,0,1:T(8,128)(2,1)S(1)}, bf16[4,1,32,1024]{3,2,0,1:T(8,128)(2,1)S(1)}, u32[]{:S(2)}, u32[]{:S(2)}) collective-permute-start(bf16[4,1,32,1024]{3,2,0,1:T(8,128)(2,1)S(1)} %maximum_bitcast_fusion.4), channel_id=1, source_target_pairs={{0,2},{1,3},{2,0},{3,1},{4,6},{5,7},{6,4},{7,5},{8,10},{9,11},{10,... | collective-permute-start | bytes 786440 | tf_op jit(solution)/shard_map/ppermute | solution.py:82
  6.8 58.6 %collective-permute-start = (bf16[4,1,32,1024]{3,2,0,1:T(8,128)(2,1)S(1)}, bf16[4,1,32,1024]{3,2,0,1:T(8,128)(2,1)S(1)}, u32[]{:S(2)}, u32[]{:S(2)}) collective-permute-start(bf16[4,1,32,1024]{3,2,0,1:T(8,128)(2,1)S(1)} %maximum_bitcast_fusion.3), channel_id=1, source_target_pairs={{0,2},{1,3},{2,0},{3,1},{4,6},{5,7},{6,4},{7,5},{8,10},{9,11},{10,... | collective-permute-start | bytes 786440 | tf_op jit(solution)/shard_map/ppermute | solution.py:82
  12.0 54.9 %collective-permute-start.37 = (bf16[1,1,32,4096]{3,2,1,0:T(8,128)(2,1)}, bf16[1,1,32,4096]{3,2,1,0:T(8,128)(2,1)S(1)}, u32[]{:S(2)}, u32[]{:S(2)}) collective-permute-start(bf16[1,1,32,4096]{3,2,1,0:T(8,128)(2,1)} %bitcast.796), channel_id=1, source_target_pairs={{0,2},{1,3},{2,0},{3,1},{4,6},{5,7},{6,4},{7,5},{8,10},{9,11},{10,... | collective-permute-start | bytes 786440 | tf_op jit(solution)/shard_map/ppermute | solution.py:82
  14.5 53.3 %collective-permute-start.46 = (bf16[1,1,128,1024]{3,2,1,0:T(8,128)(2,1)}, bf16[1,1,128,1024]{3,2,1,0:T(8,128)(2,1)S(1)}, u32[]{:S(2)}, u32[]{:S(2)}) collective-permute-start(bf16[1,1,128,1024]{3,2,1,0:T(8,128)(2,1)} %bitcast.797), channel_id=1, source_target_pairs={{0,2},{1,3},{2,0},{3,1},{4,6},{5,7},{6,4},{7,5},{8,10},{9,11},{10,... | collective-permute-start | bytes 786440 | tf_op jit(solution)/shard_map/ppermute | solution.py:82
  67.9 42.2 %collective-permute-start.47 = (bf16[1,2,128,1024]{3,2,1,0:T(8,128)(2,1)S(1)}, bf16[1,2,128,1024]{3,2,1,0:T(8,128)(2,1)S(1)}, u32[]{:S(2)}, u32[]{:S(2)}) collective-permute-start(bf16[1,2,128,1024]{3,2,1,0:T(8,128)(2,1)S(1)} %maximum_bitcast_fusion.2), channel_id=1, source_target_pairs={{0,1},{1,0},{2,3},{3,2},{4,5},{5,4},{6,7},{7,6},{8,9},{9,8},{10,11... | collective-permute-start | bytes 1572872 | tf_op jit(solution)/shard_map/ppermute | solution.py:82
  166.0 44.2 %collective-permute-start.48 = (bf16[1,512,1024]{2,1,0:T(8,128)(2,1)}, bf16[1,512,1024]{2,1,0:T(8,128)(2,1)S(1)}, u32[]{:S(2)}, u32[]{:S(2)}) collective-permute-start(bf16[1,512,1024]{2,1,0:T(8,128)(2,1)} %bitcast.53), channel_id=1, source_target_pairs={{0,8},{1,9},{2,10},{3,11},{4,12},{5,13},{6,14},{7,15},{8,0},{9,1},... | collective-permute-start | bytes 3145736 | tf_op jit(solution)/shard_map/ppermute | solution.py:82
  167.6 42.9 %collective-permute-start.49 = (bf16[1,512,1024]{2,1,0:T(8,128)(2,1)}, bf16[1,512,1024]{2,1,0:T(8,128)(2,1)}, u32[]{:S(2)}, u32[]{:S(2)}) collective-permute-start(bf16[1,512,1024]{2,1,0:T(8,128)(2,1)} %bitcast.53), channel_id=1, source_target_pairs={{0,16},{1,17},{2,18},{3,19},{4,20},{5,21},{6,22},{7,23},{8,24},{9,... | collective-permute-start | bytes 3145736 | tf_op jit(solution)/shard_map/ppermute | solution.py:82
  175.0 53.4 %collective-permute-start.39 = (bf16[1,128,4096]{2,1,0:T(8,128)(2,1)}, bf16[1,128,4096]{2,1,0:T(8,128)(2,1)}, u32[]{:S(2)}, u32[]{:S(2)}) collective-permute-start(bf16[1,128,4096]{2,1,0:T(8,128)(2,1)} %bitcast.43), channel_id=1, source_target_pairs={{0,8},{1,9},{2,10},{3,11},{4,12},{5,13},{6,14},{7,15},{8,0},{9,1},... | collective-permute-start | bytes 3145736 | tf_op jit(solution)/shard_map/ppermute | solution.py:82
  210.2 168.5 %collective-permute-start.42 = (bf16[1,128,4096]{2,1,0:T(8,128)(2,1)}, bf16[1,128,4096]{2,1,0:T(8,128)(2,1)}, u32[]{:S(2)}, u32[]{:S(2)}) collective-permute-start(bf16[1,128,4096]{2,1,0:T(8,128)(2,1)} %bitcast.43), channel_id=1, source_target_pairs={{0,4},{1,5},{2,6},{3,7},{4,0},{5,1},{6,2},{7,3},{8,12},{9,13},{10,... | collective-permute-start | bytes 3145736 | tf_op jit(solution)/shard_map/ppermute | solution.py:82
  210.5 162.9 %collective-permute-start.51 = (bf16[1,512,1024]{2,1,0:T(8,128)(2,1)}, bf16[1,512,1024]{2,1,0:T(8,128)(2,1)}, u32[]{:S(2)}, u32[]{:S(2)}) collective-permute-start(bf16[1,512,1024]{2,1,0:T(8,128)(2,1)} %bitcast.53), channel_id=1, source_target_pairs={{0,4},{1,5},{2,6},{3,7},{4,0},{5,1},{6,2},{7,3},{8,12},{9,13},{10,... | collective-permute-start | bytes 3145736 | tf_op jit(solution)/shard_map/ppermute | solution.py:82
  234.2 47.7 %collective-permute-start.8 = (bf16[2,128,1024]{2,1,0:T(8,128)(2,1)}, bf16[2,128,1024]{2,1,0:T(8,128)(2,1)}, u32[]{:S(2)}, u32[]{:S(2)}) collective-permute-start(bf16[2,128,1024]{2,1,0:T(8,128)(2,1)} %collective-permute-done.4), channel_id=1, source_target_pairs={{0,4},{1,5},{2,6},{3,7},{4,0},{5,1},{6,2},{7,3},{8,12},{9,13},{10,... | collective-permute-start | bytes 1572872 | tf_op jit(solution)/shard_map/ppermute | solution.py:82
  234.3 72.6 %collective-permute-start.29 = (bf16[2,128,1024]{2,1,0:T(8,128)(2,1)}, bf16[2,128,1024]{2,1,0:T(8,128)(2,1)}, u32[]{:S(2)}, u32[]{:S(2)}) collective-permute-start(bf16[2,128,1024]{2,1,0:T(8,128)(2,1)} %collective-permute-done.25), channel_id=1, source_target_pairs={{0,4},{1,5},{2,6},{3,7},{4,0},{5,1},{6,2},{7,3},{8,12},{9,13},{10,... | collective-permute-start | bytes 1572872 | tf_op jit(solution)/shard_map/ppermute | solution.py:82
  245.9 129.8 %collective-permute-start.41 = (bf16[1,128,4096]{2,1,0:T(8,128)(2,1)}, bf16[1,128,4096]{2,1,0:T(8,128)(2,1)}, u32[]{:S(2)}, u32[]{:S(2)}) collective-permute-start(bf16[1,128,4096]{2,1,0:T(8,128)(2,1)} %collective-permute-done.39), channel_id=1, source_target_pairs={{0,16},{1,17},{2,18},{3,19},{4,20},{5,21},{6,22},{7,23},{8,24},{9,... | collective-permute-start | bytes 3145736 | tf_op jit(solution)/shard_map/ppermute | solution.py:82
  281.8 88.8 %collective-permute-start.50 = (bf16[1,512,1024]{2,1,0:T(8,128)(2,1)}, bf16[1,512,1024]{2,1,0:T(8,128)(2,1)}, u32[]{:S(2)}, u32[]{:S(2)}) collective-permute-start(bf16[1,512,1024]{2,1,0:T(8,128)(2,1)} %collective-permute-done.49), channel_id=1, source_target_pairs={{0,8},{1,9},{2,10},{3,11},{4,12},{5,13},{6,14},{7,15},{8,0},{9,1},... | collective-permute-start | bytes 3145736 | tf_op jit(solution)/shard_map/ppermute | solution.py:82
  306.9 69.4 %collective-permute-start.52 = (bf16[1,512,1024]{2,1,0:T(8,128)(2,1)}, bf16[1,512,1024]{2,1,0:T(8,128)(2,1)S(1)}, u32[]{:S(2)}, u32[]{:S(2)}) collective-permute-start(bf16[1,512,1024]{2,1,0:T(8,128)(2,1)} %copy-done.63), channel_id=1, source_target_pairs={{0,4},{1,5},{2,6},{3,7},{4,0},{5,1},{6,2},{7,3},{8,12},{9,13},{10,... | collective-permute-start | bytes 3145736 | tf_op jit(solution)/shard_map/ppermute | solution.py:82
  515.0 196.2 %collective-permute-start.105 = (bf16[2048,1024]{1,0:T(8,128)(2,1)}, bf16[2048,1024]{1,0:T(8,128)(2,1)}, u32[]{:S(2)}, u32[]{:S(2)}) collective-permute-start(bf16[2048,1024]{1,0:T(8,128)(2,1)} %convolution_convert_fusion.2), channel_id=1, source_target_pairs={{0,4},{1,5},{2,6},{3,7},{4,0},{5,1},{6,2},{7,3},{8,12},{9,13},{10,... | collective-permute-start | bytes 12582920 | tf_op jit(solution)/shard_map/ppermute | solution.py:82
  516.5 85.7 %collective-permute-start.95 = (bf16[512,1024]{1,0:T(8,128)(2,1)}, bf16[512,1024]{1,0:T(8,128)(2,1)}, u32[]{:S(2)}, u32[]{:S(2)}) collective-permute-start(bf16[512,1024]{1,0:T(8,128)(2,1)} %convolution_convert_fusion.4), channel_id=1, source_target_pairs={{0,4},{1,5},{2,6},{3,7},{4,0},{5,1},{6,2},{7,3},{8,12},{9,13},{10,... | collective-permute-start | bytes 3145736 | tf_op jit(solution)/shard_map/ppermute | solution.py:82
  547.9 49.0 %collective-permute-start.55 = (bf16[512,1024]{1,0:T(8,128)(2,1)}, bf16[512,1024]{1,0:T(8,128)(2,1)}, u32[]{:S(2)}, u32[]{:S(2)}) collective-permute-start(bf16[512,1024]{1,0:T(8,128)(2,1)} %convolution_convert_fusion.14), channel_id=1, source_target_pairs={{0,4},{1,5},{2,6},{3,7},{4,0},{5,1},{6,2},{7,3},{8,12},{9,13},{10,... | collective-permute-start | bytes 3145736 | tf_op jit(solution)/shard_map/ppermute | solution.py:82
  547.9 51.4 %collective-permute-start.60 = (bf16[512,1024]{1,0:T(8,128)(2,1)}, bf16[512,1024]{1,0:T(8,128)(2,1)}, u32[]{:S(2)}, u32[]{:S(2)}) collective-permute-start(bf16[512,1024]{1,0:T(8,128)(2,1)} %convolution_convert_fusion.12), channel_id=1, source_target_pairs={{0,4},{1,5},{2,6},{3,7},{4,0},{5,1},{6,2},{7,3},{8,12},{9,13},{10,... | collective-permute-start | bytes 3145736 | tf_op jit(solution)/shard_map/ppermute | solution.py:82
  599.3 115.9 %collective-permute-start.100 = (bf16[512,4096]{1,0:T(8,128)(2,1)}, bf16[512,4096]{1,0:T(8,128)(2,1)S(1)}, u32[]{:S(2)}, u32[]{:S(2)}) collective-permute-start(bf16[512,4096]{1,0:T(8,128)(2,1)} %convolution_convert_fusion), channel_id=1, source_target_pairs={{0,4},{1,5},{2,6},{3,7},{4,0},{5,1},{6,2},{7,3},{8,12},{9,13},{10,... | collective-permute-start | bytes 12582920 | tf_op jit(solution)/shard_map/ppermute | solution.py:82
  715.1 42.7 %collective-permute-start.106 = (bf16[2,512,1024]{2,1,0:T(8,128)(2,1)S(1)}, bf16[2,512,1024]{2,1,0:T(8,128)(2,1)S(1)}, u32[]{:S(2)}, u32[]{:S(2)}) collective-permute-start(bf16[2,512,1024]{2,1,0:T(8,128)(2,1)S(1)} %fusion.88), channel_id=1, source_target_pairs={{0,8},{1,9},{2,10},{3,11},{4,12},{5,13},{6,14},{7,15},{8,0},{9,1},... | collective-permute-start | bytes 6291464 | tf_op jit(solution)/shard_map/ppermute | solution.py:82
  717.3 45.9 %collective-permute-start.101 = (bf16[2,128,4096]{2,1,0:T(8,128)(2,1)S(1)}, bf16[2,128,4096]{2,1,0:T(8,128)(2,1)S(1)}, u32[]{:S(2)}, u32[]{:S(2)}) collective-permute-start(bf16[2,128,4096]{2,1,0:T(8,128)(2,1)S(1)} %bitcast.747), channel_id=1, source_target_pairs={{0,16},{1,17},{2,18},{3,19},{4,20},{5,21},{6,22},{7,23},{8,24},{9,... | collective-permute-start | bytes 6291464 | tf_op jit(solution)/shard_map/ppermute | solution.py:82
  722.1 42.3 %collective-permute-start.74 = (bf16[32,1024]{1,0:T(8,128)(2,1)S(1)}, bf16[32,1024]{1,0:T(8,128)(2,1)S(1)}, u32[]{:S(2)}, u32[]{:S(2)}) collective-permute-start(bf16[32,1024]{1,0:T(8,128)(2,1)S(1)} %fusion.284), channel_id=1, source_target_pairs={{0,2},{1,3},{2,0},{3,1},{4,6},{5,7},{6,4},{7,5},{8,10},{9,11},{10,... | collective-permute-start | bytes 196616 | tf_op jit(solution)/shard_map/ppermute | solution.py:82
  725.1 41.6 %collective-permute-start.59 = (bf16[32,1024]{1,0:T(8,128)(2,1)S(1)}, bf16[32,1024]{1,0:T(8,128)(2,1)S(1)}, u32[]{:S(2)}, u32[]{:S(2)}) collective-permute-start(bf16[32,1024]{1,0:T(8,128)(2,1)S(1)} %fusion.281), channel_id=1, source_target_pairs={{0,2},{1,3},{2,0},{3,1},{4,6},{5,7},{6,4},{7,5},{8,10},{9,11},{10,... | collective-permute-start | bytes 196616 | tf_op jit(solution)/shard_map/ppermute | solution.py:82
  (258 other events, 3368.4 us)

commit v2 on v1

--- a/solution.py
+++ b/solution.py
@@ -1,6 +1,8 @@
 import jax
 import jax.numpy as jnp
 from jax import lax
+from jax.experimental import pallas as pl
+from jax.experimental.pallas import tpu as pltpu
 from jax.sharding import PartitionSpec as P
 
 HD = 64
@@ -38,27 +40,210 @@
     return jax.nn.gelu(pre_gelu, approximate=False)
 
 
-def attend(queries, key_rows, values, allowed):
-    scores = jnp.einsum("thd,shd->hts", queries, key_rows, preferred_element_type=F32)
-    scores = jnp.where(allowed, scores, MASKED)
-    log_total = jax.nn.logsumexp(scores, axis=-1, keepdims=True)
-    chances = jnp.exp(scores - log_total).astype(BF)
-    context = jnp.einsum("hts,shd->thd", chances, values, preferred_element_type=F32)
-    return (context.astype(BF), log_total)
-
-
-def attend_back(queries, key_rows, values, log_total, d_context, allowed):
-    scores = jnp.einsum("thd,shd->hts", queries, key_rows, preferred_element_type=F32)
-    scores = jnp.where(allowed, scores, MASKED)
-    chances = jnp.exp(scores - log_total)
-    d_chances = jnp.einsum("thd,shd->hts", d_context, values, preferred_element_type=F32)
-    d_scores = (
-        chances * (d_chances - jnp.sum(d_chances * chances, axis=-1, keepdims=True))
-    ).astype(BF)
-    d_queries = jnp.einsum("hts,shd->thd", d_scores, key_rows, preferred_element_type=F32)
-    d_keys = jnp.einsum("hts,thd->shd", d_scores, queries, preferred_element_type=F32)
-    d_values = jnp.einsum("hts,thd->shd", chances.astype(BF), d_context, preferred_element_type=F32)
-    return (d_queries.astype(BF), d_keys.astype(BF), d_values.astype(BF))
+def pair_stack(rows):
+    lane = lax.broadcasted_iota(jnp.int32, rows.shape, 1)
+    zero = jnp.zeros_like(rows)
+    return jnp.concatenate(
+        [jnp.where(lane < HD, rows, zero), jnp.where(lane >= HD, rows, zero)], axis=0
+    )
+
+
+def pair_merge(stacked):
+    t = stacked.shape[0] // 2
+    lane = lax.broadcasted_iota(jnp.int32, (t, 2 * HD), 1)
+    return jnp.where(lane < HD, stacked[:t], stacked[t:])
+
+
+def dot_nt(a, b):
+    return lax.dot_general(a, b, (((1,), (1,)), ((), ())), preferred_element_type=F32)
+
+
+def dot_tn(a, b):
+    return lax.dot_general(a, b, (((0,), (0,)), ((), ())), preferred_element_type=F32)
+
+
+def dot_nn(a, b):
+    return lax.dot_general(a, b, (((1,), (0,)), ((), ())), preferred_element_type=F32)
+
+
+def masked_scores(k, qs, length):
+    scores = dot_nt(k, qs)
+    slot = lax.broadcasted_iota(jnp.int32, scores.shape, 0)
+    if length is None:
+        seen = lax.broadcasted_iota(jnp.int32, scores.shape, 1) % (scores.shape[1] // 2)
+        return jnp.where(slot <= seen, scores, MASKED)
+    return jnp.where(slot < length, scores, MASKED)
+
+
+def attend_pair(q, k, v, length):
+    scores = masked_scores(k, pair_stack(q), length)
+    top = jnp.max(scores, axis=0, keepdims=True)
+    weights = jnp.exp(scores - top)
+    total = jnp.sum(weights, axis=0, keepdims=True)
+    chances = (weights * (1.0 / total)).astype(BF)
+    return pair_merge(dot_tn(chances, v)).astype(BF), top + jnp.log(total)
+
+
+def attend_pair_back(q, k, v, lse, d_out, length):
+    qs, ds_out = pair_stack(q), pair_stack(d_out)
+    chances = jnp.exp(masked_scores(k, qs, length) - lse)
+    d_chances = dot_nt(v, ds_out)
+    row = jnp.sum(d_chances * chances, axis=0, keepdims=True)
+    d_scores = (chances * (d_chances - row)).astype(BF)
+    d_q = pair_merge(dot_tn(d_scores, k)).astype(BF)
+    d_k = dot_nn(d_scores, qs).astype(BF)
+    d_v = dot_nn(chances.astype(BF), ds_out).astype(BF)
+    return d_q, d_k, d_v
+
+
+PAIR = 2 * HD
+
+
+def cross_kernel(place, lengths, q, k, v, out, lse):
+    out[...], lse[0, 0] = attend_pair(q[...], k[...], v[...], lengths[pl.program_id(0)])
+
+
+def cross_back_kernel(place, lengths, q, k, v, lse, d_out, d_q, d_k, d_v):
+    d_q[...], d_k[...], d_v[...] = attend_pair_back(
+        q[...], k[...], v[...], lse[0, 0], d_out[...], lengths[pl.program_id(0)]
+    )
+    d_q[...] = d_q[...] * jnp.asarray(HD**-0.5, BF)
+
+
+def cross_attend(q, k, v, lengths, place):
+    items = lengths.shape[0]
+    t, s, pairs = q.shape[0] // items, k.shape[0] // items, q.shape[1] // PAIR
+    rows = pl.BlockSpec((t, PAIR), lambda b, j, *_: (b, j))
+    slots = pl.BlockSpec((s, PAIR), lambda b, j, *_: (b, j))
+    placed = pl.BlockSpec((t, PAIR), lambda b, j, place, lengths: (b, place[j]))
+    lse = pl.BlockSpec((1, 1, 1, 2 * t), lambda b, j, *_: (b, j, 0, 0))
+    return pl.pallas_call(
+        cross_kernel,
+        grid_spec=pltpu.PrefetchScalarGridSpec(
+            num_scalar_prefetch=2,
+            grid=(items, pairs),
+            in_specs=[rows, slots, slots],
+            out_specs=[placed, lse],
+        ),
+        out_shape=[
+            jax.ShapeDtypeStruct(q.shape, BF),
+            jax.ShapeDtypeStruct((items, pairs, 1, 2 * t), F32),
+        ],
+        name="cross_attend",
+    )(place, lengths, q, k, v)
+
+
+def cross_attend_back(q, k, v, lse, d_out, lengths, place):
+    items = lengths.shape[0]
+    t, s, pairs = q.shape[0] // items, k.shape[0] // items, q.shape[1] // PAIR
+    rows = pl.BlockSpec((t, PAIR), lambda b, j, *_: (b, j))
+    slots = pl.BlockSpec((s, PAIR), lambda b, j, *_: (b, j))
+    placed = pl.BlockSpec((t, PAIR), lambda b, j, place, lengths: (b, place[j]))
+    lse_spec = pl.BlockSpec((1, 1, 1, 2 * t), lambda b, j, *_: (b, j, 0, 0))
+    return pl.pallas_call(
+        cross_back_kernel,
+        grid_spec=pltpu.PrefetchScalarGridSpec(
+            num_scalar_prefetch=2,
+            grid=(items, pairs),
+            in_specs=[rows, slots, slots, lse_spec, placed],
+            out_specs=[rows, slots, slots],
+        ),
+        out_shape=[
+            jax.ShapeDtypeStruct(q.shape, BF),
+            jax.ShapeDtypeStruct(k.shape, BF),
+            jax.ShapeDtypeStruct(k.shape, BF),
+        ],
+        name="cross_attend_back",
+    )(place, lengths, q, k, v, lse, d_out)
+
+
+def lanes(ref, at):
+    return ref[:, pl.ds(pl.multiple_of(at * PAIR, PAIR), PAIR)]
+
+
+def self_kernel(place, q, k, v, out, lse):
+    for j in range(q.shape[1] // PAIR):
+        cut = slice(j * PAIR, (j + 1) * PAIR)
+        found, lse[0, j] = attend_pair(q[:, cut], k[:, cut], v[:, cut], None)
+        out[:, pl.ds(pl.multiple_of(place[j] * PAIR, PAIR), PAIR)] = found
+
+
+def self_back_kernel(place, q, k, v, lse, d_out, d_q, d_k, d_v):
+    for j in range(q.shape[1] // PAIR):
+        cut = slice(j * PAIR, (j + 1) * PAIR)
+        found = attend_pair_back(
+            q[:, cut], k[:, cut], v[:, cut], lse[0, j], lanes(d_out, place[j]), None
+        )
+        d_q[:, cut] = found[0] * jnp.asarray(HD**-0.5, BF)
+        d_k[:, cut] = found[1]
+        d_v[:, cut] = found[2]
+
+
+def self_attend(q, k, v, items, place):
+    t, width = q.shape[0] // items, q.shape[1]
+    rows = pl.BlockSpec((t, width), lambda b, *_: (b, 0))
+    lse = pl.BlockSpec((1, width // PAIR, 1, 2 * t), lambda b, *_: (b, 0, 0, 0))
+    return pl.pallas_call(
+        self_kernel,
+        grid_spec=pltpu.PrefetchScalarGridSpec(
+            num_scalar_prefetch=1,
+            grid=(items,),
+            in_specs=[rows] * 3,
+            out_specs=[rows, lse],
+        ),
+        out_shape=[
+            jax.ShapeDtypeStruct(q.shape, BF),
+            jax.ShapeDtypeStruct((items, width // PAIR, 1, 2 * t), F32),
+        ],
+        name="self_attend",
+    )(place, q, k, v)
+
+
+def self_attend_back(q, k, v, lse, d_out, items, place):
+    t, width = q.shape[0] // items, q.shape[1]
+    rows = pl.BlockSpec((t, width), lambda b, *_: (b, 0))
+    lse_spec = pl.BlockSpec((1, width // PAIR, 1, 2 * t), lambda b, *_: (b, 0, 0, 0))
+    return pl.pallas_call(
+        self_back_kernel,
+        grid_spec=pltpu.PrefetchScalarGridSpec(
+            num_scalar_prefetch=1,
+            grid=(items,),
+            in_specs=[rows] * 3 + [lse_spec, rows],
+            out_specs=[rows] * 3,
+        ),
+        out_shape=[jax.ShapeDtypeStruct(q.shape, BF)] * 3,
+        name="self_attend_back",
+    )(place, q, k, v, lse, d_out)
+
+
+def back_kernel(place, *refs):
+    count = (len(refs) - 1) // 2
+    out = refs[-1]
+    total = dot_nt(refs[0][...], refs[count][...])
+    for i in range(1, count):
+        total = total + dot_nt(refs[i][...], refs[count + i][...])
+    size = total.shape[1] // place.shape[0]
+    for i in range(place.shape[0]):
+        at = pl.ds(pl.multiple_of(place[i] * size, 128), size)
+        out[:, at] = total[:, i * size : (i + 1) * size]
+
+
+def back_natural(lefts, weights, place, block):
+    m, k = lefts[0].shape
+    n = weights[0].shape[0]
+    whole = pl.BlockSpec((n, k), lambda i, *_: (0, 0), pipeline_mode=pl.Buffered(1))
+    return pl.pallas_call(
+        back_kernel,
+        grid_spec=pltpu.PrefetchScalarGridSpec(
+            num_scalar_prefetch=1,
+            grid=(m // block,),
+            in_specs=[pl.BlockSpec((block, k), lambda i, *_: (i, 0))] * len(lefts)
+            + [whole] * len(weights),
+            out_specs=pl.BlockSpec((block, n), lambda i, *_: (i, 0)),
+        ),
+        out_shape=jax.ShapeDtypeStruct((m, n), F32),
+        name="back_natural",
+    )(place, *lefts, *weights)
 
 
 class Plan:
@@ -123,6 +308,13 @@
             place = (r % 2) * (self.wide // 2) + r // 2
             pieces.append(lax.dynamic_slice_in_dim(rows, place * size, size, axis=1))
         return jnp.concatenate(pieces, axis=1)
+
+    def places(self):
+        r = lax.iota(jnp.int32, self.wide) ^ self.w
+        return (r % 2) * (self.wide // 2) + r // 2
+
+    def blocks(self):
+        return jnp.array(self.order, jnp.int32) ^ self.w
 
     def scatter(self, left_rel, right, route):
         half = left_rel.shape[1] // 2
@@ -222,14 +414,24 @@
     scaling = HD ** (-0.5)
     item_count, mem_slots, model_width = memory.shape
     row_count = inputs.shape[0]
-    seq_len = row_count // item_count
-    head_count = model_width // HD
-    head_split = (item_count, seq_len, head_count, HD)
-    mem_split = (item_count, mem_slots, head_count, HD)
-    causal = lax.broadcasted_iota(jnp.int32, (seq_len, seq_len), 0) >= lax.broadcasted_iota(
-        jnp.int32, (seq_len, seq_len), 1
-    )
-    key_slots = lax.broadcasted_iota(jnp.int32, (1, mem_slots), 1)
+    pairs = model_width // PAIR
+    paired = plan.wide == pairs
+    place = plan.places() if paired else lax.iota(jnp.int32, pairs)
+
+    def to_relative(context):
+        return context if paired else plan.relative(context)
+
+    def from_relative(context):
+        return context if paired else plan.natural(context)
+
+    def back(lefts, weights, block):
+        if (model_width // plan.wide) % 128 == 0:
+            return back_natural(lefts, weights, plan.blocks(), block)
+        total = project_back(lefts[0], weights[0])
+        for left, weight in zip(lefts[1:], weights[1:]):
+            total = total + project_back(left, weight)
+        return plan.natural(total)
+
     inputs_f = inputs.astype(F32)
 
     vectors = [self_bias, self_gain, cross_bias, cross_gain, ffn_bias_in, ffn_bias_out, ffn_gain]
@@ -248,30 +450,21 @@
     fout = plan.gather_wide(plan.gather_z(ffn_out[None]), 1)[0]
 
     x_rel = plan.relative(inputs)
-    queries = (((project(x_rel, sqk[0]) + sbias[0]) * scaling).astype(BF)).reshape(head_split)
-    key_rows = project(x_rel, sqk[1]).astype(BF).reshape(head_split)
-    values = (project(x_rel, svo[0]) + sbias[1]).astype(BF).reshape(head_split)
-    self_ctx, self_lse = jax.vmap(attend, in_axes=(0, 0, 0, None))(
-        queries, key_rows, values, causal
-    )
-    self_rel = plan.relative(self_ctx.reshape(row_count, model_width))
+    queries = ((project(x_rel, sqk[0]) + sbias[0]) * scaling).astype(BF)
+    key_rows = project(x_rel, sqk[1]).astype(BF)
+    values = (project(x_rel, svo[0]) + sbias[1]).astype(BF)
+    self_ctx, self_lse = self_attend(queries, key_rows, values, item_count, place)
+    self_rel = to_relative(self_ctx)
     first_pre = inputs_f + (project(self_rel, svo[1]) + sbias[2])
     first = layer_norm(first_pre, sgain, sbias[3])
     first_rel = plan.relative(first.astype(BF))
 
-    queries_two = (
-        ((project(first_rel, cqk[0]) + cbias[0]) * scaling).astype(BF).reshape(head_split)
-    )
+    queries_two = ((project(first_rel, cqk[0]) + cbias[0]) * scaling).astype(BF)
     mem_rel = plan.relative(memory.reshape(item_count * mem_slots, model_width))
-    mem_keys = project(mem_rel, cqk[1]).astype(BF).reshape(mem_split)
-    mem_values = (project(mem_rel, cvo[0]) + cbias[1]).astype(BF).reshape(mem_split)
-
-    def cross_item(packed):
-        item_q, item_k, item_v, item_len = packed
-        return attend(item_q, item_k, item_v, key_slots < item_len)
-
-    cross_ctx, cross_lse = lax.map(cross_item, (queries_two, mem_keys, mem_values, mem_lengths))
-    cross_rel = plan.relative(cross_ctx.reshape(row_count, model_width))
+    mem_keys = project(mem_rel, cqk[1]).astype(BF)
+    mem_values = (project(mem_rel, cvo[0]) + cbias[1]).astype(BF)
+    cross_ctx, cross_lse = cross_attend(queries_two, mem_keys, mem_values, mem_lengths, place)
+    cross_rel = to_relative(cross_ctx)
     second_pre = first + (project(cross_rel, cvo[1]) + cbias[2])
     second = layer_norm(second_pre, cgain, cbias[3])
     second_rel = plan.relative(second.astype(BF))
@@ -289,54 +482,39 @@
     g_fin = plan.scatter(second_rel, d_pre, 0)
     g_fbin = column_sums(d_pre)
     g_fbout = jnp.stack([column_sums(e_three), g_fshift])
-    d_second = d_third + plan.natural(project_back(d_pre, fin))
+    d_second = d_third + back([d_pre], [fin], row_count)
 
     _, norm_pull_two = jax.vjp(layer_norm, second_pre, cgain, cbias[3])
     d_second_pre, g_cgain, g_cshift = norm_pull_two(d_second)
     e_two = d_second_pre.astype(BF)
     g_cout = plan.scatter(cross_rel, e_two, 1)
-    d_cross_ctx = plan.natural(project_back(e_two, cvo[1]).astype(BF)).reshape(head_split)
-
-    def cross_back(packed):
-        item_q, item_k, item_v, item_lse, item_d, item_len = packed
-        return attend_back(item_q, item_k, item_v, item_lse, item_d, key_slots < item_len)
-
-    dq_two, dk_two, dv_two = lax.map(
-        cross_back, (queries_two, mem_keys, mem_values, cross_lse, d_cross_ctx, mem_lengths)
-    )
-    dq_scaled = dq_two.reshape(row_count, model_width) * scaling
-    dk_flat = dk_two.reshape(item_count * mem_slots, model_width)
-    dv_flat = dv_two.reshape(item_count * mem_slots, model_width)
+    d_cross_ctx = from_relative(project_back(e_two, cvo[1]).astype(BF))
+    dq_scaled, dk_flat, dv_flat = cross_attend_back(
+        queries_two, mem_keys, mem_values, cross_lse, d_cross_ctx, mem_lengths, place
+    )
     g_cv = plan.scatter(mem_rel, dv_flat, 1)
     g_ck = plan.scatter(mem_rel, dk_flat, 0)
     g_cq = plan.scatter(first_rel, dq_scaled, 0)
     g_cbias = jnp.stack(
         [column_sums(dq_scaled), column_sums(dv_flat), column_sums(e_two), g_cshift]
     )
-    memory_grad = plan.natural(
-        project_back(dk_flat, cqk[1]) + project_back(dv_flat, cvo[0])
-    ).reshape(item_count, mem_slots, model_width)
-    d_first = d_second_pre + plan.natural(project_back(dq_scaled, cqk[0]))
+    memory_grad = back([dk_flat, dv_flat], [cqk[1], cvo[0]], 512).reshape(memory.shape)
+    d_first = d_second_pre + back([dq_scaled], [cqk[0]], row_count)
 
     _, norm_pull_one = jax.vjp(layer_norm, first_pre, sgain, sbias[3])
     d_first_pre, g_sgain, g_sshift = norm_pull_one(d_first)
     e_one = d_first_pre.astype(BF)
     g_sout = plan.scatter(self_rel, e_one, 1)
-    d_self_ctx = plan.natural(project_back(e_one, svo[1]).astype(BF)).reshape(head_split)
-    dq_one, dk_one, dv_one = jax.vmap(attend_back, in_axes=(0, 0, 0, 0, 0, None))(
-        queries, key_rows, values, self_lse, d_self_ctx, causal
-    )
-    dq_self = dq_one.reshape(row_count, model_width) * scaling
-    dk_self = dk_one.reshape(row_count, model_width)
-    dv_self = dv_one.reshape(row_count, model_width)
+    d_self_ctx = from_relative(project_back(e_one, svo[1]).astype(BF))
+    dq_self, dk_self, dv_self = self_attend_back(
+        queries, key_rows, values, self_lse, d_self_ctx, item_count, place
+    )
     g_sv = plan.scatter(x_rel, dv_self, 1)
     g_sk = plan.scatter(x_rel, dk_self, 0)
     g_sq = plan.scatter(x_rel, dq_self, 0)
     g_sbias = jnp.stack([column_sums(dq_self), column_sums(dv_self), column_sums(e_one), g_sshift])
-    input_grad = d_first_pre + plan.natural(
-        project_back(dq_self, sqk[0])
-        + project_back(dk_self, sqk[1])
-        + project_back(dv_self, svo[0])
+    input_grad = d_first_pre + back(
+        [dq_self, dk_self, dv_self], [sqk[0], sqk[1], svo[0]], row_count
     )
 
     grads = [g_sbias, g_sgain, g_cbias, g_cgain, g_fbin, g_fbout, g_fgain]

time: 830 us -> 760 us (0.916)
  local copies, waits for them, and re-layouts: 220 us -> 99.5 us
  Pallas kernels: 0 us -> 89 us
  matrix products: 162 us -> 90.7 us
  waiting for transfers between devices: 294 us -> 319 us
  starting transfers between devices: 95.6 us -> 106 us
    pallas_call x0 -> x8, Pallas kernels: none -> 89 us  [the longest x4 34.8 us: back_natural(): pl.pallas_call(back_kernel, grid_spec=pltpu.PrefetchScalarGridSpec(num_sc...]
    unnamed x466 -> x327, local copies, waits for them, and re-layouts: 126 us -> 64.3 us
    reshape x12 -> x0, local copies, waits for them, and re-layouts: 39 us -> none  [the longest x1 11.8 us: local(): mem_keys = project(mem_rel, cqk[1]).astype(BF).reshape(mem_split)]
    dot_general x20 -> x0, matrix products: 37.5 us -> none  [the longest x3 7.38 us: attend_back(): jnp.einsum('thd,shd->hts', d_context, values, preferred_element_type=F32)]
    dot_general x10 -> x3, matrix products: 35.5 us -> 7.1 us  [project_back(): lax.dot_general(gradient, weight, (((1,), (1,)), ((), ())), preferred_ele...]
    ppermute x110, waiting for transfers between devices: 294 us -> 319 us  [swap(): return lax.ppermute(value, AXES, [(i, i ^ mask) for i in range(self.count)])]
    while x23 -> x0, local copies, waits for them, and re-layouts: 20.9 us -> none  [the longest x2 15.2 us: local(): lax.map(cross_back, (queries_two, mem_keys, mem_values, cross_lse, d_cros...]
    ppermute x110, starting transfers between devices: 95.6 us -> 106 us  [swap(): return lax.ppermute(value, AXES, [(i, i ^ mask) for i in range(self.count)])]
  transfers between devices with their start and end apart: 110 -> 110, of which waited for: 50 -> 46; matrix products, arithmetic and copies ran while one was open for 36% -> 24% of each run, Pallas kernels for 0% -> 5%
where the time goes in v2:
time: 760 us; the launch traced here: 749 us
  waiting for transfers between devices  319 us (42%)
  starting transfers between devices  106 us (14%)
  local copies, waits for them, and re-layouts  99.5 us (13%)
  matrix products  90.7 us (12%)
  Pallas kernels  89 us (12%)
  other arithmetic  40.2 us (5%)
    ppermute x110, waiting for transfers between devices, swap(): return lax.ppermute(value, AXES, [(i, i ^ mask) for i in range(self.count)])  319 us
    ppermute x110, starting transfers between devices, swap(): return lax.ppermute(value, AXES, [(i, i ^ mask) for i in range(self.count)])  106 us
    unnamed x327, local copies, waits for them, and re-layouts  64.3 us
    dot_general x20, matrix products, weight_grad(): lax.dot_general(left_rows, gradient, (((0,), (0,)), ((), ())), preferred_...  42.7 us
    dot_general x10, matrix products, project(): return jnp.dot(left_rows, weight, preferred_element_type=F32)  40.9 us
    pallas_call x4, Pallas kernels, back_natural(): pl.pallas_call(back_kernel, grid_spec=pltpu.PrefetchScalarGridSpec(num_sc...  34.8 us
    pallas_call x1, Pallas kernels, cross_attend_back(): pl.pallas_call(cross_back_kernel, grid_spec=pltpu.PrefetchScalarGridSpec(...  21.7 us
    pallas_call x1, Pallas kernels, cross_attend(): pl.pallas_call(cross_kernel, grid_spec=pltpu.PrefetchScalarGridSpec(num_s...  20.2 us
  transfers between devices with their start and end apart: 110, of which 46 were waited for; matrix products, arithmetic and copies ran while one was open for 24% of the time, Pallas kernels for 5%

profile of v2, /device:TPU:0, one launch (start us, length us, event | category | flops | bytes accessed | tf_op | source)
XLA Modules:
  0.0 749.1 jit_solution(2114569971547825672)
XLA Ops:
  42.2 13.8 %collective-permute-done.10 = bf16[2,8,128]{2,1,0:T(8,128)(2,1)S(1)} collective-permute-done((bf16[2,8,128]{2,1,0:T(8,128)(2,1)S(1)}, bf16[2,8,128]{2,1,0:T(8,128)(2,1)S(1)}, u32[]{:S(2)}, u32[]{:S(2)}) %collective-permute-start.10) | collective-permute-done | bytes 4128 | tf_op jit(solution)/shard_map/ppermute | solution.py:267
  73.0 21.4 %collective-permute-done.1 = bf16[4,2,32,1024]{3,2,0,1:T(8,128)(2,1)S(1)} collective-permute-done((bf16[4,2,32,1024]{3,2,0,1:T(8,128)(2,1)S(1)}, bf16[4,2,32,1024]{3,2,0,1:T(8,128)(2,1)S(1)}, u32[]{:S(2)}, u32[]{:S(2)}) %collective-permute-start.1) | collective-permute-done | bytes 524320 | tf_op jit(solution)/shard_map/ppermute | solution.py:267
  96.4 9.3 %collective-permute-done.22 = bf16[4,2,32,1024]{3,2,0,1:T(8,128)(2,1)S(1)} collective-permute-done((bf16[4,2,32,1024]{3,2,0,1:T(8,128)(2,1)S(1)}, bf16[4,2,32,1024]{3,2,0,1:T(8,128)(2,1)S(1)}, u32[]{:S(2)}, u32[]{:S(2)}) %collective-permute-start.22) | collective-permute-done | bytes 524320 | tf_op jit(solution)/shard_map/ppermute | solution.py:267
  131.8 8.1 %collective-permute-done.30 = bf16[2,128,1024]{2,1,0:T(8,128)(2,1)S(1)} collective-permute-done((bf16[2,128,1024]{2,1,0:T(8,128)(2,1)S(1)}, bf16[2,128,1024]{2,1,0:T(8,128)(2,1)S(1)}, u32[]{:S(2)}, u32[]{:S(2)}) %collective-permute-start.30) | collective-permute-done | bytes 524320 | tf_op jit(solution)/shard_map/ppermute | solution.py:267
  141.6 9.5 %collective-permute-done.2 = bf16[2,128,1024]{2,1,0:T(8,128)(2,1)S(1)} collective-permute-done((bf16[2,128,1024]{2,1,0:T(8,128)(2,1)S(1)}, bf16[2,128,1024]{2,1,0:T(8,128)(2,1)S(1)}, u32[]{:S(2)}, u32[]{:S(2)}) %collective-permute-start.2) | collective-permute-done | bytes 524320 | tf_op jit(solution)/shard_map/ppermute | solution.py:267
  161.5 11.3 %collective-permute-done.32 = bf16[2,128,1024]{2,1,0:T(8,128)(2,1)S(1)} collective-permute-done((bf16[2,128,1024]{2,1,0:T(8,128)(2,1)S(1)}, bf16[2,128,1024]{2,1,0:T(8,128)(2,1)S(1)}, u32[]{:S(2)}, u32[]{:S(2)}) %collective-permute-start.32) | collective-permute-done | bytes 524320 | tf_op jit(solution)/shard_map/ppermute | solution.py:267
  177.3 10.2 %collective-permute-done.4 = bf16[2,128,1024]{2,1,0:T(8,128)(2,1)S(1)} collective-permute-done((bf16[2,128,1024]{2,1,0:T(8,128)(2,1)S(1)}, bf16[2,128,1024]{2,1,0:T(8,128)(2,1)S(1)}, u32[]{:S(2)}, u32[]{:S(2)}) %collective-permute-start.4) | collective-permute-done | bytes 524320 | tf_op jit(solution)/shard_map/ppermute | solution.py:267
  189.2 22.7 %collective-permute-done.16 = bf16[2,128,1024]{2,1,0:T(8,128)(2,1)S(1)} collective-permute-done((bf16[2,128,1024]{2,1,0:T(8,128)(2,1)S(1)}, bf16[2,128,1024]{2,1,0:T(8,128)(2,1)S(1)}, u32[]{:S(2)}, u32[]{:S(2)}) %collective-permute-start.16) | collective-permute-done | bytes 524320 | tf_op jit(solution)/shard_map/ppermute | solution.py:267
  216.2 16.8 %collective-permute-done.39 = bf16[1,128,4096]{2,1,0:T(8,128)(2,1)} collective-permute-done((bf16[1,128,4096]{2,1,0:T(8,128)(2,1)S(1)}, bf16[1,128,4096]{2,1,0:T(8,128)(2,1)}, u32[]{:S(2)}, u32[]{:S(2)}) %collective-permute-start.39) | collective-permute-done | bytes 1048608 | tf_op jit(solution)/shard_map/ppermute | solution.py:267
  283.2 20.2 %cross_attend.1 = (bf16[256,1024]{1,0:T(8,128)(2,1)}, f32[2,8,1,256]{3,2,1,0:T(1,128)}) custom-call(s32[8]{0:T(128)} %fusion.148.place, s32[2]{0:T(128)} %lengths.3, bf16[256,1024]{1,0:T(8,128)(2,1)} %fusion.31.q, bf16[2048,1024]{1,0:T(8,128)(2,1)} %convolution_convert_fusion.3.k, bf16[2048,1024]{1,0:T(8,128)(2,1)} %add_convert_fusion.v), custom_call_target="tpu_custom_call" | custom-call | tf_op jit(solution)/shard_map/cross_attend/pallas_call | solution.py:120
  328.0 13.5 %multiply_convert_fusion = (bf16[256,4096]{1,0:T(8,128)(2,1)S(1)}, f32[256,4096]{1,0:T(8,128)S(1)}, f32[256,4096]{1,0:T(8,128)S(1)}) fusion(f32[4096]{0:T(1024)S(1)} %copy-done.99, bf16[256,1024]{1,0:T(8,128)(2,1)S(1)} %get-tuple-element.91, bf16[1,1024,4096]{2,1,0:T(8,128)(2,1)} %constant_dynamic-update-slice_fusion.64), kind=kOutput, calls=%fused_computation.20 | convolution fusion | flops 2216689664 | bytes 19415040 | tf_op jit(solution)/shard_map/dot_general | solution.py:17
  359.7 8.2 %back_natural.4 = f32[256,1024]{1,0:T(8,128)} custom-call(s32[8]{0:T(128)} %broadcast_xor_fusion.place, bf16[256,4096]{1,0:T(8,128)(2,1)} %get-tuple-element.60.refs_0_, bf16[1024,4096]{1,0:T(8,128)(2,1)} %bitcast.40.refs_1_), custom_call_target="tpu_custom_call" | custom-call | tf_op jit(solution)/shard_map/back_natural/pallas_call | solution.py:235
  377.2 21.7 %cross_attend_back.1 = (bf16[256,1024]{1,0:T(8,128)(2,1)}, bf16[2048,1024]{1,0:T(8,128)(2,1)}, bf16[2048,1024]{1,0:T(8,128)(2,1)}) custom-call(s32[8]{0:T(128)} %fusion.148.place, s32[2]{0:T(128)} %lengths.3, bf16[256,1024]{1,0:T(8,128)(2,1)} %fusion.31.q, bf16[2048,1024]{1,0:T(8,128)(2,1)} %convolution_convert_fusion.3.k, ...), custom_call_target="tpu_custom_call" | custom-call | tf_op jit(solution)/shard_map/cross_attend_back/pallas_call | solution.py:143
  416.4 7.9 %self_attend_back.1 = (bf16[256,1024]{1,0:T(8,128)(2,1)}, bf16[256,1024]{1,0:T(8,128)(2,1)}, bf16[256,1024]{1,0:T(8,128)(2,1)}) custom-call(s32[8]{0:T(128)} %fusion.148.place, bf16[256,1024]{1,0:T(8,128)(2,1)} %fusion.30.q, bf16[256,1024]{1,0:T(8,128)(2,1)} %convolution_convert_fusion.20.k, bf16[256,1024]{1,0:T(8,128)(2,1)} %fusion.34.v, ...), custom_call_target="tpu_custom_call" | custom-call | tf_op jit(solution)/shard_map/self_attend_back/pallas_call | solution.py:206
  473.0 15.5 %back_natural.7 = f32[2048,1024]{1,0:T(8,128)} custom-call(s32[8]{0:T(128)} %broadcast_xor_fusion.place, bf16[2048,1024]{1,0:T(8,128)(2,1)} %get-tuple-element.34.refs_0_, bf16[2048,1024]{1,0:T(8,128)(2,1)} %get-tuple-element.35.refs_1_, bf16[1024,1024]{1,0:T(8,128)(2,1)} %get-tuple-element.155.refs_2_, bf16[1024,1024]{1,0:T(8,128)(2,1)} %slice_bitcast_fusion.3.refs_3_), custom_call_target="tpu_custom_call" | custom-call | tf_op jit(solution)/shard_map/back_natural/pallas_call | solution.py:235
  522.3 10.4 %collective-permute-done.91 = bf16[2,128,1024]{2,1,0:T(8,128)(2,1)S(1)} collective-permute-done((bf16[2,128,1024]{2,1,0:T(8,128)(2,1)S(1)}, bf16[2,128,1024]{2,1,0:T(8,128)(2,1)S(1)}, u32[]{:S(2)}, u32[]{:S(2)}) %collective-permute-start.91) | collective-permute-done | bytes 524320 | tf_op jit(solution)/shard_map/ppermute | solution.py:267
  534.3 9.6 %collective-permute-done.71 = bf16[2,128,1024]{2,1,0:T(8,128)(2,1)S(1)} collective-permute-done((bf16[2,128,1024]{2,1,0:T(8,128)(2,1)S(1)}, bf16[2,128,1024]{2,1,0:T(8,128)(2,1)S(1)}, u32[]{:S(2)}, u32[]{:S(2)}) %collective-permute-start.71) | collective-permute-done | bytes 524320 | tf_op jit(solution)/shard_map/ppermute | solution.py:267
  544.7 9.5 %collective-permute-done.66 = bf16[2,128,1024]{2,1,0:T(8,128)(2,1)S(1)} collective-permute-done((bf16[2,128,1024]{2,1,0:T(8,128)(2,1)S(1)}, bf16[2,128,1024]{2,1,0:T(8,128)(2,1)S(1)}, u32[]{:S(2)}, u32[]{:S(2)}) %collective-permute-start.66) | collective-permute-done | bytes 524320 | tf_op jit(solution)/shard_map/ppermute | solution.py:267
  557.9 11.2 %collective-permute-done.81 = bf16[2,128,1024]{2,1,0:T(8,128)(2,1)S(1)} collective-permute-done((bf16[2,128,1024]{2,1,0:T(8,128)(2,1)S(1)}, bf16[2,128,1024]{2,1,0:T(8,128)(2,1)S(1)}, u32[]{:S(2)}, u32[]{:S(2)}) %collective-permute-start.81) | collective-permute-done | bytes 524320 | tf_op jit(solution)/shard_map/ppermute | solution.py:267
  641.3 28.9 %collective-permute-done.101 = bf16[2,128,4096]{2,1,0:T(8,128)(2,1)S(1)} collective-permute-done((bf16[2,128,4096]{2,1,0:T(8,128)(2,1)S(1)}, bf16[2,128,4096]{2,1,0:T(8,128)(2,1)S(1)}, u32[]{:S(2)}, u32[]{:S(2)}) %collective-permute-start.101) | collective-permute-done | bytes 2097184 | tf_op jit(solution)/shard_map/ppermute | solution.py:267
  673.1 16.1 %collective-permute-done.106 = bf16[2,512,1024]{2,1,0:T(8,128)(2,1)S(1)} collective-permute-done((bf16[2,512,1024]{2,1,0:T(8,128)(2,1)S(1)}, bf16[2,512,1024]{2,1,0:T(8,128)(2,1)S(1)}, u32[]{:S(2)}, u32[]{:S(2)}) %collective-permute-start.106) | collective-permute-done | bytes 2097184 | tf_op jit(solution)/shard_map/ppermute | solution.py:267
  691.8 14.7 %collective-permute-done.102 = bf16[128,4096]{1,0:T(8,128)(2,1)S(1)} collective-permute-done((bf16[128,4096]{1,0:T(8,128)(2,1)S(1)}, bf16[128,4096]{1,0:T(8,128)(2,1)S(1)}, u32[]{:S(2)}, u32[]{:S(2)}) %collective-permute-start.102) | collective-permute-done | bytes 1048608 | tf_op jit(solution)/shard_map/ppermute | solution.py:267
  710.1 14.3 %collective-permute-done.103 = bf16[2,32,4096]{2,1,0:T(8,128)(2,1)S(1)} collective-permute-done((bf16[2,32,4096]{2,1,0:T(8,128)(2,1)S(1)}, bf16[2,32,4096]{2,1,0:T(8,128)(2,1)S(1)}, u32[]{:S(2)}, u32[]{:S(2)}) %collective-permute-start.103) | collective-permute-done | bytes 524320 | tf_op jit(solution)/shard_map/ppermute | solution.py:267
  735.5 8.7 %collective-permute-done.104 = bf16[32,4096]{1,0:T(8,128)(2,1)S(1)} collective-permute-done((bf16[32,4096]{1,0:T(8,128)(2,1)S(1)}, bf16[32,4096]{1,0:T(8,128)(2,1)S(1)}, u32[]{:S(2)}, u32[]{:S(2)}) %collective-permute-start.104) | collective-permute-done | bytes 262176 | tf_op jit(solution)/shard_map/ppermute | solution.py:267
  (801 shorter events, 411.6 us)
Async XLA Ops:
  7.9 60.5 %collective-permute-start.21 = (bf16[4,1,32,1024]{3,2,0,1:T(8,128)(2,1)S(1)}, bf16[4,1,32,1024]{3,2,0,1:T(8,128)(2,1)S(1)}, u32[]{:S(2)}, u32[]{:S(2)}) collective-permute-start(bf16[4,1,32,1024]{3,2,0,1:T(8,128)(2,1)S(1)} %maximum_bitcast_fusion.5), channel_id=1, source_target_pairs={{0,2},{1,3},{2,0},{3,1},{4,6},{5,7},{6,4},{7,5},{8,10},{9,11},{10,... | collective-permute-start | bytes 786440 | tf_op jit(solution)/shard_map/ppermute | solution.py:267
  11.6 56.9 %collective-permute-start = (bf16[4,1,32,1024]{3,2,0,1:T(8,128)(2,1)S(1)}, bf16[4,1,32,1024]{3,2,0,1:T(8,128)(2,1)S(1)}, u32[]{:S(2)}, u32[]{:S(2)}) collective-permute-start(bf16[4,1,32,1024]{3,2,0,1:T(8,128)(2,1)S(1)} %maximum_bitcast_fusion.4), channel_id=1, source_target_pairs={{0,2},{1,3},{2,0},{3,1},{4,6},{5,7},{6,4},{7,5},{8,10},{9,11},{10,... | collective-permute-start | bytes 786440 | tf_op jit(solution)/shard_map/ppermute | solution.py:267
  12.0 56.3 %collective-permute-start.46 = (bf16[1,1,128,1024]{3,2,1,0:T(8,128)(2,1)}, bf16[1,1,128,1024]{3,2,1,0:T(8,128)(2,1)S(1)}, u32[]{:S(2)}, u32[]{:S(2)}) collective-permute-start(bf16[1,1,128,1024]{3,2,1,0:T(8,128)(2,1)} %bitcast.524), channel_id=1, source_target_pairs={{0,2},{1,3},{2,0},{3,1},{4,6},{5,7},{6,4},{7,5},{8,10},{9,11},{10,... | collective-permute-start | bytes 786440 | tf_op jit(solution)/shard_map/ppermute | solution.py:267
  14.5 56.3 %collective-permute-start.37 = (bf16[1,1,32,4096]{3,2,1,0:T(8,128)(2,1)}, bf16[1,1,32,4096]{3,2,1,0:T(8,128)(2,1)S(1)}, u32[]{:S(2)}, u32[]{:S(2)}) collective-permute-start(bf16[1,1,32,4096]{3,2,1,0:T(8,128)(2,1)} %bitcast.525), channel_id=1, source_target_pairs={{0,2},{1,3},{2,0},{3,1},{4,6},{5,7},{6,4},{7,5},{8,10},{9,11},{10,... | collective-permute-start | bytes 786440 | tf_op jit(solution)/shard_map/ppermute | solution.py:267
  68.4 48.4 %collective-permute-start.47 = (bf16[1,2,128,1024]{3,2,1,0:T(8,128)(2,1)S(1)}, bf16[1,2,128,1024]{3,2,1,0:T(8,128)(2,1)S(1)}, u32[]{:S(2)}, u32[]{:S(2)}) collective-permute-start(bf16[1,2,128,1024]{3,2,1,0:T(8,128)(2,1)S(1)} %maximum_bitcast_fusion.3), channel_id=1, source_target_pairs={{0,1},{1,0},{2,3},{3,2},{4,5},{5,4},{6,7},{7,6},{8,9},{9,8},{10,11... | collective-permute-start | bytes 1572872 | tf_op jit(solution)/shard_map/ppermute | solution.py:267
  71.0 42.9 %collective-permute-start.38 = (bf16[1,2,32,4096]{3,2,1,0:T(8,128)(2,1)S(1)}, bf16[1,2,32,4096]{3,2,1,0:T(8,128)(2,1)S(1)}, u32[]{:S(2)}, u32[]{:S(2)}) collective-permute-start(bf16[1,2,32,4096]{3,2,1,0:T(8,128)(2,1)S(1)} %maximum_bitcast_fusion.2), channel_id=1, source_target_pairs={{0,1},{1,0},{2,3},{3,2},{4,5},{5,4},{6,7},{7,6},{8,9},{9,8},{10,11... | collective-permute-start | bytes 1572872 | tf_op jit(solution)/shard_map/ppermute | solution.py:267
  174.4 38.2 %collective-permute-start.48 = (bf16[1,512,1024]{2,1,0:T(8,128)(2,1)}, bf16[1,512,1024]{2,1,0:T(8,128)(2,1)}, u32[]{:S(2)}, u32[]{:S(2)}) collective-permute-start(bf16[1,512,1024]{2,1,0:T(8,128)(2,1)} %bitcast.49), channel_id=1, source_target_pairs={{0,8},{1,9},{2,10},{3,11},{4,12},{5,13},{6,14},{7,15},{8,0},{9,1},... | collective-permute-start | bytes 3145736 | tf_op jit(solution)/shard_map/ppermute | solution.py:267
  176.0 38.1 %collective-permute-start.49 = (bf16[1,512,1024]{2,1,0:T(8,128)(2,1)}, bf16[1,512,1024]{2,1,0:T(8,128)(2,1)}, u32[]{:S(2)}, u32[]{:S(2)}) collective-permute-start(bf16[1,512,1024]{2,1,0:T(8,128)(2,1)} %bitcast.49), channel_id=1, source_target_pairs={{0,16},{1,17},{2,18},{3,19},{4,20},{5,21},{6,22},{7,23},{8,24},{9,... | collective-permute-start | bytes 3145736 | tf_op jit(solution)/shard_map/ppermute | solution.py:267
  176.6 35.3 %collective-permute-start.16 = (bf16[2,128,1024]{2,1,0:T(8,128)(2,1)S(1)}, bf16[2,128,1024]{2,1,0:T(8,128)(2,1)S(1)}, u32[]{:S(2)}, u32[]{:S(2)}) collective-permute-start(bf16[2,128,1024]{2,1,0:T(8,128)(2,1)S(1)} %collective-permute-done.15), channel_id=1, source_target_pairs={{0,8},{1,9},{2,10},{3,11},{4,12},{5,13},{6,14},{7,15},{8,0},{9,1},... | collective-permute-start | bytes 1572872 | tf_op jit(solution)/shard_map/ppermute | solution.py:267
  187.5 45.4 %collective-permute-start.39 = (bf16[1,128,4096]{2,1,0:T(8,128)(2,1)S(1)}, bf16[1,128,4096]{2,1,0:T(8,128)(2,1)}, u32[]{:S(2)}, u32[]{:S(2)}) collective-permute-start(bf16[1,128,4096]{2,1,0:T(8,128)(2,1)S(1)} %bitcast.473), channel_id=1, source_target_pairs={{0,8},{1,9},{2,10},{3,11},{4,12},{5,13},{6,14},{7,15},{8,0},{9,1},... | collective-permute-start | bytes 3145736 | tf_op jit(solution)/shard_map/ppermute | solution.py:267
  212.6 108.8 %collective-permute-start.42 = (bf16[1,128,4096]{2,1,0:T(8,128)(2,1)S(1)}, bf16[1,128,4096]{2,1,0:T(8,128)(2,1)}, u32[]{:S(2)}, u32[]{:S(2)}) collective-permute-start(bf16[1,128,4096]{2,1,0:T(8,128)(2,1)S(1)} %bitcast.475), channel_id=1, source_target_pairs={{0,4},{1,5},{2,6},{3,7},{4,0},{5,1},{6,2},{7,3},{8,12},{9,13},{10,... | collective-permute-start | bytes 3145736 | tf_op jit(solution)/shard_map/ppermute | solution.py:267
  214.2 99.3 %collective-permute-start.51 = (bf16[1,512,1024]{2,1,0:T(8,128)(2,1)}, bf16[1,512,1024]{2,1,0:T(8,128)(2,1)}, u32[]{:S(2)}, u32[]{:S(2)}) collective-permute-start(bf16[1,512,1024]{2,1,0:T(8,128)(2,1)} %bitcast.49), channel_id=1, source_target_pairs={{0,4},{1,5},{2,6},{3,7},{4,0},{5,1},{6,2},{7,3},{8,12},{9,13},{10,... | collective-permute-start | bytes 3145736 | tf_op jit(solution)/shard_map/ppermute | solution.py:267
  242.8 73.4 %collective-permute-start.41 = (bf16[1,128,4096]{2,1,0:T(8,128)(2,1)}, bf16[1,128,4096]{2,1,0:T(8,128)(2,1)}, u32[]{:S(2)}, u32[]{:S(2)}) collective-permute-start(bf16[1,128,4096]{2,1,0:T(8,128)(2,1)} %collective-permute-done.39), channel_id=1, source_target_pairs={{0,16},{1,17},{2,18},{3,19},{4,20},{5,21},{6,22},{7,23},{8,24},{9,... | collective-permute-start | bytes 3145736 | tf_op jit(solution)/shard_map/ppermute | solution.py:267
  245.1 66.0 %collective-permute-start.50 = (bf16[1,512,1024]{2,1,0:T(8,128)(2,1)}, bf16[1,512,1024]{2,1,0:T(8,128)(2,1)}, u32[]{:S(2)}, u32[]{:S(2)}) collective-permute-start(bf16[1,512,1024]{2,1,0:T(8,128)(2,1)} %collective-permute-done.49), channel_id=1, source_target_pairs={{0,8},{1,9},{2,10},{3,11},{4,12},{5,13},{6,14},{7,15},{8,0},{9,1},... | collective-permute-start | bytes 3145736 | tf_op jit(solution)/shard_map/ppermute | solution.py:267
  266.5 49.7 %collective-permute-start.52 = (bf16[1,512,1024]{2,1,0:T(8,128)(2,1)}, bf16[1,512,1024]{2,1,0:T(8,128)(2,1)}, u32[]{:S(2)}, u32[]{:S(2)}) collective-permute-start(bf16[1,512,1024]{2,1,0:T(8,128)(2,1)} %collective-permute-done.48), channel_id=1, source_target_pairs={{0,4},{1,5},{2,6},{3,7},{4,0},{5,1},{6,2},{7,3},{8,12},{9,13},{10,... | collective-permute-start | bytes 3145736 | tf_op jit(solution)/shard_map/ppermute | solution.py:267
  452.1 44.9 %collective-permute-start.95 = (bf16[512,1024]{1,0:T(8,128)(2,1)}, bf16[512,1024]{1,0:T(8,128)(2,1)}, u32[]{:S(2)}, u32[]{:S(2)}) collective-permute-start(bf16[512,1024]{1,0:T(8,128)(2,1)} %convolution_convert_fusion.4), channel_id=1, source_target_pairs={{0,4},{1,5},{2,6},{3,7},{4,0},{5,1},{6,2},{7,3},{8,12},{9,13},{10,... | collective-permute-start | bytes 3145736 | tf_op jit(solution)/shard_map/ppermute | solution.py:267
  453.7 38.0 %collective-permute-start.55 = (bf16[512,1024]{1,0:T(8,128)(2,1)}, bf16[512,1024]{1,0:T(8,128)(2,1)}, u32[]{:S(2)}, u32[]{:S(2)}) collective-permute-start(bf16[512,1024]{1,0:T(8,128)(2,1)} %convolution_convert_fusion.14), channel_id=1, source_target_pairs={{0,4},{1,5},{2,6},{3,7},{4,0},{5,1},{6,2},{7,3},{8,12},{9,13},{10,... | collective-permute-start | bytes 3145736 | tf_op jit(solution)/shard_map/ppermute | solution.py:267
  469.5 37.2 %collective-permute-start.90 = (bf16[512,1024]{1,0:T(8,128)(2,1)}, bf16[512,1024]{1,0:T(8,128)(2,1)}, u32[]{:S(2)}, u32[]{:S(2)}) collective-permute-start(bf16[512,1024]{1,0:T(8,128)(2,1)} %convolution_convert_fusion.16), channel_id=1, source_target_pairs={{0,4},{1,5},{2,6},{3,7},{4,0},{5,1},{6,2},{7,3},{8,12},{9,13},{10,... | collective-permute-start | bytes 3145736 | tf_op jit(solution)/shard_map/ppermute | solution.py:267
  500.4 122.3 %collective-permute-start.100 = (bf16[512,4096]{1,0:T(8,128)(2,1)S(1)}, bf16[512,4096]{1,0:T(8,128)(2,1)S(1)}, u32[]{:S(2)}, u32[]{:S(2)}) collective-permute-start(bf16[512,4096]{1,0:T(8,128)(2,1)S(1)} %copy-done.22), channel_id=1, source_target_pairs={{0,4},{1,5},{2,6},{3,7},{4,0},{5,1},{6,2},{7,3},{8,12},{9,13},{10,... | collective-permute-start | bytes 12582920 | tf_op jit(solution)/shard_map/ppermute | solution.py:267
  502.3 135.5 %collective-permute-start.105 = (bf16[2048,1024]{1,0:T(8,128)(2,1)}, bf16[2048,1024]{1,0:T(8,128)(2,1)S(1)}, u32[]{:S(2)}, u32[]{:S(2)}) collective-permute-start(bf16[2048,1024]{1,0:T(8,128)(2,1)} %convolution_convert_fusion.2), channel_id=1, source_target_pairs={{0,4},{1,5},{2,6},{3,7},{4,0},{5,1},{6,2},{7,3},{8,12},{9,13},{10,... | collective-permute-start | bytes 12582920 | tf_op jit(solution)/shard_map/ppermute | solution.py:267
  627.3 42.9 %collective-permute-start.101 = (bf16[2,128,4096]{2,1,0:T(8,128)(2,1)S(1)}, bf16[2,128,4096]{2,1,0:T(8,128)(2,1)S(1)}, u32[]{:S(2)}, u32[]{:S(2)}) collective-permute-start(bf16[2,128,4096]{2,1,0:T(8,128)(2,1)S(1)} %bitcast.477), channel_id=1, source_target_pairs={{0,16},{1,17},{2,18},{3,19},{4,20},{5,21},{6,22},{7,23},{8,24},{9,... | collective-permute-start | bytes 6291464 | tf_op jit(solution)/shard_map/ppermute | solution.py:267
  633.4 39.7 %collective-permute-start.84 = (bf16[32,1024]{1,0:T(8,128)(2,1)S(1)}, bf16[32,1024]{1,0:T(8,128)(2,1)S(1)}, u32[]{:S(2)}, u32[]{:S(2)}) collective-permute-start(bf16[32,1024]{1,0:T(8,128)(2,1)S(1)} %fusion.137), channel_id=1, source_target_pairs={{0,2},{1,3},{2,0},{3,1},{4,6},{5,7},{6,4},{7,5},{8,10},{9,11},{10,... | collective-permute-start | bytes 196616 | tf_op jit(solution)/shard_map/ppermute | solution.py:267
  640.7 48.6 %collective-permute-start.106 = (bf16[2,512,1024]{2,1,0:T(8,128)(2,1)S(1)}, bf16[2,512,1024]{2,1,0:T(8,128)(2,1)S(1)}, u32[]{:S(2)}, u32[]{:S(2)}) collective-permute-start(bf16[2,512,1024]{2,1,0:T(8,128)(2,1)S(1)} %fusion.11), channel_id=1, source_target_pairs={{0,8},{1,9},{2,10},{3,11},{4,12},{5,13},{6,14},{7,15},{8,0},{9,1},... | collective-permute-start | bytes 6291464 | tf_op jit(solution)/shard_map/ppermute | solution.py:267
  671.0 35.4 %collective-permute-start.102 = (bf16[128,4096]{1,0:T(8,128)(2,1)S(1)}, bf16[128,4096]{1,0:T(8,128)(2,1)S(1)}, u32[]{:S(2)}, u32[]{:S(2)}) collective-permute-start(bf16[128,4096]{1,0:T(8,128)(2,1)S(1)} %fusion.39), channel_id=1, source_target_pairs={{0,8},{1,9},{2,10},{3,11},{4,12},{5,13},{6,14},{7,15},{8,0},{9,1},... | collective-permute-start | bytes 3145736 | tf_op jit(solution)/shard_map/ppermute | solution.py:267
  (211 other events, 2993.1 us)

commit v3 on v2

v3 whole, which is shorter than its diff:
```python
import functools

import jax
import jax.numpy as jnp
from jax import lax
from jax.experimental import pallas as pl
from jax.experimental.pallas import tpu as pltpu
from jax.sharding import PartitionSpec as P

HD = 64
EPSILON = 1e-05
MASKED = -1e30
AXES = ("wide", "narrow")
BF = jnp.bfloat16
F32 = jnp.float32


def project(left_rows, weight):
    return jnp.dot(left_rows, weight, preferred_element_type=F32)


def project_back(gradient, weight):
    return lax.dot_general(gradient, weight, (((1,), (1,)), ((), ())), preferred_element_type=F32)


def weight_grad(left_rows, gradient):
    return lax.dot_general(left_rows, gradient, (((0,), (0,)), ((), ())), preferred_element_type=F32)


def column_sums(gradient):
    return jnp.sum(gradient.astype(F32), axis=0)


def layer_norm(hidden, gain_row, shift_row):
    average = jnp.mean(hidden, axis=-1, keepdims=True)
    centred = hidden - average
    variance = jnp.mean(centred * centred, axis=-1, keepdims=True)
    return centred * lax.rsqrt(variance + EPSILON) * gain_row + shift_row


def gelu_exact(pre_gelu):
    return jax.nn.gelu(pre_gelu, approximate=False)


def pair_stack(rows):
    lane = lax.broadcasted_iota(jnp.int32, rows.shape, 1)
    zero = jnp.zeros_like(rows)
    return jnp.concatenate(
        [jnp.where(lane < HD, rows, zero), jnp.where(lane >= HD, rows, zero)], axis=0
    )


def pair_merge(stacked):
    t = stacked.shape[0] // 2
    lane = lax.broadcasted_iota(jnp.int32, (t, 2 * HD), 1)
    return jnp.where(lane < HD, stacked[:t], stacked[t:])


def dot_nt(a, b):
    return lax.dot_general(a, b, (((1,), (1,)), ((), ())), preferred_element_type=F32)


def dot_tn(a, b):
    return lax.dot_general(a, b, (((0,), (0,)), ((), ())), preferred_element_type=F32)


def dot_nn(a, b):
    return lax.dot_general(a, b, (((1,), (0,)), ((), ())), preferred_element_type=F32)


def masked_scores(k, qs, length):
    scores = dot_nt(k, qs)
    slot = lax.broadcasted_iota(jnp.int32, scores.shape, 0)
    if length is None:
        seen = lax.broadcasted_iota(jnp.int32, scores.shape, 1) % (scores.shape[1] // 2)
        return jnp.where(slot <= seen, scores, MASKED)
    return jnp.where(slot < length, scores, MASKED)


def attend_pair(q, k, v, length):
    scores = masked_scores(k, pair_stack(q), length)
    top = jnp.max(scores, axis=0, keepdims=True)
    weights = jnp.exp(scores - top)
    total = jnp.sum(weights, axis=0, keepdims=True)
    chances = (weights * (1.0 / total)).astype(BF)
    return pair_merge(dot_tn(chances, v)).astype(BF), top + jnp.log(total)


def attend_pair_back(q, k, v, lse, d_out, length):
    qs, ds_out = pair_stack(q), pair_stack(d_out)
    chances = jnp.exp(masked_scores(k, qs, length) - lse)
    d_chances = dot_nt(v, ds_out)
    row = jnp.sum(d_chances * chances, axis=0, keepdims=True)
    d_scores = (chances * (d_chances - row)).astype(BF)
    d_q = pair_merge(dot_tn(d_scores, k)).astype(BF)
    d_k = dot_nn(d_scores, qs).astype(BF)
    d_v = dot_nn(chances.astype(BF), ds_out).astype(BF)
    return d_q, d_k, d_v


PAIR = 2 * HD


def cross_kernel(place, length, q, k, v, *refs):
    out, lse = refs[-2:]
    out[...], lse[0, 0] = attend_pair(q[...], k[...], v[...], length[0])


def cross_back_kernel(place, length, q, k, v, lse, d_out, *refs):
    d_q, d_k, d_v = refs[-3:]
    d_q[...], d_k[...], d_v[...] = attend_pair_back(
        q[...], k[...], v[...], lse[0, 0], d_out[...], length[0]
    )
    d_q[...] = d_q[...] * jnp.asarray(HD**-0.5, BF)


def cross_call(kernel, q, k, lengths, place, item, values, in_specs, out_specs, out_shape, so_far):
    return pl.pallas_call(
        kernel,
        grid_spec=pltpu.PrefetchScalarGridSpec(
            num_scalar_prefetch=2,
            grid=(q.shape[1] // PAIR,),
            in_specs=in_specs + [pl.BlockSpec(memory_space=pl.ANY)] * len(so_far),
            out_specs=out_specs,
        ),
        out_shape=out_shape,
        input_output_aliases={2 + len(values) + i: i for i in range(len(so_far))},
        name="cross_attend",
    )(place, lax.slice_in_dim(lengths, item, item + 1), *values, *so_far)


def cross_specs(q, k, items, item):
    t, s = q.shape[0] // items, k.shape[0] // items
    rows = pl.BlockSpec((t, PAIR), lambda j, *_: (item, j))
    slots = pl.BlockSpec((s, PAIR), lambda j, *_: (item, j))
    placed = pl.BlockSpec((t, PAIR), lambda j, place, length: (item, place[j]))
    lse = pl.BlockSpec((1, 1, 1, 2 * t), lambda j, *_: (item, j, 0, 0))
    return rows, slots, placed, lse


def cross_attend(q, k, v, lengths, place, item, so_far):
    items = lengths.shape[0]
    rows, slots, placed, lse = cross_specs(q, k, items, item)
    out_shape = [
        jax.ShapeDtypeStruct(q.shape, BF),
        jax.ShapeDtypeStruct((items, q.shape[1] // PAIR, 1, 2 * q.shape[0] // items), F32),
    ]
    return cross_call(
        cross_kernel, q, k, lengths, place, item, (q, k, v),
        [rows, slots, slots], [placed, lse], out_shape, so_far,
    )


def cross_attend_back(q, k, v, lse, d_out, lengths, place, item, so_far):
    rows, slots, placed, lse_spec = cross_specs(q, k, lengths.shape[0], item)
    out_shape = [jax.ShapeDtypeStruct(a.shape, BF) for a in (q, k, k)]
    return cross_call(
        cross_back_kernel, q, k, lengths, place, item, (q, k, v, lse, d_out),
        [rows, slots, slots, lse_spec, placed], [rows, slots, slots], out_shape, so_far,
    )


def lanes(ref, at):
    return ref[:, pl.ds(pl.multiple_of(at * PAIR, PAIR), PAIR)]


def self_kernel(place, q, k, v, out, lse):
    for j in range(q.shape[1] // PAIR):
        cut = slice(j * PAIR, (j + 1) * PAIR)
        found, lse[0, j] = attend_pair(q[:, cut], k[:, cut], v[:, cut], None)
        out[:, pl.ds(pl.multiple_of(place[j] * PAIR, PAIR), PAIR)] = found


def self_back_kernel(place, q, k, v, lse, d_out, d_q, d_k, d_v):
    for j in range(q.shape[1] // PAIR):
        cut = slice(j * PAIR, (j + 1) * PAIR)
        found = attend_pair_back(
            q[:, cut], k[:, cut], v[:, cut], lse[0, j], lanes(d_out, place[j]), None
        )
        d_q[:, cut] = found[0] * jnp.asarray(HD**-0.5, BF)
        d_k[:, cut] = found[1]
        d_v[:, cut] = found[2]


def self_attend(qkv, items, place):
    _, rows, width = qkv.shape
    t = rows // items

    def part(i):
        return pl.BlockSpec((None, t, width), lambda b, *_: (i, b, 0))

    lse = pl.BlockSpec((1, width // PAIR, 1, 2 * t), lambda b, *_: (b, 0, 0, 0))
    return pl.pallas_call(
        self_kernel,
        grid_spec=pltpu.PrefetchScalarGridSpec(
            num_scalar_prefetch=1,
            grid=(items,),
            in_specs=[part(0), part(1), part(2)],
            out_specs=[pl.BlockSpec((t, width), lambda b, *_: (b, 0)), lse],
        ),
        out_shape=[
            jax.ShapeDtypeStruct((rows, width), BF),
            jax.ShapeDtypeStruct((items, width // PAIR, 1, 2 * t), F32),
        ],
        name="self_attend",
    )(place, qkv, qkv, qkv)


def self_attend_back(qkv, lse, d_out, items, place):
    _, m, width = qkv.shape
    t = m // items

    def part(i):
        return pl.BlockSpec((None, t, width), lambda b, *_: (i, b, 0))

    rows = pl.BlockSpec((t, width), lambda b, *_: (b, 0))
    lse_spec = pl.BlockSpec((1, width // PAIR, 1, 2 * t), lambda b, *_: (b, 0, 0, 0))
    return pl.pallas_call(
        self_back_kernel,
        grid_spec=pltpu.PrefetchScalarGridSpec(
            num_scalar_prefetch=1,
            grid=(items,),
            in_specs=[part(0), part(1), part(2), lse_spec, rows],
            out_specs=[rows] * 3,
        ),
        out_shape=[jax.ShapeDtypeStruct((m, width), BF)] * 3,
        name="self_attend_back",
    )(place, qkv, qkv, qkv, lse, d_out)


def stacked(array, i, **kw):
    return pl.BlockSpec((None,) + array.shape[1:], lambda *_: (i, 0, 0), **kw)


def project_kernel(scales, x0, x1, near, far, bias, out):
    total = dot_nn(x0[...], near[...]) + dot_nn(x1[...], far[...]) + bias[...]
    j = pl.program_id(0)
    scale = scales[0]
    for i in range(1, len(scales)):
        scale = jnp.where(j == i, scales[i], scale)
    out[...] = (total * scale).astype(out.dtype)


def stack_project(rows, weights, first, bias, scales, dtype):
    near, far = weights
    m, h = rows[0].shape
    n = near.shape[2]
    count = len(scales)
    whole = pl.BlockSpec((m, h), lambda j: (0, 0))
    weight = pl.BlockSpec((None, h, n), lambda j: (first + j, 0, 0))
    return pl.pallas_call(
        functools.partial(project_kernel, scales),
        grid=(count,),
        in_specs=[whole, whole, weight, weight, pl.BlockSpec((None, 1, n), lambda j: (j, 0, 0))],
        out_specs=pl.BlockSpec((None, m, n), lambda j: (j, 0, 0)),
        out_shape=jax.ShapeDtypeStruct((count, m, n), dtype),
        name="stack_project",
    )(*rows, near, far, bias)


def grads_kernel(products, *refs):
    ins, (keep, send) = refs[:-2], refs[-2:]
    for i, (left, right, start) in enumerate(products):

        @pl.when(pl.program_id(0) == i)
        def _():
            to = ins[right][:, start : start + keep.shape[1]]
            keep[...] = dot_tn(ins[left][...], to).astype(BF)
            send[...] = dot_tn(ins[left + 1][...], to).astype(BF)


def stack_grads(lefts, rights, products):
    arrays = [half for left in lefts for half in left] + list(rights)
    n = products[0][3]
    r = lefts[0][0].shape[1]
    table = [(2 * left, 2 * len(lefts) + right, start) for left, right, start, _ in products]
    out = pl.BlockSpec((None, r, n), lambda i: (i, 0, 0))
    shape = jax.ShapeDtypeStruct((len(products), r, n), BF)
    return pl.pallas_call(
        functools.partial(grads_kernel, table),
        grid=(len(products),),
        in_specs=[
            pl.BlockSpec(a.shape, lambda i: (0, 0), pipeline_mode=pl.Buffered(1)) for a in arrays
        ],
        out_specs=[out, out],
        out_shape=[shape, shape],
        name="stack_grads",
    )(*arrays)


def back_kernel(blocks, *refs):
    count = (len(refs) - 1) // 3
    out = refs[-1]
    size = out.shape[1] // blocks.shape[0]
    for half in range(2):
        total = dot_nt(refs[0][...], refs[count + half][...])
        for i in range(1, count):
            total = total + dot_nt(refs[i][...], refs[count + 2 * i + half][...])
        for i in range(total.shape[1] // size):
            to = blocks[half * (blocks.shape[0] // 2) + i]
            at = pl.ds(pl.multiple_of(to * size, 128), size)
            out[:, at] = total[:, i * size : (i + 1) * size].astype(out.dtype)


def back_natural(lefts, weights, picks, blocks, rows, dtype):
    m = lefts[0].shape[0]
    near, far = weights
    if picks is None:
        near, far, picks = near[None], far[None], [0]
    n = 2 * near.shape[1]
    in_specs = [pl.BlockSpec((rows, a.shape[1]), lambda i, *_: (i, 0)) for a in lefts]
    values = []
    for p in picks:
        in_specs += [stacked(near, p, pipeline_mode=pl.Buffered(1))] * 2
        values += [near, far]
    return pl.pallas_call(
        back_kernel,
        grid_spec=pltpu.PrefetchScalarGridSpec(
            num_scalar_prefetch=1,
            grid=(m // rows,),
            in_specs=in_specs,
            out_specs=pl.BlockSpec((rows, n), lambda i, *_: (i, 0)),
        ),
        out_shape=jax.ShapeDtypeStruct((m, n), dtype),
        name="back_natural",
    )(blocks, *lefts, *values)


def memory_kernel(x0, x1, k0, k1, v0, v1, bias, keys, values):
    keys[...] = (dot_nn(x0[...], k0[...]) + dot_nn(x1[...], k1[...])).astype(BF)
    total = dot_nn(x0[...], v0[...]) + dot_nn(x1[...], v1[...])
    values[...] = (total + bias[...]).astype(BF)


def memory_project(rows, weights, key_pick, value_pick, bias, block):
    near, far = weights
    m, h = rows[0].shape
    n = near.shape[2]
    once = pl.Buffered(1)
    return pl.pallas_call(
        memory_kernel,
        grid=(m // block,),
        in_specs=[pl.BlockSpec((block, h), lambda i: (i, 0))] * 2
        + [stacked(near, key_pick, pipeline_mode=once)] * 2
        + [stacked(near, value_pick, pipeline_mode=once)] * 2
        + [pl.BlockSpec((1, n), lambda i: (0, 0))],
        out_specs=[pl.BlockSpec((block, n), lambda i: (i, 0))] * 2,
        out_shape=[jax.ShapeDtypeStruct((m, n), BF)] * 2,
        name="memory_project",
    )(*rows, near, far, near, far, bias)


def add_split_kernel(*refs):
    count = len(refs) // 6
    for i in range(count):
        keep_s, got_s, keep_k, got_k = refs[4 * i : 4 * i + 4]
        send, keep = refs[4 * count + 2 * i : 4 * count + 2 * i + 2]
        send[...] = (keep_s[...].astype(F32) + got_s[...].astype(F32)).astype(BF)
        keep[...] = (keep_k[...].astype(F32) + got_k[...].astype(F32)).astype(BF)


def add_split(parts):
    in_specs, out_specs, shapes, values = [], [], [], []
    for keep, got, first, count, low in parts:
        _, blocks, rows, n = keep.shape

        def spec(value, first=first, low=low, rows=rows, n=n):
            def index(i, j):
                high, rest = j >> low, j & ((1 << low) - 1)
                return first + i, (high << (low + 1)) | (value << low) | rest, 0, 0

            return pl.BlockSpec((None, None, rows, n), index)

        in_specs += [spec(1), spec(1), spec(0), spec(0)]
        values += [keep, got, keep, got]
        out_specs += [pl.BlockSpec((None, None, rows, n), lambda i, j: (i, j, 0, 0))] * 2
        shapes += [jax.ShapeDtypeStruct((count, blocks // 2, rows, n), BF)] * 2
    found = pl.pallas_call(
        add_split_kernel,
        grid=shapes[0].shape[:2],
        in_specs=in_specs,
        out_specs=out_specs,
        out_shape=shapes,
        name="add_split",
    )(*values)
    return found[0::2], found[1::2]


class Plan:
    def __init__(self):
        self.wide = lax.axis_size("wide")
        self.narrow = lax.axis_size("narrow")
        self.count = self.wide * self.narrow
        self.w = lax.axis_index("wide")
        self.z = lax.axis_index("narrow")
        self.me = self.w * self.narrow + self.z
        bits = self.wide.bit_length() - 1
        rest = [1 << b for b in range(1, bits)]
        half = len(rest) // 2
        self.core = self.narrow
        xs = [m * self.narrow for m in rest[:half]]
        ys = [m * self.narrow for m in rest[half:]]
        self.across = sorted([*xs, *ys], reverse=True)
        self.routes = ([*xs, *ys], [*ys, *xs])
        self.zs = [1 << b for b in range(self.narrow.bit_length() - 1)]
        self.order = [r for r in range(self.wide) if r % 2 == 0] + [
            r for r in range(self.wide) if r % 2 == 1
        ]

    def bit(self, index, mask):
        return (index // mask) % 2

    def step(self, stream, after=None, during=None):
        sends = [value for value, _ in stream.sends]
        if after is not None:
            sends, _ = lax.optimization_barrier((sends, after))
        got = [
            lax.ppermute(v, AXES, [(i, i ^ m) for i in range(self.count)])
            for v, (_, m) in zip(sends, stream.sends)
        ]
        if during is not None:
            got, _ = lax.optimization_barrier((got, during))
        stream.feed(got)
        return got

    def across_steps(self, stream, after, during=None):
        for _ in self.across[1:]:
            after = self.step(stream, after, during)
        return after

    def finish(self, stream):
        while stream.result is None:
            self.step(stream)

    def relative(self, rows):
        size = rows.shape[1] // self.wide
        pieces = [
            lax.dynamic_slice_in_dim(rows, (jnp.int32(r) ^ self.w) * size, size, axis=1)
            for r in self.order
        ]
        half = self.wide // 2
        return jnp.concatenate(pieces[:half], axis=1), jnp.concatenate(pieces[half:], axis=1)

    def natural(self, rows):
        size = rows.shape[1] // self.wide
        pieces = []
        for i in range(self.wide):
            r = jnp.int32(i) ^ self.w
            place = (r % 2) * (self.wide // 2) + r // 2
            pieces.append(lax.dynamic_slice_in_dim(rows, place * size, size, axis=1))
        return jnp.concatenate(pieces, axis=1)

    def places(self):
        r = lax.iota(jnp.int32, self.wide) ^ self.w
        return (r % 2) * (self.wide // 2) + r // 2

    def blocks(self):
        return jnp.array(self.order, jnp.int32) ^ self.w

    def gather(self, part, split, join):
        k, rows, n = part.shape
        have = part.reshape(k, 1, rows, n)
        for mask in reversed(self.zs):
            (other,) = yield [(have, mask)]
            low = self.bit(self.z, mask) == 0
            have = jnp.stack(
                [jnp.where(low, have, other), jnp.where(low, other, have)], axis=2
            ).reshape(k, -1, rows, n)
        sets = [piece for piece in split(have.reshape(k, -1, n))]
        bits = len(self.across)
        for step in range(bits):
            got = yield [(s, route[step]) for s, route in zip(sets, self.routes)]
            sets = [jnp.stack([s, g]) for s, g in zip(sets, got)]
        whole = []
        for s, route in zip(sets, self.routes):
            axes = [list(reversed(route)).index(mask) for mask in self.across]
            s = jnp.transpose(s, [bits, *axes, bits + 1, bits + 2])
            whole.append(s.reshape(s.shape[0], -1, s.shape[-1]))
        near = join(*whole)
        (far,) = yield [(near, self.core)]
        return near, far

    def scatter(self, lefts, rights, products):
        keep, send = stack_grads(lefts, rights, products)
        (got,) = yield [(send, self.core)]
        count, r, n = keep.shape
        bits = len(self.across)
        shape = (count, 1 << bits, r >> bits, n)
        keep, got = keep.reshape(shape), got.reshape(shape)
        pairs = [(keep, got, 0, count // 2), (keep, got, count // 2, count // 2)]
        lefts = [list(self.across) for _ in pairs]
        for step in reversed(range(bits)):
            masks, parts = [], []
            for i, pair in enumerate(pairs):
                mask = self.routes[i][step]
                axis = lefts[i].index(mask)
                parts.append((*pair, len(lefts[i]) - 1 - axis))
                lefts[i].pop(axis)
                masks.append(mask)
            sends, keeps = add_split(parts)
            gots = yield list(zip(sends, masks))
            pairs = [(k, g, 0, count // 2) for k, g in zip(keeps, gots)]
        acc = jnp.concatenate([k.astype(F32) + g.astype(F32) for k, g, _, _ in pairs], axis=0)
        own = (r >> bits) // self.narrow
        acc = acc.reshape((count,) + (2,) * len(self.zs) + (own, n))
        for mask in self.zs:
            axis = len(acc.shape) - 3
            place = self.bit(self.z, mask)
            send = lax.dynamic_index_in_dim(acc, 1 - place, axis, keepdims=False).astype(BF)
            acc = lax.dynamic_index_in_dim(acc, place, axis, keepdims=False)
            (got,) = yield [(send, mask)]
            acc = acc + got.astype(F32)
        return acc

    def gather_small(self, vector):
        n = vector.shape[0]
        have = vector.reshape(1, n // 128, 128)
        for mask in [1 << b for b in range(self.count.bit_length() - 1)]:
            (other,) = yield [(have, mask)]
            low = self.bit(self.me, mask) == 0
            have = jnp.concatenate(
                [jnp.where(low, have, other), jnp.where(low, other, have)], axis=0
            )
        return have.reshape(self.count, n)

    def scatter_small(self, table):
        n = table.shape[1]
        have = table.reshape(self.count, n // 128, 128)
        for mask in [1 << b for b in reversed(range(self.count.bit_length() - 1))]:
            place = self.bit(self.me, mask)
            keep = lax.dynamic_slice_in_dim(have, place * mask, mask, axis=0)
            send = lax.dynamic_slice_in_dim(have, (1 - place) * mask, mask, axis=0)
            (got,) = yield [(send, mask)]
            have = keep + got
        return have.reshape(n)


class Stream:
    def __init__(self, steps):
        self.steps, self.result = steps, None
        self.sends = next(steps)

    def feed(self, got):
        try:
            self.sends = self.steps.send(list(got))
        except StopIteration as end:
            self.result = end.value


def pad_lanes(table):
    return jnp.pad(table, ((0, 0), (0, -table.shape[1] % 1024)))


def local(
    inputs,
    memory,
    mem_lengths,
    self_qkv,
    self_out,
    self_bias,
    self_gain,
    cross_qkv,
    cross_out,
    cross_bias,
    cross_gain,
    ffn_in,
    ffn_out,
    ffn_bias_in,
    ffn_bias_out,
    ffn_gain,
    out_grad,
):
    plan = Plan()
    scaling = HD ** (-0.5)
    item_count, mem_slots, model_width = memory.shape
    row_count = inputs.shape[0]
    pairs = model_width // PAIR
    paired = plan.wide == pairs
    place = plan.places() if paired else lax.iota(jnp.int32, pairs)

    def context_back(rows, weights):
        if paired:
            here = lax.iota(jnp.int32, plan.wide)
            return back_natural([rows], weights, [3], here, row_count, BF)
        return plan.natural(backward(rows, (weights[0][3], weights[1][3]))).astype(BF)

    def to_relative(context):
        half = model_width // 2
        return (context[:, :half], context[:, half:]) if paired else plan.relative(context)

    def back(lefts, weights, picks, rows, dtype=F32):
        if (model_width // plan.wide) % 128 == 0:
            return back_natural(lefts, weights, picks, plan.blocks(), rows, dtype)
        total = 0.0
        for i, left in enumerate(lefts):
            near, far = weights if picks is None else (weights[0][picks[i]], weights[1][picks[i]])
            total = total + backward(left, (near, far))
        return plan.natural(total).astype(dtype)

    def forward(rows, weight):
        return project(rows[0], weight[0]) + project(rows[1], weight[1])

    def backward(rows, weight):
        return jnp.concatenate(
            [project_back(rows, weight[0]), project_back(rows, weight[1])], axis=1
        )

    inputs_f = inputs.astype(F32)

    share, hidden_share = self_gain.shape[0], ffn_bias_in.shape[0]
    small_rows = jnp.concatenate(
        [self_bias, self_gain[None], cross_bias, cross_gain[None], ffn_bias_out, ffn_gain[None]],
        axis=0,
    )
    vector_count = small_rows.shape[0]
    small = Stream(
        plan.gather_small(
            pad_lanes(jnp.concatenate([small_rows.reshape(1, -1), ffn_bias_in[None]], axis=1))[0]
        )
    )

    def four(have):
        return have[:2], have[2:]

    def each(a, b):
        return jnp.concatenate([a, b], axis=0)

    def columns(have):
        half = have.shape[-1] // 2
        return have[..., :half], have[..., half:]

    def one(a, b):
        return jnp.concatenate([a[0], b[0]], axis=1)

    selfs = Stream(
        plan.gather(jnp.concatenate([self_qkv, self_out[None]], axis=0), four, each)
    )
    crosses = Stream(
        plan.gather(jnp.concatenate([cross_qkv, cross_out[None]], axis=0), four, each)
    )
    fins = Stream(plan.gather(ffn_in[None], columns, one))
    fouts = Stream(plan.gather(ffn_out[None], columns, one))
    after = plan.step(small)
    for _ in plan.zs:
        after = (plan.step(selfs, after), plan.step(small))
    after = (after, plan.step(small))
    for _ in plan.across[2:]:
        after = plan.step(selfs, after)
    last = plan.step(selfs, after)
    plan.finish(small)
    cross_z = plan.step(crosses, after)
    last = plan.step(selfs, (last, cross_z, small.result))
    for _ in plan.zs[1:]:
        cross_z = plan.step(crosses, cross_z)
    self_core = plan.step(selfs, cross_z)
    last = plan.step(crosses, last)
    fin_z = plan.step(fins, cross_z)
    table = small.result.astype(F32)
    vectors = table[:, : vector_count * share].reshape(plan.count, vector_count, share)
    vectors = jnp.swapaxes(vectors, 0, 1).reshape(vector_count, model_width)
    sbias, sgain, cbias, cgain, fbout, fgain = (
        vectors[:4],
        vectors[4],
        vectors[5:9],
        vectors[9],
        vectors[10:12],
        vectors[12],
    )
    fbin = table[:, vector_count * share :][:, :hidden_share].reshape(-1)

    x_rel = plan.relative(inputs)
    no_bias = jnp.zeros((model_width,), F32)
    qkv = stack_project(
        x_rel,
        selfs.result,
        0,
        jnp.stack([sbias[0], no_bias, sbias[1]])[:, None],
        (scaling, 1.0, 1.0),
        BF,
    )
    self_ctx, self_lse = self_attend(qkv, item_count, place)
    self_rel = to_relative(self_ctx)
    first_pre = inputs_f + stack_project(self_rel, selfs.result, 3, sbias[None, 2:3], (1.0,), F32)[0]
    first = layer_norm(first_pre, sgain, sbias[3])
    first_rel = plan.relative(first.astype(BF))
    last = plan.across_steps(crosses, (last, self_core, fin_z), first_rel)
    for _ in plan.zs[1:]:
        fin_z = plan.step(fins, fin_z)
    fout_z = plan.step(fouts, fin_z)
    cross_core = plan.step(crosses)
    last = plan.step(fins, (last, fout_z))
    for _ in plan.zs[1:]:
        fout_z = plan.step(fouts, fout_z)
    queries_two = stack_project(first_rel, crosses.result, 0, cbias[None, 0:1], (scaling,), BF)[0]
    mem_rel = plan.relative(memory.reshape(item_count * mem_slots, model_width))
    mem_keys, mem_values = memory_project(mem_rel, crosses.result, 1, 2, cbias[1:2], 512)
    last = plan.across_steps(
        fins, (last, cross_core, fout_z), (queries_two, mem_keys, mem_values)
    )
    fin_core = plan.step(fins)
    cross_out = ()
    for item in range(item_count):
        cross_out = cross_attend(
            queries_two, mem_keys, mem_values, mem_lengths, place, item, cross_out
        )
        if item == 0:
            last = plan.step(fouts, last, cross_out)
    cross_ctx, cross_lse = cross_out
    fin = fins.result
    cross_rel = to_relative(cross_ctx)
    second_pre = first + stack_project(cross_rel, crosses.result, 3, cbias[None, 2:3], (1.0,), F32)[0]
    second = layer_norm(second_pre, cgain, cbias[3])
    second_rel = plan.relative(second.astype(BF))
    plan.across_steps(fouts, (last, fin_core), second_rel)

    pre_gelu = forward(second_rel, fin) + fbin
    hidden, gelu_pull = jax.vjp(gelu_exact, pre_gelu)
    hidden_rel = plan.relative(hidden.astype(BF))
    plan.step(fouts, None, hidden_rel)
    fout = fouts.result
    third_pre = second + (forward(hidden_rel, fout) + fbout[0])
    layer_out, norm_pull = jax.vjp(layer_norm, third_pre, fgain, fbout[1])

    d_third, g_fgain, g_fshift = norm_pull(out_grad.astype(F32))
    e_three = d_third.astype(BF)
    half = model_width // 2
    to_fout = Stream(
        plan.scatter([hidden_rel], [e_three], [(0, 0, 0, half), (0, 0, half, half)])
    )
    d_pre = gelu_pull(plan.natural(backward(e_three, fout)))[0].astype(BF)
    plan.step(to_fout, None, d_pre)
    half = d_pre.shape[1] // 2
    to_fin = Stream(plan.scatter([second_rel], [d_pre], [(0, 0, 0, half), (0, 0, half, half)]))
    g_fbin = column_sums(d_pre)
    d_second = d_third + back([d_pre], fin, None, row_count)

    _, norm_pull_two = jax.vjp(layer_norm, second_pre, cgain, cbias[3])
    d_second_pre, g_cgain, g_cshift = norm_pull_two(d_second)
    e_two = d_second_pre.astype(BF)
    last = plan.step(to_fout, None, (e_two, [v for v, _ in to_fin.sends]))
    plan.step(to_fin)
    d_cross_ctx = context_back(e_two, crosses.result)
    cross_back = ()
    for item in range(item_count):
        cross_back = cross_attend_back(
            queries_two, mem_keys, mem_values, cross_lse, d_cross_ctx, mem_lengths, place,
            item, cross_back,
        )
        if item == 0:
            last = plan.across_steps(to_fout, last, cross_back)
    dq_scaled, dk_flat, dv_flat = cross_back
    to_cross = Stream(
        plan.scatter(
            [first_rel, mem_rel, cross_rel],
            [dq_scaled, dk_flat, dv_flat, e_two],
            [(0, 0, 0, model_width), (1, 1, 0, model_width), (1, 2, 0, model_width), (2, 3, 0, model_width)],
        )
    )
    last = plan.step(to_fin, last, [v for v, _ in to_cross.sends])
    plan.step(to_cross)
    for _ in plan.zs:
        fout_last = plan.step(to_fout)
    d_first = d_second_pre + back([dq_scaled], crosses.result, [0], row_count)

    _, norm_pull_one = jax.vjp(layer_norm, first_pre, sgain, sbias[3])
    d_first_pre, g_sgain, g_sshift = norm_pull_one(d_first)
    e_one = d_first_pre.astype(BF)
    d_self_ctx = context_back(e_one, selfs.result)
    last = plan.across_steps(to_fin, (last, fout_last), d_self_ctx)
    dq_self, dk_self, dv_self = self_attend_back(qkv, self_lse, d_self_ctx, item_count, place)
    to_self = Stream(
        plan.scatter(
            [x_rel, self_rel],
            [dq_self, dk_self, dv_self, e_one],
            [(0, 0, 0, model_width), (0, 1, 0, model_width), (0, 2, 0, model_width), (1, 3, 0, model_width)],
        )
    )
    last = plan.step(to_cross, last, [v for v, _ in to_self.sends])
    plan.step(to_self)
    for _ in plan.zs:
        fin_last = plan.step(to_fin)
    input_grad = d_first_pre + back(
        [dq_self, dk_self, dv_self], selfs.result, [0, 1, 2], row_count
    )
    last = plan.across_steps(to_cross, (last, fin_last), input_grad)
    memory_grad = back([dk_flat, dv_flat], crosses.result, [1, 2], 512).reshape(memory.shape)
    last = plan.step(to_self, last, memory_grad)
    for _ in plan.zs:
        cross_last = plan.step(to_cross)
    plan.across_steps(to_self, (last, cross_last))
    plan.finish(to_self)
    grads = jnp.stack(
        [
            column_sums(dq_self),
            column_sums(dv_self),
            column_sums(e_one),
            g_sshift,
            g_sgain,
            column_sums(dq_scaled),
            column_sums(dv_flat),
            column_sums(e_two),
            g_cshift,
            g_cgain,
            column_sums(e_three),
            g_fshift,
            g_fgain,
        ]
    )
    grads = jnp.swapaxes(grads.reshape(vector_count, plan.count, share), 0, 1)
    to_small = Stream(
        plan.scatter_small(
            pad_lanes(
                jnp.concatenate(
                    [grads.reshape(plan.count, -1), g_fbin.reshape(plan.count, -1)], axis=1
                )
            )
        )
    )
    plan.finish(to_small)
    small_sums = to_small.result
    found = small_sums[: vector_count * share].reshape(vector_count, share)
    g_hidden = small_sums[vector_count * share :][:hidden_share]
    g_self, g_cross = to_self.result, to_cross.result
    g_fout = jnp.concatenate([to_fout.result[0], to_fout.result[1]], axis=1)
    g_fin = jnp.concatenate([to_fin.result[0], to_fin.result[1]], axis=1)
    return (
        layer_out.astype(BF),
        input_grad,
        memory_grad,
        g_self[:3],
        g_self[3],
        found[:4],
        found[4],
        g_cross[:3],
        g_cross[3],
        found[5:9],
        found[9],
        g_fin,
        g_fout,
        g_hidden,
        found[10:12],
        found[12],
    )


def solution(mesh):
    both = ("wide", "narrow")
    placed = (
        P(both, None),
        P(both, None, None),
        P(both),
        P(None, both, None),
        P(both, None),
        P(None, both),
        P(both),
        P(None, both, None),
        P(both, None),
        P(None, both),
        P(both),
        P(both, None),
        P(both, None),
        P(both),
        P(None, both),
        P(both),
        P(both, None),
    )
    return jax.shard_map(
        local,
        mesh=mesh,
        in_specs=placed,
        out_specs=(
            P(both, None),
            P(both, None),
            P(both, None, None),
            P(None, both, None),
            P(both, None),
            P(None, both),
            P(both),
            P(None, both, None),
            P(both, None),
            P(None, both),
            P(both),
            P(both, None),
            P(both, None),
            P(both),
            P(None, both),
            P(both),
        ),
        check_vma=False,
    )
```

time: 760 us -> 651 us (0.86)
  Pallas kernels: 89 us -> 208 us
  waiting for transfers between devices: 319 us -> 211 us
  matrix products: 90.7 us -> 28.3 us
  local copies, waits for them, and re-layouts: 99.5 us -> 46.9 us
  starting transfers between devices: 106 us -> 72.3 us
  other arithmetic: 40.2 us -> 73.8 us
    pallas_call x2 -> x21, Pallas kernels: 41.9 us -> 152 us  [the longest x4 50.1 us: cross_call(): pl.pallas_call(kernel, grid_spec=pltpu.PrefetchScalarGridSpec(num_scalar_...]
    ppermute x110 -> x66, waiting for transfers between devices: 319 us -> 211 us  [step(): lax.ppermute(v, AXES, [(i, i ^ m) for i in range(self.count)])]
    unnamed x327 -> x119, local copies, waits for them, and re-layouts: 64.3 us -> 14.9 us
    dot_general x20 -> x0, matrix products: 42.7 us -> none  [weight_grad(): lax.dot_general(left_rows, gradient, (((0,), (0,)), ((), ())), preferred_...]
    ppermute x110 -> x66, starting transfers between devices: 106 us -> 72.3 us  [step(): lax.ppermute(v, AXES, [(i, i ^ m) for i in range(self.count)])]
    dot_general x10 -> x4, matrix products: 40.9 us -> 22 us  [project(): return jnp.dot(left_rows, weight, preferred_element_type=F32)]
    concatenate x0 -> x18, other arithmetic: none -> 16.6 us  [the longest x5 5.71 us: relative(): jnp.concatenate(pieces[:half], axis=1)]
    slice x25 -> x19, local copies, waits for them, and re-layouts: 2.01 us -> 12.4 us  [the longest x2 3.76 us: to_relative(): context[:, half:]]
  transfers between devices with their start and end apart: 110 -> 66, of which waited for: 46 -> 32; matrix products, arithmetic and copies ran while one was open for 24% -> 15% of each run, Pallas kernels for 5% -> 29%
where the time goes in v3:
time: 651 us; the launch traced here: 643 us
  waiting for transfers between devices  211 us (32%)
  Pallas kernels  208 us (32%)
  other arithmetic  73.8 us (11%)
  starting transfers between devices  72.3 us (11%)
  local copies, waits for them, and re-layouts  46.9 us (7%)
  matrix products  28.3 us (4%)
    ppermute x66, waiting for transfers between devices, step(): lax.ppermute(v, AXES, [(i, i ^ m) for i in range(self.count)])  211 us
    ppermute x66, starting transfers between devices, step(): lax.ppermute(v, AXES, [(i, i ^ m) for i in range(self.count)])  72.3 us
    pallas_call x4, Pallas kernels, cross_call(): pl.pallas_call(kernel, grid_spec=pltpu.PrefetchScalarGridSpec(num_scalar_...  50.1 us
    pallas_call x6, Pallas kernels, back_natural(): pl.pallas_call(back_kernel, grid_spec=pltpu.PrefetchScalarGridSpec(num_sc...  42.5 us
    pallas_call x4, Pallas kernels, stack_grads(): pl.pallas_call(functools.partial(grads_kernel, table), grid=(len(products...  37 us
    pallas_call x8, Pallas kernels, add_split(): pl.pallas_call(add_split_kernel, grid=shapes[0].shape[:2], in_specs=in_sp...  36.3 us
    dot_general x4, matrix products, project(): return jnp.dot(left_rows, weight, preferred_element_type=F32)  22 us
    pallas_call x4, Pallas kernels, stack_project(): pl.pallas_call(functools.partial(project_kernel, scales), grid=(count,),...  16.2 us
  transfers between devices with their start and end apart: 66, of which 32 were waited for; matrix products, arithmetic and copies ran while one was open for 15% of the time, Pallas kernels for 29%

profile of v3, /device:TPU:0, one launch (start us, length us, event | category | flops | bytes accessed | tf_op | source)
XLA Modules:
  0.0 642.7 jit_solution(12651675547398789370)
XLA Ops:
  11.5 10.9 %collective-permute-done.1 = bf16[4,1,32,1024]{3,2,0,1:T(8,128)(2,1)S(1)} collective-permute-done((bf16[4,1,32,1024]{3,2,0,1:T(8,128)(2,1)S(1)}, bf16[4,1,32,1024]{3,2,0,1:T(8,128)(2,1)S(1)}, u32[]{:S(2)}, u32[]{:S(2)}) %collective-permute-start.1) | collective-permute-done | bytes 262176 | tf_op jit(solution)/shard_map/ppermute | solution.py:418
  27.1 9.2 %collective-permute-done.3 = bf16[4,2,32,1024]{3,2,1,0:T(8,128)(2,1)S(1)} collective-permute-done((bf16[4,2,32,1024]{3,2,1,0:T(8,128)(2,1)S(1)}, bf16[4,2,32,1024]{3,2,1,0:T(8,128)(2,1)S(1)}, u32[]{:S(2)}, u32[]{:S(2)}) %collective-permute-start.3) | collective-permute-done | bytes 524320 | tf_op jit(solution)/shard_map/ppermute | solution.py:418
  56.1 22.3 %collective-permute-done.10 = bf16[2,2,128,1024]{3,2,1,0:T(8,128)(2,1)S(1)} collective-permute-done((bf16[2,2,128,1024]{3,2,1,0:T(8,128)(2,1)S(1)}, bf16[2,2,128,1024]{3,2,1,0:T(8,128)(2,1)S(1)}, u32[]{:S(2)}, u32[]{:S(2)}) %collective-permute-start.10) | collective-permute-done | bytes 1048608 | tf_op jit(solution)/shard_map/ppermute | solution.py:418
  92.5 7.5 %collective-permute-done.15 = bf16[2,128,1024]{2,1,0:T(8,128)(2,1)S(1)} collective-permute-done((bf16[2,128,1024]{2,1,0:T(8,128)(2,1)S(1)}, bf16[2,128,1024]{2,1,0:T(8,128)(2,1)S(1)}, u32[]{:S(2)}, u32[]{:S(2)}) %collective-permute-start.15) | collective-permute-done | bytes 524320 | tf_op jit(solution)/shard_map/ppermute | solution.py:418
  135.8 12.4 %collective-permute-done.20 = bf16[1,2,32,4096]{3,2,1,0:T(8,128)(2,1)S(1)} collective-permute-done((bf16[1,2,32,4096]{3,2,1,0:T(8,128)(2,1)S(1)}, bf16[1,2,32,4096]{3,2,1,0:T(8,128)(2,1)S(1)}, u32[]{:S(2)}, u32[]{:S(2)}) %collective-permute-start.20) | collective-permute-done | bytes 524320 | tf_op jit(solution)/shard_map/ppermute | solution.py:418
  151.7 11.1 %collective-permute-done.21 = bf16[1,1,128,1024]{3,2,1,0:T(8,128)(2,1)S(1)} collective-permute-done((bf16[1,1,128,1024]{3,2,1,0:T(8,128)(2,1)S(1)}, bf16[1,1,128,1024]{3,2,1,0:T(8,128)(2,1)S(1)}, u32[]{:S(2)}, u32[]{:S(2)}) %collective-permute-start.21) | collective-permute-done | bytes 262176 | tf_op jit(solution)/shard_map/ppermute | solution.py:418
  165.2 10.6 %collective-permute-done.23 = bf16[1,128,2048]{2,1,0:T(8,128)(2,1)S(1)} collective-permute-done((bf16[1,128,2048]{2,1,0:T(8,128)(2,1)S(1)}, bf16[1,128,2048]{2,1,0:T(8,128)(2,1)S(1)}, u32[]{:S(2)}, u32[]{:S(2)}) %collective-permute-start.23) | collective-permute-done | bytes 524320 | tf_op jit(solution)/shard_map/ppermute | solution.py:418
  192.1 12.9 %memory_project.1 = (bf16[2048,1024]{1,0:T(8,128)(2,1)}, bf16[2048,1024]{1,0:T(8,128)(2,1)}) custom-call(bf16[2048,512]{1,0:T(8,128)(2,1)} %get-tuple-element.415.x0.refs_2_, bf16[2048,512]{1,0:T(8,128)(2,1)} %get-tuple-element.416.x1.refs_3_, bf16[4,512,1024]{2,1,0:T(8,128)(2,1)} %copy-done, bf16[4,512,1024]{2,1,0:T(8,128)(2,1)} %copy-done.1, ...), custom_call_target="tpu_custom_call" | custom-call | tf_op jit(solution)/shard_map/memory_project/pallas_call | solution.py:340
  220.5 11.9 %cross_attend.4 = (bf16[256,1024]{1,0:T(8,128)(2,1)}, f32[2,8,1,256]{3,2,1,0:T(1,128)}) custom-call(s32[8]{0:T(128)} %fusion.51.place, s32[1]{0:T(128)} %get-tuple-element.408.length, bf16[256,1024]{1,0:T(8,128)(2,1)} %bitcast.265, bf16[2048,1024]{1,0:T(8,128)(2,1)} %get-tuple-element.153.k, bf16[2048,1024]{1,0:T(8,128)(2,1)} %get-tuple-element.154.v), custom_call_target="tpu_custom_call" | custom-call | tf_op jit(solution)/shard_map/cross_attend/pallas_call | solution.py:118
  232.4 12.4 %cross_attend.5 = (bf16[256,1024]{1,0:T(8,128)(2,1)}, f32[2,8,1,256]{3,2,1,0:T(1,128)}) custom-call(s32[8]{0:T(128)} %fusion.51.place, s32[1]{0:T(128)} %get-tuple-element.409.length, bf16[256,1024]{1,0:T(8,128)(2,1)} %bitcast.266, bf16[2048,1024]{1,0:T(8,128)(2,1)} %get-tuple-element.153.k, ...), custom_call_target="tpu_custom_call", output_to_operand_aliasing={{0}: (5, {}), {1}: (6, {})} | custom-call | tf_op jit(solution)/shard_map/cross_attend/pallas_call | solution.py:118
  256.0 20.8 %collective-permute-done.30 = bf16[2,1,512,512]{3,2,1,0:T(8,128)(2,1)S(1)} collective-permute-done((bf16[2,1,512,512]{3,2,1,0:T(8,128)(2,1)S(1)}, bf16[2,1,512,512]{3,2,1,0:T(8,128)(2,1)S(1)}, u32[]{:S(2)}, u32[]{:S(2)}) %collective-permute-start.30) | collective-permute-done | bytes 1048608 | tf_op jit(solution)/shard_map/ppermute | solution.py:418
  285.6 13.6 %multiply_convert_fusion = (bf16[256,4096]{1,0:T(8,128)(2,1)S(1)}, f32[256,4096]{1,0:T(8,128)}, f32[256,4096]{1,0:T(8,128)}) fusion(f32[4096]{0:T(1024)S(1)} %slice_bitcast_fusion.6, f32[256,4096]{1,0:T(8,128)S(1)} %fusion.53, bf16[512,4096]{1,0:T(8,128)(2,1)} %collective-permute-done.27, bf16[256,128]{1,0:T(8,128)(2,1)S(1)} %get-tuple-element.360, ...), kind=kOutput, calls=%fused_computation.27 | convolution fusion | flops 1145044992 | bytes 19152896 | tf_op jit(solution)/shard_map/dot_general | solution.py:19
  338.9 8.2 %back_natural.6 = f32[256,1024]{1,0:T(8,128)} custom-call(s32[8]{0:T(128)} %broadcast_xor_fusion.blocks, bf16[256,4096]{1,0:T(8,128)(2,1)} %get-tuple-element.285.refs_0_.refs_2_, bf16[1,512,4096]{2,1,0:T(8,128)(2,1)} %get-tuple-element.300.refs_1_, bf16[1,512,4096]{2,1,0:T(8,128)(2,1)} %bitcast.93.refs_2_), custom_call_target="tpu_custom_call" | custom-call | tf_op jit(solution)/shard_map/back_natural/pallas_call | solution.py:316
  356.5 21.4 %collective-permute-done.37.refs_1_.refs_3_ = bf16[1,2,512,512]{3,2,1,0:T(8,128)(2,1)} collective-permute-done((bf16[1,2,512,512]{3,2,1,0:T(8,128)(2,1)}, bf16[1,2,512,512]{3,2,1,0:T(8,128)(2,1)}, u32[]{:S(2)}, u32[]{:S(2)}) %collective-permute-start.37) | collective-permute-done | bytes 1048608 | tf_op jit(solution)/shard_map/ppermute | solution.py:418
  388.7 12.7 %cross_attend.6 = (bf16[256,1024]{1,0:T(8,128)(2,1)}, bf16[2048,1024]{1,0:T(8,128)(2,1)}, bf16[2048,1024]{1,0:T(8,128)(2,1)}) custom-call(s32[8]{0:T(128)} %fusion.51.place, s32[1]{0:T(128)} %get-tuple-element.408.length, bf16[256,1024]{1,0:T(8,128)(2,1)} %bitcast.267, bf16[2048,1024]{1,0:T(8,128)(2,1)} %get-tuple-element.153.k, ...), custom_call_target="tpu_custom_call" | custom-call | tf_op jit(solution)/shard_map/cross_attend/pallas_call | solution.py:118
  407.5 13.1 %cross_attend.7 = (bf16[256,1024]{1,0:T(8,128)(2,1)}, bf16[2048,1024]{1,0:T(8,128)(2,1)}, bf16[2048,1024]{1,0:T(8,128)(2,1)}) custom-call(s32[8]{0:T(128)} %fusion.51.place, s32[1]{0:T(128)} %get-tuple-element.409.length, bf16[256,1024]{1,0:T(8,128)(2,1)} %bitcast.268, ...), custom_call_target="tpu_custom_call", output_to_operand_aliasing={{0}: (7, {}), {1}: (8, {}), {2}: (9, {})} | custom-call | tf_op jit(solution)/shard_map/cross_attend/pallas_call | solution.py:118
  435.0 17.3 %stack_grads.5 = (bf16[4,512,1024]{2,1,0:T(8,128)(2,1)}, bf16[4,512,1024]{2,1,0:T(8,128)(2,1)}) custom-call(bf16[256,512]{1,0:T(8,128)(2,1)} %pad_maximum_fusion.31.x0.refs_0_, bf16[256,512]{1,0:T(8,128)(2,1)} %pad_maximum_fusion.32.x1.refs_1_, bf16[2048,512]{1,0:T(8,128)(2,1)} %get-tuple-element.415.x0.refs_2_, ...), custom_call_target="tpu_custom_call" | custom-call | tf_op jit(solution)/shard_map/stack_grads/pallas_call | solution.py:279
  465.2 7.2 %collective-permute-done.44 = bf16[2,128,512]{2,1,0:T(8,128)(2,1)S(1)} collective-permute-done((bf16[2,128,512]{2,1,0:T(8,128)(2,1)S(1)}, bf16[2,128,512]{2,1,0:T(8,128)(2,1)S(1)}, u32[]{:S(2)}, u32[]{:S(2)}) %collective-permute-start.44) | collective-permute-done | bytes 262176 | tf_op jit(solution)/shard_map/ppermute | solution.py:418
  479.7 7.9 %self_attend_back.1 = (bf16[256,1024]{1,0:T(8,128)(2,1)}, bf16[256,1024]{1,0:T(8,128)(2,1)}, bf16[256,1024]{1,0:T(8,128)(2,1)}) custom-call(s32[8]{0:T(128)} %fusion.51.place, bf16[3,256,1024]{2,1,0:T(8,128)(2,1)} %stack_project.4.q.k.v, bf16[3,256,1024]{2,1,0:T(8,128)(2,1)} %stack_project.4.q.k.v, bf16[3,256,1024]{2,1,0:T(8,128)(2,1)} %stack_project.4.q.k.v, ...), custom_call_target="tpu_custom_call" | custom-call | tf_op jit(solution)/shard_map/self_attend_back/pallas_call | solution.py:218
  523.2 18.0 %collective-permute-done.47.refs_1_.refs_3_ = bf16[2,2,128,1024]{3,2,1,0:T(8,128)(2,1)S(1)} collective-permute-done((bf16[2,2,128,1024]{3,2,1,0:T(8,128)(2,1)}, bf16[2,2,128,1024]{3,2,1,0:T(8,128)(2,1)S(1)}, u32[]{:S(2)}, u32[]{:S(2)}) %collective-permute-start.47) | collective-permute-done | bytes 1048608 | tf_op jit(solution)/shard_map/ppermute | solution.py:418
  550.2 15.4 %back_natural.11 = f32[2048,1024]{1,0:T(8,128)} custom-call(s32[8]{0:T(128)} %broadcast_xor_fusion.blocks, bf16[2048,1024]{1,0:T(8,128)(2,1)} %get-tuple-element.185.refs_0_.refs_7_, bf16[2048,1024]{1,0:T(8,128)(2,1)} %get-tuple-element.186.refs_1_.refs_8_, bf16[4,512,1024]{2,1,0:T(8,128)(2,1)} %copy-done, bf16[4,512,1024]{2,1,0:T(8,128)(2,1)} %copy-done.1, ...), custom_call_target="tpu_custom_call" | custom-call | tf_op jit(solution)/shard_map/back_natural/pallas_call | solution.py:316
  585.7 15.5 %collective-permute-done.53.refs_1_.refs_3_ = bf16[2,2,128,1024]{3,2,1,0:T(8,128)(2,1)S(1)} collective-permute-done((bf16[2,2,128,1024]{3,2,1,0:T(8,128)(2,1)}, bf16[2,2,128,1024]{3,2,1,0:T(8,128)(2,1)S(1)}, u32[]{:S(2)}, u32[]{:S(2)}) %collective-permute-start.53) | collective-permute-done | bytes 1048608 | tf_op jit(solution)/shard_map/ppermute | solution.py:418
  609.4 7.9 %collective-permute-done.57 = bf16[2,1,128,1024]{3,2,1,0:T(8,128)(2,1)S(1)} collective-permute-done((bf16[2,1,128,1024]{3,2,1,0:T(8,128)(2,1)}, bf16[2,1,128,1024]{3,2,1,0:T(8,128)(2,1)S(1)}, u32[]{:S(2)}, u32[]{:S(2)}) %collective-permute-start.57) | collective-permute-done | bytes 524320 | tf_op jit(solution)/shard_map/ppermute | solution.py:418
  621.7 8.9 %collective-permute-done.59 = bf16[4,2,32,1024]{3,2,0,1:T(8,128)(2,1)S(1)} collective-permute-done((bf16[4,2,32,1024]{3,2,0,1:T(8,128)(2,1)S(1)}, bf16[4,2,32,1024]{3,2,0,1:T(8,128)(2,1)S(1)}, u32[]{:S(2)}, u32[]{:S(2)}) %collective-permute-start.59) | collective-permute-done | bytes 524320 | tf_op jit(solution)/shard_map/ppermute | solution.py:418
  (475 shorter events, 331.3 us)
Async XLA Ops:
  55.3 26.2 %collective-permute-start.12 = (bf16[4,2,32,1024]{3,2,1,0:T(8,128)(2,1)S(1)}, bf16[4,2,32,1024]{3,2,1,0:T(8,128)(2,1)S(1)}, u32[]{:S(2)}, u32[]{:S(2)}) collective-permute-start(bf16[4,2,32,1024]{3,2,1,0:T(8,128)(2,1)S(1)} %maximum_bitcast_fusion.6), channel_id=1, source_target_pairs={{0,1},{1,0},{2,3},{3,2},{4,5},{5,4},{6,7},{7,6},{8,9},{9,8},{10,11... | collective-permute-start | bytes 1572872 | tf_op jit(solution)/shard_map/ppermute | solution.py:418
  81.5 24.5 %collective-permute-start.13 = (bf16[4,512,1024]{2,1,0:T(8,128)(2,1)}, bf16[4,512,1024]{2,1,0:T(8,128)(2,1)}, u32[]{:S(2)}, u32[]{:S(2)}) collective-permute-start(bf16[4,512,1024]{2,1,0:T(8,128)(2,1)} %pad_maximum_fusion.near.refs_1_.refs_3_.refs_5_.refs_7_), channel_id=1, source_target_pairs={{0,4},{1,5},{2,6},{3,7},{4,0},{5,1},{6,2},{7,3},{8,12},{9,13},{10,... | collective-permute-start | bytes 12582920 | tf_op jit(solution)/shard_map/ppermute | solution.py:418
  133.6 44.5 %collective-permute-start.19 = (bf16[4,512,1024]{2,1,0:T(8,128)(2,1)S(1)}, bf16[4,512,1024]{2,1,0:T(8,128)(2,1)S(1)}, u32[]{:S(2)}, u32[]{:S(2)}) collective-permute-start(bf16[4,512,1024]{2,1,0:T(8,128)(2,1)S(1)} %pad_maximum_fusion.1.near.k0.v0.refs_1_.refs_2_.refs_4_), channel_id=1, source_target_pairs={{0,4},{1,5},{2,6},{3,7},{4,0},{5,1},{6,2},{7,3},{8,12},{9,13},{10,... | collective-permute-start | bytes 12582920 | tf_op jit(solution)/shard_map/ppermute | solution.py:418
  180.2 24.8 %collective-permute-start.25 = (bf16[2,1,128,2048]{3,2,1,0:T(8,128)(2,1)}, bf16[2,1,128,2048]{3,2,1,0:T(8,128)(2,1)}, u32[]{:S(2)}, u32[]{:S(2)}) collective-permute-start(bf16[2,1,128,2048]{3,2,1,0:T(8,128)(2,1)} %get-tuple-element.163), channel_id=1, source_target_pairs={{0,16},{1,17},{2,18},{3,19},{4,20},{5,21},{6,22},{7,23},{8,24},{9,... | collective-permute-start | bytes 3145736 | tf_op jit(solution)/shard_map/ppermute | solution.py:418
  212.8 38.9 %collective-permute-start.27 = (bf16[512,4096]{1,0:T(8,128)(2,1)}, bf16[512,4096]{1,0:T(8,128)(2,1)}, u32[]{:S(2)}, u32[]{:S(2)}) collective-permute-start(bf16[512,4096]{1,0:T(8,128)(2,1)} %get-tuple-element.301), channel_id=1, source_target_pairs={{0,4},{1,5},{2,6},{3,7},{4,0},{5,1},{6,2},{7,3},{8,12},{9,13},{10,... | collective-permute-start | bytes 12582920 | tf_op jit(solution)/shard_map/ppermute | solution.py:418
  251.7 25.1 %collective-permute-start.30 = (bf16[2,1,512,512]{3,2,1,0:T(8,128)(2,1)S(1)}, bf16[2,1,512,512]{3,2,1,0:T(8,128)(2,1)S(1)}, u32[]{:S(2)}, u32[]{:S(2)}) collective-permute-start(bf16[2,1,512,512]{3,2,1,0:T(8,128)(2,1)S(1)} %get-tuple-element.171), channel_id=1, source_target_pairs={{0,16},{1,17},{2,18},{3,19},{4,20},{5,21},{6,22},{7,23},{8,24},{9,... | collective-permute-start | bytes 3145736 | tf_op jit(solution)/shard_map/ppermute | solution.py:418
  253.5 24.7 %collective-permute-start.31 = (bf16[2,1,512,512]{3,2,1,0:T(8,128)(2,1)S(1)}, bf16[2,1,512,512]{3,2,1,0:T(8,128)(2,1)S(1)}, u32[]{:S(2)}, u32[]{:S(2)}) collective-permute-start(bf16[2,1,512,512]{3,2,1,0:T(8,128)(2,1)S(1)} %get-tuple-element.172), channel_id=1, source_target_pairs={{0,8},{1,9},{2,10},{3,11},{4,12},{5,13},{6,14},{7,15},{8,0},{9,1},... | collective-permute-start | bytes 3145736 | tf_op jit(solution)/shard_map/ppermute | solution.py:418
  322.6 24.4 %collective-permute-start.36 = (bf16[2,2048,512]{2,1,0:T(8,128)(2,1)}, bf16[2,2048,512]{2,1,0:T(8,128)(2,1)}, u32[]{:S(2)}, u32[]{:S(2)}) collective-permute-start(bf16[2,2048,512]{2,1,0:T(8,128)(2,1)} %get-tuple-element.203), channel_id=1, source_target_pairs={{0,4},{1,5},{2,6},{3,7},{4,0},{5,1},{6,2},{7,3},{8,12},{9,13},{10,... | collective-permute-start | bytes 12582920 | tf_op jit(solution)/shard_map/ppermute | solution.py:418
  338.1 63.3 %collective-permute-start.35 = (bf16[2,512,2048]{2,1,0:T(8,128)(2,1)}, bf16[2,512,2048]{2,1,0:T(8,128)(2,1)}, u32[]{:S(2)}, u32[]{:S(2)}) collective-permute-start(bf16[2,512,2048]{2,1,0:T(8,128)(2,1)} %get-tuple-element.198), channel_id=1, source_target_pairs={{0,4},{1,5},{2,6},{3,7},{4,0},{5,1},{6,2},{7,3},{8,12},{9,13},{10,... | collective-permute-start | bytes 12582920 | tf_op jit(solution)/shard_map/ppermute | solution.py:418
  352.3 25.7 %collective-permute-start.37 = (bf16[1,2,512,512]{3,2,1,0:T(8,128)(2,1)}, bf16[1,2,512,512]{3,2,1,0:T(8,128)(2,1)}, u32[]{:S(2)}, u32[]{:S(2)}) collective-permute-start(bf16[1,2,512,512]{3,2,1,0:T(8,128)(2,1)} %get-tuple-element.206), channel_id=1, source_target_pairs={{0,16},{1,17},{2,18},{3,19},{4,20},{5,21},{6,22},{7,23},{8,24},{9,... | collective-permute-start | bytes 3145736 | tf_op jit(solution)/shard_map/ppermute | solution.py:418
  352.7 25.3 %collective-permute-start.38 = (bf16[1,2,512,512]{3,2,1,0:T(8,128)(2,1)}, bf16[1,2,512,512]{3,2,1,0:T(8,128)(2,1)}, u32[]{:S(2)}, u32[]{:S(2)}) collective-permute-start(bf16[1,2,512,512]{3,2,1,0:T(8,128)(2,1)} %get-tuple-element.207), channel_id=1, source_target_pairs={{0,8},{1,9},{2,10},{3,11},{4,12},{5,13},{6,14},{7,15},{8,0},{9,1},... | collective-permute-start | bytes 3145736 | tf_op jit(solution)/shard_map/ppermute | solution.py:418
  381.7 24.9 %collective-permute-start.39 = (bf16[1,1,512,512]{3,2,1,0:T(8,128)(2,1)}, bf16[1,1,512,512]{3,2,1,0:T(8,128)(2,1)S(1)}, u32[]{:S(2)}, u32[]{:S(2)}) collective-permute-start(bf16[1,1,512,512]{3,2,1,0:T(8,128)(2,1)} %get-tuple-element.213), channel_id=1, source_target_pairs={{0,8},{1,9},{2,10},{3,11},{4,12},{5,13},{6,14},{7,15},{8,0},{9,1},... | collective-permute-start | bytes 1572872 | tf_op jit(solution)/shard_map/ppermute | solution.py:418
  382.3 24.3 %collective-permute-start.40 = (bf16[1,1,512,512]{3,2,1,0:T(8,128)(2,1)}, bf16[1,1,512,512]{3,2,1,0:T(8,128)(2,1)S(1)}, u32[]{:S(2)}, u32[]{:S(2)}) collective-permute-start(bf16[1,1,512,512]{3,2,1,0:T(8,128)(2,1)} %get-tuple-element.214), channel_id=1, source_target_pairs={{0,16},{1,17},{2,18},{3,19},{4,20},{5,21},{6,22},{7,23},{8,24},{9,... | collective-permute-start | bytes 1572872 | tf_op jit(solution)/shard_map/ppermute | solution.py:418
  425.4 30.4 %collective-permute-start.43 = (bf16[2,2,128,512]{3,2,0,1:T(8,128)(2,1)}, bf16[2,2,128,512]{3,2,0,1:T(8,128)(2,1)}, u32[]{:S(2)}, u32[]{:S(2)}) collective-permute-start(bf16[2,2,128,512]{3,2,0,1:T(8,128)(2,1)} %fusion.15), channel_id=1, source_target_pairs={{0,1},{1,0},{2,3},{3,2},{4,5},{5,4},{6,7},{7,6},{8,9},{9,8},{10,11... | collective-permute-start | bytes 1572872 | tf_op jit(solution)/shard_map/ppermute | solution.py:418
  433.0 28.5 %collective-permute-start.41 = (bf16[1,2,128,2048]{3,2,1,0:T(8,128)(2,1)}, bf16[1,2,128,2048]{3,2,1,0:T(8,128)(2,1)}, u32[]{:S(2)}, u32[]{:S(2)}) collective-permute-start(bf16[1,2,128,2048]{3,2,1,0:T(8,128)(2,1)} %get-tuple-element.217), channel_id=1, source_target_pairs={{0,16},{1,17},{2,18},{3,19},{4,20},{5,21},{6,22},{7,23},{8,24},{9,... | collective-permute-start | bytes 3145736 | tf_op jit(solution)/shard_map/ppermute | solution.py:418
  434.5 27.1 %collective-permute-start.42 = (bf16[1,2,128,2048]{3,2,1,0:T(8,128)(2,1)}, bf16[1,2,128,2048]{3,2,1,0:T(8,128)(2,1)}, u32[]{:S(2)}, u32[]{:S(2)}) collective-permute-start(bf16[1,2,128,2048]{3,2,1,0:T(8,128)(2,1)} %get-tuple-element.218), channel_id=1, source_target_pairs={{0,8},{1,9},{2,10},{3,11},{4,12},{5,13},{6,14},{7,15},{8,0},{9,1},... | collective-permute-start | bytes 3145736 | tf_op jit(solution)/shard_map/ppermute | solution.py:418
  452.4 57.3 %collective-permute-start.34 = (bf16[4,512,1024]{2,1,0:T(8,128)(2,1)}, bf16[4,512,1024]{2,1,0:T(8,128)(2,1)}, u32[]{:S(2)}, u32[]{:S(2)}) collective-permute-start(bf16[4,512,1024]{2,1,0:T(8,128)(2,1)} %get-tuple-element.193), channel_id=1, source_target_pairs={{0,4},{1,5},{2,6},{3,7},{4,0},{5,1},{6,2},{7,3},{8,12},{9,13},{10,... | collective-permute-start | bytes 12582920 | tf_op jit(solution)/shard_map/ppermute | solution.py:418
  472.5 26.4 %collective-permute-start.45 = (bf16[1,1,128,2048]{3,2,1,0:T(8,128)(2,1)}, bf16[1,1,128,2048]{3,2,1,0:T(8,128)(2,1)S(1)}, u32[]{:S(2)}, u32[]{:S(2)}) collective-permute-start(bf16[1,1,128,2048]{3,2,1,0:T(8,128)(2,1)} %get-tuple-element.226), channel_id=1, source_target_pairs={{0,8},{1,9},{2,10},{3,11},{4,12},{5,13},{6,14},{7,15},{8,0},{9,1},... | collective-permute-start | bytes 1572872 | tf_op jit(solution)/shard_map/ppermute | solution.py:418
  474.0 24.9 %collective-permute-start.46 = (bf16[1,1,128,2048]{3,2,1,0:T(8,128)(2,1)}, bf16[1,1,128,2048]{3,2,1,0:T(8,128)(2,1)}, u32[]{:S(2)}, u32[]{:S(2)}) collective-permute-start(bf16[1,1,128,2048]{3,2,1,0:T(8,128)(2,1)} %get-tuple-element.227), channel_id=1, source_target_pairs={{0,16},{1,17},{2,18},{3,19},{4,20},{5,21},{6,22},{7,23},{8,24},{9,... | collective-permute-start | bytes 1572872 | tf_op jit(solution)/shard_map/ppermute | solution.py:418
  498.9 72.9 %collective-permute-start.33 = (bf16[4,512,1024]{2,1,0:T(8,128)(2,1)}, bf16[4,512,1024]{2,1,0:T(8,128)(2,1)}, u32[]{:S(2)}, u32[]{:S(2)}) collective-permute-start(bf16[4,512,1024]{2,1,0:T(8,128)(2,1)} %get-tuple-element.188), channel_id=1, source_target_pairs={{0,4},{1,5},{2,6},{3,7},{4,0},{5,1},{6,2},{7,3},{8,12},{9,13},{10,... | collective-permute-start | bytes 12582920 | tf_op jit(solution)/shard_map/ppermute | solution.py:418
  515.5 25.6 %collective-permute-start.47 = (bf16[2,2,128,1024]{3,2,1,0:T(8,128)(2,1)}, bf16[2,2,128,1024]{3,2,1,0:T(8,128)(2,1)S(1)}, u32[]{:S(2)}, u32[]{:S(2)}) collective-permute-start(bf16[2,2,128,1024]{3,2,1,0:T(8,128)(2,1)} %get-tuple-element.230), channel_id=1, source_target_pairs={{0,16},{1,17},{2,18},{3,19},{4,20},{5,21},{6,22},{7,23},{8,24},{9,... | collective-permute-start | bytes 3145736 | tf_op jit(solution)/shard_map/ppermute | solution.py:418
  517.0 25.3 %collective-permute-start.48 = (bf16[2,2,128,1024]{3,2,1,0:T(8,128)(2,1)}, bf16[2,2,128,1024]{3,2,1,0:T(8,128)(2,1)S(1)}, u32[]{:S(2)}, u32[]{:S(2)}) collective-permute-start(bf16[2,2,128,1024]{3,2,1,0:T(8,128)(2,1)} %get-tuple-element.231), channel_id=1, source_target_pairs={{0,8},{1,9},{2,10},{3,11},{4,12},{5,13},{6,14},{7,15},{8,0},{9,1},... | collective-permute-start | bytes 3145736 | tf_op jit(solution)/shard_map/ppermute | solution.py:418
  520.1 26.8 %collective-permute-start.50 = (bf16[2,32,2048]{2,1,0:T(8,128)(2,1)}, bf16[2,32,2048]{2,1,0:T(8,128)(2,1)}, u32[]{:S(2)}, u32[]{:S(2)}) collective-permute-start(bf16[2,32,2048]{2,1,0:T(8,128)(2,1)} %fusion.38), channel_id=1, source_target_pairs={{0,2},{1,3},{2,0},{3,1},{4,6},{5,7},{6,4},{7,5},{8,10},{9,11},{10,... | collective-permute-start | bytes 786440 | tf_op jit(solution)/shard_map/ppermute | solution.py:418
  523.1 42.5 %collective-permute-start.64 = (f32[2,8,128]{2,1,0:T(8,128)S(1)}, f32[2,8,128]{2,1,0:T(8,128)S(1)}, u32[]{:S(2)}, u32[]{:S(2)}) collective-permute-start(f32[2,8,128]{2,1,0:T(8,128)S(1)} %constant_dynamic-slice_fusion.2), channel_id=1, source_target_pairs={{0,2},{1,3},{2,0},{3,1},{4,6},{5,7},{6,4},{7,5},{8,10},{9,11},{10,... | collective-permute-start | bytes 24584 | tf_op jit(solution)/shard_map/ppermute | solution.py:418
  (101 other events, 1118.1 us)

commit v4 on v3

--- a/solution.py
+++ b/solution.py
@@ -1,4 +1,5 @@
 import functools
+import math
 
 import jax
 import jax.numpy as jnp
@@ -36,10 +37,6 @@
     centred = hidden - average
     variance = jnp.mean(centred * centred, axis=-1, keepdims=True)
     return centred * lax.rsqrt(variance + EPSILON) * gain_row + shift_row
-
-
-def gelu_exact(pre_gelu):
-    return jax.nn.gelu(pre_gelu, approximate=False)
 
 
 def pair_stack(rows):
@@ -99,19 +96,32 @@
 
 
 PAIR = 2 * HD
+UNROLL = 2
+
+
+def lane_block(at):
+    return pl.ds(pl.multiple_of(at * PAIR, PAIR), PAIR)
 
 
 def cross_kernel(place, length, q, k, v, *refs):
     out, lse = refs[-2:]
-    out[...], lse[0, 0] = attend_pair(q[...], k[...], v[...], length[0])
+    for u in range(UNROLL):
+        cut = slice(u * PAIR, (u + 1) * PAIR)
+        found, lse[0, u] = attend_pair(q[:, cut], k[:, cut], v[:, cut], length[0])
+        out[:, lane_block(place[pl.program_id(0) * UNROLL + u])] = found
 
 
 def cross_back_kernel(place, length, q, k, v, lse, d_out, *refs):
     d_q, d_k, d_v = refs[-3:]
-    d_q[...], d_k[...], d_v[...] = attend_pair_back(
-        q[...], k[...], v[...], lse[0, 0], d_out[...], length[0]
-    )
-    d_q[...] = d_q[...] * jnp.asarray(HD**-0.5, BF)
+    for u in range(UNROLL):
+        cut = slice(u * PAIR, (u + 1) * PAIR)
+        cotangent = d_out[:, lane_block(place[pl.program_id(0) * UNROLL + u])]
+        found = attend_pair_back(
+            q[:, cut], k[:, cut], v[:, cut], lse[0, u], cotangent, length[0]
+        )
+        d_q[:, cut] = found[0] * jnp.asarray(HD**-0.5, BF)
+        d_k[:, cut] = found[1]
+        d_v[:, cut] = found[2]
 
 
 def cross_call(kernel, q, k, lengths, place, item, values, in_specs, out_specs, out_shape, so_far):
@@ -119,7 +129,7 @@
         kernel,
         grid_spec=pltpu.PrefetchScalarGridSpec(
             num_scalar_prefetch=2,
-            grid=(q.shape[1] // PAIR,),
+            grid=(q.shape[1] // PAIR // UNROLL,),
             in_specs=in_specs + [pl.BlockSpec(memory_space=pl.ANY)] * len(so_far),
             out_specs=out_specs,
         ),
@@ -130,11 +140,11 @@
 
 
 def cross_specs(q, k, items, item):
-    t, s = q.shape[0] // items, k.shape[0] // items
-    rows = pl.BlockSpec((t, PAIR), lambda j, *_: (item, j))
-    slots = pl.BlockSpec((s, PAIR), lambda j, *_: (item, j))
-    placed = pl.BlockSpec((t, PAIR), lambda j, place, length: (item, place[j]))
-    lse = pl.BlockSpec((1, 1, 1, 2 * t), lambda j, *_: (item, j, 0, 0))
+    t, s, n = q.shape[0] // items, k.shape[0] // items, PAIR * UNROLL
+    rows = pl.BlockSpec((t, n), lambda j, *_: (item, j))
+    slots = pl.BlockSpec((s, n), lambda j, *_: (item, j))
+    placed = pl.BlockSpec((t, q.shape[1]), lambda j, *_: (item, 0))
+    lse = pl.BlockSpec((1, UNROLL, 1, 2 * t), lambda j, *_: (item, j, 0, 0))
     return rows, slots, placed, lse
 
 
@@ -326,6 +336,171 @@
     )(blocks, *lefts, *values)
 
 
+def normed(hidden):
+    centred = hidden - jnp.mean(hidden, axis=-1, keepdims=True)
+    scale = lax.rsqrt(jnp.mean(centred * centred, axis=-1, keepdims=True) + EPSILON)
+    return centred * scale, scale
+
+
+def norm_kernel(blocks, branch, residual, gain, shift, pre, out, rel0, rel1):
+    pre[...] = residual[...].astype(F32) + branch[...]
+    out[...] = normed(pre[...])[0] * gain[...] + shift[...]
+    half = blocks.shape[0] // 2
+    size = out.shape[1] // blocks.shape[0]
+    for i in range(2 * half):
+        rel, at = (rel0, i) if i < half else (rel1, i - half)
+        block = out[:, pl.ds(pl.multiple_of(blocks[i] * size, 128), size)]
+        rel[:, at * size : (at + 1) * size] = block.astype(BF)
+
+
+def norm(branch, residual, gain, shift, blocks):
+    m, n = branch.shape
+    rows = m // 2
+    full = pl.BlockSpec((rows, n), lambda i, *_: (i, 0))
+    halves = pl.BlockSpec((rows, n // 2), lambda i, *_: (i, 0))
+    row = pl.BlockSpec((1, n), lambda i, *_: (0, 0))
+    pre, out, rel0, rel1 = pl.pallas_call(
+        norm_kernel,
+        grid_spec=pltpu.PrefetchScalarGridSpec(
+            num_scalar_prefetch=1,
+            grid=(2,),
+            in_specs=[full, full, row, row],
+            out_specs=[full, full, halves, halves],
+        ),
+        out_shape=[
+            jax.ShapeDtypeStruct((m, n), F32),
+            jax.ShapeDtypeStruct((m, n), F32),
+            jax.ShapeDtypeStruct((m, n // 2), BF),
+            jax.ShapeDtypeStruct((m, n // 2), BF),
+        ],
+        name="norm",
+    )(blocks, branch, residual, gain, shift)
+    return pre, out, (rel0, rel1)
+
+
+def norm_back_kernel(count, *refs):
+    pre, gain = refs[count : count + 2]
+    d_pre, low, sums = refs[-3:]
+    cotangent = refs[0][...].astype(F32)
+    for ref in refs[1:count]:
+        cotangent = cotangent + ref[...]
+    z, scale = normed(pre[...])
+    if len(refs) > count + 5:
+        shift, out = refs[count + 2], refs[-4]
+        out[...] = (z * gain[...] + shift[...]).astype(BF)
+    inner = cotangent * gain[...]
+    found = scale * (
+        inner
+        - jnp.mean(inner, axis=-1, keepdims=True)
+        - z * jnp.mean(inner * z, axis=-1, keepdims=True)
+    )
+    d_pre[...] = found
+    low[...] = found.astype(BF)
+
+    @pl.when(pl.program_id(0) == 0)
+    def _():
+        sums[...] = jnp.zeros_like(sums)
+
+    rows = [found.astype(BF).astype(F32), cotangent, cotangent * z]
+    for i, value in enumerate(rows):
+        sums[i : i + 1, :] += jnp.sum(value, axis=0, keepdims=True)
+
+
+def norm_back(cotangents, pre, gain, shift=None):
+    m, n = pre.shape
+    rows = m // 2
+    full = pl.BlockSpec((rows, n), lambda i: (i, 0))
+    row = pl.BlockSpec((1, n), lambda i: (0, 0))
+    extra = [] if shift is None else [shift]
+    out_specs = [full, full, pl.BlockSpec((8, n), lambda i: (0, 0))]
+    out_shape = [
+        jax.ShapeDtypeStruct((m, n), F32),
+        jax.ShapeDtypeStruct((m, n), BF),
+        jax.ShapeDtypeStruct((8, n), F32),
+    ]
+    if shift is not None:
+        out_specs, out_shape = [full] + out_specs, [jax.ShapeDtypeStruct((m, n), BF)] + out_shape
+    return pl.pallas_call(
+        functools.partial(norm_back_kernel, len(cotangents)),
+        grid=(2,),
+        in_specs=[full] * (len(cotangents) + 1) + [row] * (1 + len(extra)),
+        out_specs=out_specs,
+        out_shape=out_shape,
+        name="norm_back",
+    )(*cotangents, pre, gain, *extra)
+
+
+def gelu_parts(u):
+    half_erf = 0.5 * (1.0 + lax.erf(u * (0.5**0.5)))
+    return u * half_erf, half_erf + u * jnp.exp(-0.5 * u * u) * (0.5 / math.pi) ** 0.5
+
+
+def ffn_up_kernel(places, x0, x1, near, far, bias, hidden, slope):
+    u = dot_nn(x0[...], near[...]) + dot_nn(x1[...], far[...]) + bias[...]
+    value, slope[...] = gelu_parts(u)
+    hidden[...] = value.astype(BF)
+
+
+def ffn_up(rows, weight, bias, places):
+    near, far = weight
+    m, h = rows[0].shape
+    n = near.shape[1]
+    size = n // places.shape[0]
+    whole = pl.BlockSpec((m, h), lambda j, *_: (0, 0))
+    columns = pl.BlockSpec((h, size), lambda j, *_: (0, j))
+    return pl.pallas_call(
+        ffn_up_kernel,
+        grid_spec=pltpu.PrefetchScalarGridSpec(
+            num_scalar_prefetch=1,
+            grid=(n // size,),
+            in_specs=[whole, whole, columns, columns, pl.BlockSpec((1, size), lambda j, *_: (0, j))],
+            out_specs=[
+                pl.BlockSpec((m, size), lambda j, places: (0, places[j])),
+                pl.BlockSpec((m, size), lambda j, places: (0, j)),
+            ],
+        ),
+        out_shape=[jax.ShapeDtypeStruct((m, n), BF), jax.ShapeDtypeStruct((m, n), F32)],
+        name="ffn_up",
+    )(places, *rows, near, far, bias)
+
+
+def ffn_down_back_kernel(blocks, cotangent, near, far, slope, out):
+    chosen = pl.program_id(0) < pl.num_programs(0) // 2
+
+    @pl.when(chosen)
+    def _():
+        out[...] = (dot_nt(cotangent[...], near[...]) * slope[...]).astype(BF)
+
+    @pl.when(jnp.logical_not(chosen))
+    def _():
+        out[...] = (dot_nt(cotangent[...], far[...]) * slope[...]).astype(BF)
+
+
+def ffn_down_back(cotangent, weight, slope, blocks):
+    near, far = weight
+    m, k = cotangent.shape
+    count = blocks.shape[0]
+    half = count // 2
+    size = near.shape[0] // half
+    natural = pl.BlockSpec((m, size), lambda j, blocks: (0, blocks[j]))
+    return pl.pallas_call(
+        ffn_down_back_kernel,
+        grid_spec=pltpu.PrefetchScalarGridSpec(
+            num_scalar_prefetch=1,
+            grid=(count,),
+            in_specs=[
+                pl.BlockSpec((m, k), lambda j, *_: (0, 0)),
+                pl.BlockSpec((size, k), lambda j, *_: (jnp.minimum(j, half - 1), 0)),
+                pl.BlockSpec((size, k), lambda j, *_: (jnp.maximum(j - half, 0), 0)),
+                natural,
+            ],
+            out_specs=natural,
+        ),
+        out_shape=jax.ShapeDtypeStruct((m, count * size), BF),
+        name="ffn_down_back",
+    )(blocks, cotangent, near, far, slope)
+
+
 def memory_kernel(x0, x1, k0, k1, v0, v1, bias, keys, values):
     keys[...] = (dot_nn(x0[...], k0[...]) + dot_nn(x1[...], k1[...])).astype(BF)
     total = dot_nn(x0[...], v0[...]) + dot_nn(x1[...], v1[...])
@@ -419,14 +594,14 @@
             for v, (_, m) in zip(sends, stream.sends)
         ]
         if during is not None:
-            got, _ = lax.optimization_barrier((got, during))
+            got, during = lax.optimization_barrier((got, during))
         stream.feed(got)
-        return got
-
-    def across_steps(self, stream, after, during=None):
+        return got if during is None else (got, during)
+
+    def across_steps(self, stream, after, during):
         for _ in self.across[1:]:
-            after = self.step(stream, after, during)
-        return after
+            after, during = self.step(stream, after, during)
+        return after, during
 
     def finish(self, stream):
         while stream.result is None:
@@ -540,6 +715,12 @@
         self.steps, self.result = steps, None
         self.sends = next(steps)
 
+    def values(self):
+        return [value for value, _ in self.sends]
+
+    def replace(self, values):
+        self.sends = [(v, mask) for v, (_, mask) in zip(values, self.sends)]
+
     def feed(self, got):
         try:
             self.sends = self.steps.send(list(got))
@@ -605,7 +786,14 @@
             [project_back(rows, weight[0]), project_back(rows, weight[1])], axis=1
         )
 
-    inputs_f = inputs.astype(F32)
+
+    def add_norm(branch, residual, gain, shift):
+        if (model_width // plan.wide) % 128 == 0:
+            return norm(branch, residual, gain[None], shift[None], plan.blocks())
+        pre = residual.astype(F32) + branch
+        out = layer_norm(pre, gain, shift)
+        return pre, out, plan.relative(out.astype(BF))
+
 
     share, hidden_share = self_gain.shape[0], ffn_bias_in.shape[0]
     small_rows = jnp.concatenate(
@@ -653,8 +841,8 @@
     for _ in plan.zs[1:]:
         cross_z = plan.step(crosses, cross_z)
     self_core = plan.step(selfs, cross_z)
-    last = plan.step(crosses, last)
     fin_z = plan.step(fins, cross_z)
+    last, fin_z = plan.step(crosses, last, fin_z)
     table = small.result.astype(F32)
     vectors = table[:, : vector_count * share].reshape(plan.count, vector_count, share)
     vectors = jnp.swapaxes(vectors, 0, 1).reshape(vector_count, model_width)
@@ -680,65 +868,62 @@
     )
     self_ctx, self_lse = self_attend(qkv, item_count, place)
     self_rel = to_relative(self_ctx)
-    first_pre = inputs_f + stack_project(self_rel, selfs.result, 3, sbias[None, 2:3], (1.0,), F32)[0]
-    first = layer_norm(first_pre, sgain, sbias[3])
-    first_rel = plan.relative(first.astype(BF))
-    last = plan.across_steps(crosses, (last, self_core, fin_z), first_rel)
+    branch = stack_project(self_rel, selfs.result, 3, sbias[None, 2:3], (1.0,), F32)[0]
+    after = (last, self_core, fin_z)
     for _ in plan.zs[1:]:
         fin_z = plan.step(fins, fin_z)
     fout_z = plan.step(fouts, fin_z)
+    last, (branch, fout_z) = plan.across_steps(crosses, after, (branch, fout_z))
+    first_pre, first, first_rel = add_norm(branch, inputs, sgain, sbias[3])
     cross_core = plan.step(crosses)
-    last = plan.step(fins, (last, fout_z))
     for _ in plan.zs[1:]:
         fout_z = plan.step(fouts, fout_z)
+    last, _ = plan.step(fins, last, (cross_core, fout_z))
+
     queries_two = stack_project(first_rel, crosses.result, 0, cbias[None, 0:1], (scaling,), BF)[0]
     mem_rel = plan.relative(memory.reshape(item_count * mem_slots, model_width))
     mem_keys, mem_values = memory_project(mem_rel, crosses.result, 1, 2, cbias[1:2], 512)
-    last = plan.across_steps(
-        fins, (last, cross_core, fout_z), (queries_two, mem_keys, mem_values)
-    )
-    fin_core = plan.step(fins)
     cross_out = ()
     for item in range(item_count):
         cross_out = cross_attend(
             queries_two, mem_keys, mem_values, mem_lengths, place, item, cross_out
         )
         if item == 0:
-            last = plan.step(fouts, last, cross_out)
+            last, cross_out = plan.across_steps(fins, last, cross_out)
+    fin_core = plan.step(fins)
+    last, (cross_out, _) = plan.step(fouts, last, (cross_out, fin_core))
     cross_ctx, cross_lse = cross_out
     fin = fins.result
     cross_rel = to_relative(cross_ctx)
-    second_pre = first + stack_project(cross_rel, crosses.result, 3, cbias[None, 2:3], (1.0,), F32)[0]
-    second = layer_norm(second_pre, cgain, cbias[3])
-    second_rel = plan.relative(second.astype(BF))
-    plan.across_steps(fouts, (last, fin_core), second_rel)
-
-    pre_gelu = forward(second_rel, fin) + fbin
-    hidden, gelu_pull = jax.vjp(gelu_exact, pre_gelu)
-    hidden_rel = plan.relative(hidden.astype(BF))
-    plan.step(fouts, None, hidden_rel)
+    branch = stack_project(cross_rel, crosses.result, 3, cbias[None, 2:3], (1.0,), F32)[0]
+    second_pre, second, second_rel = add_norm(branch, first, cgain, cbias[3])
+
+    places = plan.places()
+    hidden, slope = ffn_up(second_rel, fin, fbin[None], places)
+    _, (hidden, slope) = plan.across_steps(fouts, last, (hidden, slope))
+    half = hidden.shape[1] // 2
+    hidden_rel = (hidden[:, :half], hidden[:, half:])
+    plan.step(fouts)
     fout = fouts.result
     third_pre = second + (forward(hidden_rel, fout) + fbout[0])
-    layer_out, norm_pull = jax.vjp(layer_norm, third_pre, fgain, fbout[1])
-
-    d_third, g_fgain, g_fshift = norm_pull(out_grad.astype(F32))
-    e_three = d_third.astype(BF)
+
+    layer_out, d_third, e_three, third_sums = norm_back(
+        [out_grad], third_pre, fgain[None], fbout[1:2]
+    )
     half = model_width // 2
     to_fout = Stream(
         plan.scatter([hidden_rel], [e_three], [(0, 0, 0, half), (0, 0, half, half)])
     )
-    d_pre = gelu_pull(plan.natural(backward(e_three, fout)))[0].astype(BF)
-    plan.step(to_fout, None, d_pre)
+    d_pre = ffn_down_back(e_three, fout, slope, plan.blocks())
+    _, d_pre = plan.step(to_fout, None, d_pre)
     half = d_pre.shape[1] // 2
     to_fin = Stream(plan.scatter([second_rel], [d_pre], [(0, 0, 0, half), (0, 0, half, half)]))
-    g_fbin = column_sums(d_pre)
-    d_second = d_third + back([d_pre], fin, None, row_count)
-
-    _, norm_pull_two = jax.vjp(layer_norm, second_pre, cgain, cbias[3])
-    d_second_pre, g_cgain, g_cshift = norm_pull_two(d_second)
-    e_two = d_second_pre.astype(BF)
-    last = plan.step(to_fout, None, (e_two, [v for v, _ in to_fin.sends]))
-    plan.step(to_fin)
+    d_hidden = back([d_pre], fin, None, row_count)
+    last, (d_hidden, fin_sends) = plan.step(to_fout, None, (d_hidden, to_fin.values()))
+    to_fin.replace(fin_sends)
+    fin_core = plan.step(to_fin)
+
+    d_second_pre, e_two, second_sums = norm_back([d_third, d_hidden], second_pre, cgain[None])
     d_cross_ctx = context_back(e_two, crosses.result)
     cross_back = ()
     for item in range(item_count):
@@ -747,7 +932,7 @@
             item, cross_back,
         )
         if item == 0:
-            last = plan.across_steps(to_fout, last, cross_back)
+            last, (cross_back, _) = plan.across_steps(to_fout, last, (cross_back, fin_core))
     dq_scaled, dk_flat, dv_flat = cross_back
     to_cross = Stream(
         plan.scatter(
@@ -756,17 +941,21 @@
             [(0, 0, 0, model_width), (1, 1, 0, model_width), (1, 2, 0, model_width), (2, 3, 0, model_width)],
         )
     )
-    last = plan.step(to_fin, last, [v for v, _ in to_cross.sends])
-    plan.step(to_cross)
-    for _ in plan.zs:
+    d_queries = back([dq_scaled], crosses.result, [0], row_count)
+    for _ in plan.zs[1:]:
         fout_last = plan.step(to_fout)
-    d_first = d_second_pre + back([dq_scaled], crosses.result, [0], row_count)
-
-    _, norm_pull_one = jax.vjp(layer_norm, first_pre, sgain, sbias[3])
-    d_first_pre, g_sgain, g_sshift = norm_pull_one(d_first)
-    e_one = d_first_pre.astype(BF)
+    last, (d_queries, _, cross_sends) = plan.step(
+        to_fin, last, (d_queries, fout_last, to_cross.values())
+    )
+    to_cross.replace(cross_sends)
+    cross_core = plan.step(to_cross)
+    fout_last = plan.step(to_fout)
+
+    d_first_pre, e_one, first_sums = norm_back([d_second_pre, d_queries], first_pre, sgain[None])
     d_self_ctx = context_back(e_one, selfs.result)
-    last = plan.across_steps(to_fin, (last, fout_last), d_self_ctx)
+    last, (d_self_ctx, *_) = plan.across_steps(
+        to_fin, last, (d_self_ctx, cross_core, fout_last)
+    )
     dq_self, dk_self, dv_self = self_attend_back(qkv, self_lse, d_self_ctx, item_count, place)
     to_self = Stream(
         plan.scatter(
@@ -775,47 +964,55 @@
             [(0, 0, 0, model_width), (0, 1, 0, model_width), (0, 2, 0, model_width), (1, 3, 0, model_width)],
         )
     )
-    last = plan.step(to_cross, last, [v for v, _ in to_self.sends])
-    plan.step(to_self)
-    for _ in plan.zs:
+    for _ in plan.zs[1:]:
         fin_last = plan.step(to_fin)
-    input_grad = d_first_pre + back(
-        [dq_self, dk_self, dv_self], selfs.result, [0, 1, 2], row_count
-    )
-    last = plan.across_steps(to_cross, (last, fin_last), input_grad)
-    memory_grad = back([dk_flat, dv_flat], crosses.result, [1, 2], 512).reshape(memory.shape)
-    last = plan.step(to_self, last, memory_grad)
-    for _ in plan.zs:
+    last, (_, self_sends) = plan.step(to_cross, last, (fin_last, to_self.values()))
+    to_self.replace(self_sends)
+    self_core = plan.step(to_self)
+    fin_last = plan.step(to_fin)
+    late, _ = lax.optimization_barrier(((dq_self, dk_self, dv_self), last))
+    d_inputs = back(late, selfs.result, [0, 1, 2], row_count)
+    last, (d_inputs, *_) = plan.across_steps(
+        to_cross, last, (d_inputs, self_core, fin_last)
+    )
+    input_grad = d_first_pre + d_inputs
+    late, _ = lax.optimization_barrier(((dk_flat, dv_flat), last))
+    memory_grad = back(late, crosses.result, [1, 2], 512).reshape(memory.shape)
+    for _ in plan.zs[1:]:
         cross_last = plan.step(to_cross)
-    plan.across_steps(to_self, (last, cross_last))
-    plan.finish(to_self)
-    grads = jnp.stack(
+    last, _ = plan.step(to_self, last, (memory_grad, cross_last))
+    cross_last = plan.step(to_cross)
+    last, _ = plan.across_steps(to_self, last, cross_last)
+    sums, _ = lax.optimization_barrier(((dq_self, dv_self, dq_scaled, dv_flat, d_pre), last))
+    sum_dq, sum_dv, sum_dq2, sum_dv2, sum_hidden = [column_sums(v) for v in sums]
+    grads = jnp.concatenate(
         [
-            column_sums(dq_self),
-            column_sums(dv_self),
-            column_sums(e_one),
-            g_sshift,
-            g_sgain,
-            column_sums(dq_scaled),
-            column_sums(dv_flat),
-            column_sums(e_two),
-            g_cshift,
-            g_cgain,
-            column_sums(e_three),
-            g_fshift,
-            g_fgain,
-        ]
+            sum_dq[None],
+            sum_dv[None],
+            first_sums[:3],
+            sum_dq2[None],
+            sum_dv2[None],
+            second_sums[:3],
+            third_sums[:3],
+        ],
+        axis=0,
     )
     grads = jnp.swapaxes(grads.reshape(vector_count, plan.count, share), 0, 1)
     to_small = Stream(
         plan.scatter_small(
             pad_lanes(
                 jnp.concatenate(
-                    [grads.reshape(plan.count, -1), g_fbin.reshape(plan.count, -1)], axis=1
+                    [grads.reshape(plan.count, -1), sum_hidden.reshape(plan.count, -1)], axis=1
                 )
             )
         )
     )
+    for _ in plan.zs[1:]:
+        plan.step(to_small)
+        plan.step(to_small)
+        plan.step(to_small, plan.step(to_self))
+    for stream in (to_self, to_cross, to_fin, to_fout):
+        plan.finish(stream)
     plan.finish(to_small)
     small_sums = to_small.result
     found = small_sums[: vector_count * share].reshape(vector_count, share)
@@ -824,7 +1021,7 @@
     g_fout = jnp.concatenate([to_fout.result[0], to_fout.result[1]], axis=1)
     g_fin = jnp.concatenate([to_fin.result[0], to_fin.result[1]], axis=1)
     return (
-        layer_out.astype(BF),
+        layer_out,
         input_grad,
         memory_grad,
         g_self[:3],

time: 651 us -> 582 us (0.89)
  waiting for transfers between devices: 211 us -> 148 us
  Pallas kernels: 208 us -> 243 us
  matrix products: 28.3 us -> 4.73 us
  other arithmetic: 73.8 us -> 55.1 us
  local copies, waits for them, and re-layouts: 46.9 us -> 54.9 us
    ppermute x66, waiting for transfers between devices: 211 us -> 148 us  [step(): lax.ppermute(v, AXES, [(i, i ^ m) for i in range(self.count)])]
    pallas_call x0 -> x7, Pallas kernels: none -> 38 us  [the longest x1 10.9 us: ffn_up(): pl.pallas_call(ffn_up_kernel, grid_spec=pltpu.PrefetchScalarGridSpec(num_...]
    dot_general x4 -> x2, matrix products: 22 us -> 4.73 us  [project(): return jnp.dot(left_rows, weight, preferred_element_type=F32)]
    reduce_sum x11 -> x0, other arithmetic: 8.69 us -> none  [the longest x3 3.92 us: layer_norm(): return centred * lax.rsqrt(variance + EPSILON) * gain_row + shift_row]
    slice x0 -> x11, local copies, waits for them, and re-layouts: none -> 8.47 us  [the longest x1 3.25 us: local(): hidden_rel = (hidden[:, :half], hidden[:, half:])]
    reduce_sum x8 -> x5, other arithmetic: 10.4 us -> 3.22 us  [column_sums(): return jnp.sum(gradient.astype(F32), axis=0)]
    unnamed x119 -> x129, local copies, waits for them, and re-layouts: 14.9 us -> 8.78 us
  transfers between devices with their start and end apart: 66 -> 66, of which waited for: 32 -> 32; matrix products, arithmetic and copies ran while one was open for 15% -> 11% of each run, Pallas kernels for 29% -> 36%
where the time goes in v4:
time: 582 us; the launch traced here: 574 us
  Pallas kernels  243 us (42%)
  waiting for transfers between devices  148 us (25%)
  starting transfers between devices  65.8 us (11%)
  other arithmetic  55.1 us (9%)
  local copies, waits for them, and re-layouts  54.9 us (9%)
    ppermute x66, waiting for transfers between devices, step(): lax.ppermute(v, AXES, [(i, i ^ m) for i in range(self.count)])  148 us
    ppermute x66, starting transfers between devices, step(): lax.ppermute(v, AXES, [(i, i ^ m) for i in range(self.count)])  65.8 us
    pallas_call x4, Pallas kernels, cross_call(): pl.pallas_call(kernel, grid_spec=pltpu.PrefetchScalarGridSpec(num_scalar_...  47.7 us
    pallas_call x6, Pallas kernels, back_natural(): pl.pallas_call(back_kernel, grid_spec=pltpu.PrefetchScalarGridSpec(num_sc...  42.4 us
    pallas_call x4, Pallas kernels, stack_grads(): pl.pallas_call(functools.partial(grads_kernel, table), grid=(len(products...  37 us
    pallas_call x8, Pallas kernels, add_split(): pl.pallas_call(add_split_kernel, grid=shapes[0].shape[:2], in_specs=in_sp...  36.3 us
    pallas_call x4, Pallas kernels, stack_project(): pl.pallas_call(functools.partial(project_kernel, scales), grid=(count,),...  16.1 us
    pallas_call x1, Pallas kernels, memory_project(): pl.pallas_call(memory_kernel, grid=(m // block,), in_specs=[pl.BlockSpec(...  13 us
  transfers between devices with their start and end apart: 66, of which 32 were waited for; matrix products, arithmetic and copies ran while one was open for 11% of the time, Pallas kernels for 36%

profile of v4, /device:TPU:0, one launch (start us, length us, event | category | flops | bytes accessed | tf_op | source)
XLA Modules:
  0.0 574.1 jit_solution(16516985577638225853)
XLA Ops:
  11.5 10.9 %collective-permute-done.1 = bf16[4,1,32,1024]{3,2,0,1:T(8,128)(2,1)S(1)} collective-permute-done((bf16[4,1,32,1024]{3,2,0,1:T(8,128)(2,1)S(1)}, bf16[4,1,32,1024]{3,2,0,1:T(8,128)(2,1)S(1)}, u32[]{:S(2)}, u32[]{:S(2)}) %collective-permute-start.1) | collective-permute-done | bytes 262176 | tf_op jit(solution)/shard_map/ppermute | solution.py:593
  27.0 9.2 %collective-permute-done.3 = bf16[4,2,32,1024]{3,2,1,0:T(8,128)(2,1)S(1)} collective-permute-done((bf16[4,2,32,1024]{3,2,1,0:T(8,128)(2,1)S(1)}, bf16[4,2,32,1024]{3,2,1,0:T(8,128)(2,1)S(1)}, u32[]{:S(2)}, u32[]{:S(2)}) %collective-permute-start.3) | collective-permute-done | bytes 524320 | tf_op jit(solution)/shard_map/ppermute | solution.py:593
  56.1 22.1 %collective-permute-done.12 = bf16[2,2,128,1024]{3,2,1,0:T(8,128)(2,1)S(1)} collective-permute-done((bf16[2,2,128,1024]{3,2,1,0:T(8,128)(2,1)S(1)}, bf16[2,2,128,1024]{3,2,1,0:T(8,128)(2,1)S(1)}, u32[]{:S(2)}, u32[]{:S(2)}) %collective-permute-start.12) | collective-permute-done | bytes 1048608 | tf_op jit(solution)/shard_map/ppermute | solution.py:593
  88.1 12.4 %collective-permute-done.8 = bf16[1,1,32,4096]{3,2,1,0:T(8,128)(2,1)S(1)} collective-permute-done((bf16[1,1,32,4096]{3,2,1,0:T(8,128)(2,1)S(1)}, bf16[1,1,32,4096]{3,2,1,0:T(8,128)(2,1)S(1)}, u32[]{:S(2)}, u32[]{:S(2)}) %collective-permute-start.8) | collective-permute-done | bytes 262176 | tf_op jit(solution)/shard_map/ppermute | solution.py:593
  146.1 8.7 %collective-permute-done.18 = bf16[1,2,128,1024]{3,2,1,0:T(8,128)(2,1)S(1)} collective-permute-done((bf16[1,2,128,1024]{3,2,1,0:T(8,128)(2,1)S(1)}, bf16[1,2,128,1024]{3,2,1,0:T(8,128)(2,1)S(1)}, u32[]{:S(2)}, u32[]{:S(2)}) %collective-permute-start.18) | collective-permute-done | bytes 524320 | tf_op jit(solution)/shard_map/ppermute | solution.py:593
  177.7 13.0 %memory_project.1 = (bf16[2048,1024]{1,0:T(8,128)(2,1)}, bf16[2048,1024]{1,0:T(8,128)(2,1)}) custom-call(bf16[2048,512]{1,0:T(8,128)(2,1)} %pad_maximum_fusion.4.x0.refs_2_, bf16[2048,512]{1,0:T(8,128)(2,1)} %pad_maximum_fusion.5.x1.refs_3_, bf16[4,512,1024]{2,1,0:T(8,128)(2,1)} %copy-done, bf16[4,512,1024]{2,1,0:T(8,128)(2,1)} %copy-done.1, ...), custom_call_target="tpu_custom_call" | custom-call | tf_op jit(solution)/shard_map/memory_project/pallas_call | solution.py:515
  190.6 11.4 %cross_attend.4 = (bf16[256,1024]{1,0:T(8,128)(2,1)}, f32[2,8,1,256]{3,2,1,0:T(1,128)}) custom-call(s32[8]{0:T(128)} %fusion.17.place.places, s32[1]{0:T(128)} %get-tuple-element.463.length, bf16[256,1024]{1,0:T(8,128)(2,1)} %bitcast.256, bf16[2048,1024]{1,0:T(8,128)(2,1)} %get-tuple-element.221.k, bf16[2048,1024]{1,0:T(8,128)(2,1)} %get-tuple-element.222.v), custom_call_target="tpu_custom_call" | custom-call | tf_op jit(solution)/shard_map/cross_attend/pallas_call | solution.py:128
  212.8 11.9 %cross_attend.5 = (bf16[256,1024]{1,0:T(8,128)(2,1)}, f32[2,8,1,256]{3,2,1,0:T(1,128)}) custom-call(s32[8]{0:T(128)} %fusion.17.place.places, s32[1]{0:T(128)} %get-tuple-element.462.length, bf16[256,1024]{1,0:T(8,128)(2,1)} %bitcast.257, bf16[2048,1024]{1,0:T(8,128)(2,1)} %get-tuple-element.221.k, ...), custom_call_target="tpu_custom_call", output_to_operand_aliasing={{0}: (5, {}), {1}: (6, {})} | custom-call | tf_op jit(solution)/shard_map/cross_attend/pallas_call | solution.py:128
  241.7 10.9 %ffn_up.1 = (bf16[256,4096]{1,0:T(8,128)(2,1)}, f32[256,4096]{1,0:T(8,128)}) custom-call(s32[8]{0:T(128)} %fusion.17.place.places, bf16[256,512]{1,0:T(8,128)(2,1)} %get-tuple-element.240.x0.refs_0_, bf16[256,512]{1,0:T(8,128)(2,1)} %get-tuple-element.241.x1.refs_1_, bf16[512,4096]{1,0:T(8,128)(2,1)} %get-tuple-element.378.near, ...), custom_call_target="tpu_custom_call" | custom-call | tf_op jit(solution)/shard_map/ffn_up/pallas_call | solution.py:451
  277.4 6.3 %stack_grads.4 = (bf16[2,2048,512]{2,1,0:T(8,128)(2,1)}, bf16[2,2048,512]{2,1,0:T(8,128)(2,1)}) custom-call(bf16[256,2048]{1,0:T(8,128)(2,1)} %get-tuple-element.388.refs_0_, bf16[256,2048]{1,0:T(8,128)(2,1)} %get-tuple-element.387.refs_1_, bf16[256,1024]{1,0:T(8,128)(2,1)} %get-tuple-element.249.refs_2_.cotangent), custom_call_target="tpu_custom_call" | custom-call | tf_op jit(solution)/shard_map/stack_grads/pallas_call | solution.py:289
  283.8 10.5 %ffn_down_back.1.refs_0_.refs_2_ = bf16[256,4096]{1,0:T(8,128)(2,1)} custom-call(s32[8]{0:T(128)} %broadcast_xor_fusion.blocks, bf16[256,1024]{1,0:T(8,128)(2,1)} %get-tuple-element.249.refs_2_.cotangent, bf16[2048,1024]{1,0:T(8,128)(2,1)} %pad_maximum_fusion.3.near, bf16[2048,1024]{1,0:T(8,128)(2,1)} %collective-permute-done.32.far, ...), custom_call_target="tpu_custom_call" | custom-call | tf_op jit(solution)/shard_map/ffn_down_back/pallas_call | solution.py:486
  300.8 6.5 %stack_grads.5 = (bf16[2,512,2048]{2,1,0:T(8,128)(2,1)}, bf16[2,512,2048]{2,1,0:T(8,128)(2,1)}) custom-call(bf16[256,512]{1,0:T(8,128)(2,1)} %get-tuple-element.240.x0.refs_0_, bf16[256,512]{1,0:T(8,128)(2,1)} %get-tuple-element.241.x1.refs_1_, bf16[256,4096]{1,0:T(8,128)(2,1)} %ffn_down_back.1.refs_0_.refs_2_), custom_call_target="tpu_custom_call" | custom-call | tf_op jit(solution)/shard_map/stack_grads/pallas_call | solution.py:289
  307.3 8.2 %back_natural.6.refs_1_ = f32[256,1024]{1,0:T(8,128)} custom-call(s32[8]{0:T(128)} %broadcast_xor_fusion.blocks, bf16[256,4096]{1,0:T(8,128)(2,1)} %ffn_down_back.1.refs_0_.refs_2_, bf16[1,512,4096]{2,1,0:T(8,128)(2,1)} %get-tuple-element.377.refs_1_, bf16[1,512,4096]{2,1,0:T(8,128)(2,1)} %bitcast.95.refs_2_), custom_call_target="tpu_custom_call" | custom-call | tf_op jit(solution)/shard_map/back_natural/pallas_call | solution.py:326
  315.5 9.7 %collective-permute-done.34.refs_1_.refs_3_ = bf16[1,2,512,512]{3,2,1,0:T(8,128)(2,1)S(1)} collective-permute-done((bf16[1,2,512,512]{3,2,1,0:T(8,128)(2,1)}, bf16[1,2,512,512]{3,2,1,0:T(8,128)(2,1)S(1)}, u32[]{:S(2)}, u32[]{:S(2)}) %collective-permute-start.34) | collective-permute-done | bytes 1048608 | tf_op jit(solution)/shard_map/ppermute | solution.py:593
  340.0 12.2 %cross_attend.6 = (bf16[256,1024]{1,0:T(8,128)(2,1)}, bf16[2048,1024]{1,0:T(8,128)(2,1)}, bf16[2048,1024]{1,0:T(8,128)(2,1)}) custom-call(s32[8]{0:T(128)} %fusion.17.place.places, s32[1]{0:T(128)} %get-tuple-element.463.length, bf16[256,1024]{1,0:T(8,128)(2,1)} %bitcast.258, bf16[2048,1024]{1,0:T(8,128)(2,1)} %get-tuple-element.221.k, ...), custom_call_target="tpu_custom_call" | custom-call | tf_op jit(solution)/shard_map/cross_attend/pallas_call | solution.py:128
  361.3 12.2 %cross_attend.7 = (bf16[256,1024]{1,0:T(8,128)(2,1)}, bf16[2048,1024]{1,0:T(8,128)(2,1)}, bf16[2048,1024]{1,0:T(8,128)(2,1)}) custom-call(s32[8]{0:T(128)} %fusion.17.place.places, s32[1]{0:T(128)} %get-tuple-element.462.length, bf16[256,1024]{1,0:T(8,128)(2,1)} %bitcast.259, ...), custom_call_target="tpu_custom_call", output_to_operand_aliasing={{0}: (7, {}), {1}: (8, {}), {2}: (9, {})} | custom-call | tf_op jit(solution)/shard_map/cross_attend/pallas_call | solution.py:128
  373.5 17.4 %stack_grads.6 = (bf16[4,512,1024]{2,1,0:T(8,128)(2,1)}, bf16[4,512,1024]{2,1,0:T(8,128)(2,1)}) custom-call(bf16[256,512]{1,0:T(8,128)(2,1)} %get-tuple-element.219.x0.refs_0_, bf16[256,512]{1,0:T(8,128)(2,1)} %get-tuple-element.220.x1.refs_1_, bf16[2048,512]{1,0:T(8,128)(2,1)} %pad_maximum_fusion.4.x0.refs_2_, ...), custom_call_target="tpu_custom_call" | custom-call | tf_op jit(solution)/shard_map/stack_grads/pallas_call | solution.py:289
  428.8 8.1 %self_attend_back.1 = (bf16[256,1024]{1,0:T(8,128)(2,1)}, bf16[256,1024]{1,0:T(8,128)(2,1)}, bf16[256,1024]{1,0:T(8,128)(2,1)}) custom-call(s32[8]{0:T(128)} %fusion.17.place.places, bf16[3,256,1024]{2,1,0:T(8,128)(2,1)} %stack_project.4.q.k.v, bf16[3,256,1024]{2,1,0:T(8,128)(2,1)} %stack_project.4.q.k.v, bf16[3,256,1024]{2,1,0:T(8,128)(2,1)} %stack_project.4.q.k.v, ...), custom_call_target="tpu_custom_call" | custom-call | tf_op jit(solution)/shard_map/self_attend_back/pallas_call | solution.py:228
  437.0 6.8 %stack_grads.7 = (bf16[4,512,1024]{2,1,0:T(8,128)(2,1)}, bf16[4,512,1024]{2,1,0:T(8,128)(2,1)}) custom-call(bf16[256,512]{1,0:T(8,128)(2,1)} %pad_maximum_fusion.27.x0.refs_0_, bf16[256,512]{1,0:T(8,128)(2,1)} %pad_maximum_fusion.28.x1.refs_1_, bf16[256,512]{1,0:T(8,128)(2,1)} %get-tuple-element.432.x0.refs_2_, ...), custom_call_target="tpu_custom_call" | custom-call | tf_op jit(solution)/shard_map/stack_grads/pallas_call | solution.py:289
  464.5 6.8 %back_natural.10 = f32[256,1024]{1,0:T(8,128)} custom-call(s32[8]{0:T(128)} %broadcast_xor_fusion.blocks, bf16[256,1024]{1,0:T(8,128)(2,1)} %get-tuple-element.355.refs_4_.refs_0_, bf16[256,1024]{1,0:T(8,128)(2,1)} %get-tuple-element.328.refs_5_.refs_1_, bf16[256,1024]{1,0:T(8,128)(2,1)} %get-tuple-element.356.refs_6_.refs_2_, ...), custom_call_target="tpu_custom_call" | custom-call | tf_op jit(solution)/shard_map/back_natural/pallas_call | solution.py:326
  487.8 15.2 %back_natural.11 = f32[2048,1024]{1,0:T(8,128)} custom-call(s32[8]{0:T(128)} %broadcast_xor_fusion.blocks, bf16[2048,1024]{1,0:T(8,128)(2,1)} %get-tuple-element.334.refs_7_.refs_0_, bf16[2048,1024]{1,0:T(8,128)(2,1)} %get-tuple-element.359.refs_8_.refs_1_, bf16[4,512,1024]{2,1,0:T(8,128)(2,1)} %copy-done, bf16[4,512,1024]{2,1,0:T(8,128)(2,1)} %copy-done.1, ...), custom_call_target="tpu_custom_call" | custom-call | tf_op jit(solution)/shard_map/back_natural/pallas_call | solution.py:326
  521.8 7.9 %collective-permute-done.58 = bf16[4,32,1024]{2,1,0:T(8,128)(2,1)S(1)} collective-permute-done((bf16[4,32,1024]{2,1,0:T(8,128)(2,1)S(1)}, bf16[4,32,1024]{2,1,0:T(8,128)(2,1)S(1)}, u32[]{:S(2)}, u32[]{:S(2)}) %collective-permute-start.58) | collective-permute-done | bytes 262176 | tf_op jit(solution)/shard_map/ppermute | solution.py:593
  545.2 6.8 %collective-permute-done.59 = bf16[4,2,32,1024]{3,2,0,1:T(8,128)(2,1)S(1)} collective-permute-done((bf16[4,2,32,1024]{3,2,0,1:T(8,128)(2,1)S(1)}, bf16[4,2,32,1024]{3,2,0,1:T(8,128)(2,1)S(1)}, u32[]{:S(2)}, u32[]{:S(2)}) %collective-permute-start.59) | collective-permute-done | bytes 524320 | tf_op jit(solution)/shard_map/ppermute | solution.py:593
  565.1 7.2 %collective-permute-done.60 = bf16[4,32,1024]{2,1,0:T(8,128)(2,1)S(1)} collective-permute-done((bf16[4,32,1024]{2,1,0:T(8,128)(2,1)S(1)}, bf16[4,32,1024]{2,1,0:T(8,128)(2,1)S(1)}, u32[]{:S(2)}, u32[]{:S(2)}) %collective-permute-start.60) | collective-permute-done | bytes 262176 | tf_op jit(solution)/shard_map/ppermute | solution.py:593
  (446 shorter events, 319.6 us)
Async XLA Ops:
  54.0 24.2 %collective-permute-start.12 = (bf16[2,2,128,1024]{3,2,1,0:T(8,128)(2,1)S(1)}, bf16[2,2,128,1024]{3,2,1,0:T(8,128)(2,1)S(1)}, u32[]{:S(2)}, u32[]{:S(2)}) collective-permute-start(bf16[2,2,128,1024]{3,2,1,0:T(8,128)(2,1)S(1)} %get-tuple-element.197), channel_id=1, source_target_pairs={{0,16},{1,17},{2,18},{3,19},{4,20},{5,21},{6,22},{7,23},{8,24},{9,... | collective-permute-start | bytes 3145736 | tf_op jit(solution)/shard_map/ppermute | solution.py:593
  54.5 24.1 %collective-permute-start.13 = (bf16[2,2,128,1024]{3,2,1,0:T(8,128)(2,1)S(1)}, bf16[2,2,128,1024]{3,2,1,0:T(8,128)(2,1)S(1)}, u32[]{:S(2)}, u32[]{:S(2)}) collective-permute-start(bf16[2,2,128,1024]{3,2,1,0:T(8,128)(2,1)S(1)} %get-tuple-element.198), channel_id=1, source_target_pairs={{0,8},{1,9},{2,10},{3,11},{4,12},{5,13},{6,14},{7,15},{8,0},{9,1},... | collective-permute-start | bytes 3145736 | tf_op jit(solution)/shard_map/ppermute | solution.py:593
  55.3 26.1 %collective-permute-start.7 = (bf16[4,2,32,1024]{3,2,1,0:T(8,128)(2,1)S(1)}, bf16[4,2,32,1024]{3,2,1,0:T(8,128)(2,1)S(1)}, u32[]{:S(2)}, u32[]{:S(2)}) collective-permute-start(bf16[4,2,32,1024]{3,2,1,0:T(8,128)(2,1)S(1)} %copy_bitcast_fusion), channel_id=1, source_target_pairs={{0,1},{1,0},{2,3},{3,2},{4,5},{5,4},{6,7},{7,6},{8,9},{9,8},{10,11... | collective-permute-start | bytes 1572872 | tf_op jit(solution)/shard_map/ppermute | solution.py:593
  81.4 25.9 %collective-permute-start.19 = (bf16[4,512,1024]{2,1,0:T(8,128)(2,1)}, bf16[4,512,1024]{2,1,0:T(8,128)(2,1)}, u32[]{:S(2)}, u32[]{:S(2)}) collective-permute-start(bf16[4,512,1024]{2,1,0:T(8,128)(2,1)} %pad_maximum_fusion.near.refs_1_.refs_3_.refs_5_.refs_7_), channel_id=1, source_target_pairs={{0,4},{1,5},{2,6},{3,7},{4,0},{5,1},{6,2},{7,3},{8,12},{9,13},{10,... | collective-permute-start | bytes 12582920 | tf_op jit(solution)/shard_map/ppermute | solution.py:593
  84.2 25.2 %collective-permute-start.11 = (bf16[16,8,128]{2,1,0:T(8,128)(2,1)S(1)}, bf16[16,8,128]{2,1,0:T(8,128)(2,1)S(1)}, u32[]{:S(2)}, u32[]{:S(2)}) collective-permute-start(bf16[16,8,128]{2,1,0:T(8,128)(2,1)S(1)} %pad_maximum_fusion.30), channel_id=1, source_target_pairs={{0,16},{1,17},{2,18},{3,19},{4,20},{5,21},{6,22},{7,23},{8,24},{9,... | collective-permute-start | bytes 98312 | tf_op jit(solution)/shard_map/ppermute | solution.py:593
  107.2 28.3 %collective-permute-start.20 = (bf16[2,2,128,1024]{3,2,1,0:T(8,128)(2,1)}, bf16[2,2,128,1024]{3,2,1,0:T(8,128)(2,1)}, u32[]{:S(2)}, u32[]{:S(2)}) collective-permute-start(bf16[2,2,128,1024]{3,2,1,0:T(8,128)(2,1)} %get-tuple-element.207), channel_id=1, source_target_pairs={{0,16},{1,17},{2,18},{3,19},{4,20},{5,21},{6,22},{7,23},{8,24},{9,... | collective-permute-start | bytes 3145736 | tf_op jit(solution)/shard_map/ppermute | solution.py:593
  107.9 27.6 %collective-permute-start.21 = (bf16[2,2,128,1024]{3,2,1,0:T(8,128)(2,1)}, bf16[2,2,128,1024]{3,2,1,0:T(8,128)(2,1)}, u32[]{:S(2)}, u32[]{:S(2)}) collective-permute-start(bf16[2,2,128,1024]{3,2,1,0:T(8,128)(2,1)} %get-tuple-element.208), channel_id=1, source_target_pairs={{0,8},{1,9},{2,10},{3,11},{4,12},{5,13},{6,14},{7,15},{8,0},{9,1},... | collective-permute-start | bytes 3145736 | tf_op jit(solution)/shard_map/ppermute | solution.py:593
  161.8 40.2 %collective-permute-start.25 = (bf16[2,1,128,2048]{3,2,1,0:T(8,128)(2,1)}, bf16[2,1,128,2048]{3,2,1,0:T(8,128)(2,1)}, u32[]{:S(2)}, u32[]{:S(2)}) collective-permute-start(bf16[2,1,128,2048]{3,2,1,0:T(8,128)(2,1)} %get-tuple-element.216), channel_id=1, source_target_pairs={{0,16},{1,17},{2,18},{3,19},{4,20},{5,21},{6,22},{7,23},{8,24},{9,... | collective-permute-start | bytes 3145736 | tf_op jit(solution)/shard_map/ppermute | solution.py:593
  162.4 39.6 %collective-permute-start.26 = (bf16[2,1,128,2048]{3,2,1,0:T(8,128)(2,1)}, bf16[2,1,128,2048]{3,2,1,0:T(8,128)(2,1)}, u32[]{:S(2)}, u32[]{:S(2)}) collective-permute-start(bf16[2,1,128,2048]{3,2,1,0:T(8,128)(2,1)} %get-tuple-element.217), channel_id=1, source_target_pairs={{0,8},{1,9},{2,10},{3,11},{4,12},{5,13},{6,14},{7,15},{8,0},{9,1},... | collective-permute-start | bytes 3145736 | tf_op jit(solution)/shard_map/ppermute | solution.py:593
  229.4 24.7 %collective-permute-start.30 = (bf16[2,1,512,512]{3,2,1,0:T(8,128)(2,1)}, bf16[2,1,512,512]{3,2,1,0:T(8,128)(2,1)}, u32[]{:S(2)}, u32[]{:S(2)}) collective-permute-start(bf16[2,1,512,512]{3,2,1,0:T(8,128)(2,1)} %get-tuple-element.238), channel_id=1, source_target_pairs={{0,16},{1,17},{2,18},{3,19},{4,20},{5,21},{6,22},{7,23},{8,24},{9,... | collective-permute-start | bytes 3145736 | tf_op jit(solution)/shard_map/ppermute | solution.py:593
  230.7 24.5 %collective-permute-start.31 = (bf16[2,1,512,512]{3,2,1,0:T(8,128)(2,1)}, bf16[2,1,512,512]{3,2,1,0:T(8,128)(2,1)}, u32[]{:S(2)}, u32[]{:S(2)}) collective-permute-start(bf16[2,1,512,512]{3,2,1,0:T(8,128)(2,1)} %get-tuple-element.239), channel_id=1, source_target_pairs={{0,8},{1,9},{2,10},{3,11},{4,12},{5,13},{6,14},{7,15},{8,0},{9,1},... | collective-permute-start | bytes 3145736 | tf_op jit(solution)/shard_map/ppermute | solution.py:593
  299.4 25.7 %collective-permute-start.34 = (bf16[1,2,512,512]{3,2,1,0:T(8,128)(2,1)}, bf16[1,2,512,512]{3,2,1,0:T(8,128)(2,1)S(1)}, u32[]{:S(2)}, u32[]{:S(2)}) collective-permute-start(bf16[1,2,512,512]{3,2,1,0:T(8,128)(2,1)} %get-tuple-element.254), channel_id=1, source_target_pairs={{0,16},{1,17},{2,18},{3,19},{4,20},{5,21},{6,22},{7,23},{8,24},{9,... | collective-permute-start | bytes 3145736 | tf_op jit(solution)/shard_map/ppermute | solution.py:593
  300.2 25.4 %collective-permute-start.35 = (bf16[1,2,512,512]{3,2,1,0:T(8,128)(2,1)}, bf16[1,2,512,512]{3,2,1,0:T(8,128)(2,1)S(1)}, u32[]{:S(2)}, u32[]{:S(2)}) collective-permute-start(bf16[1,2,512,512]{3,2,1,0:T(8,128)(2,1)} %get-tuple-element.255), channel_id=1, source_target_pairs={{0,8},{1,9},{2,10},{3,11},{4,12},{5,13},{6,14},{7,15},{8,0},{9,1},... | collective-permute-start | bytes 3145736 | tf_op jit(solution)/shard_map/ppermute | solution.py:593
  325.6 26.7 %collective-permute-start.36 = (bf16[2,512,2048]{2,1,0:T(8,128)(2,1)}, bf16[2,512,2048]{2,1,0:T(8,128)(2,1)}, u32[]{:S(2)}, u32[]{:S(2)}) collective-permute-start(bf16[2,512,2048]{2,1,0:T(8,128)(2,1)} %get-tuple-element.262), channel_id=1, source_target_pairs={{0,4},{1,5},{2,6},{3,7},{4,0},{5,1},{6,2},{7,3},{8,12},{9,13},{10,... | collective-permute-start | bytes 12582920 | tf_op jit(solution)/shard_map/ppermute | solution.py:593
  330.2 22.1 %collective-permute-start.37 = (bf16[1,1,512,512]{3,2,1,0:T(8,128)(2,1)}, bf16[1,1,512,512]{3,2,1,0:T(8,128)(2,1)S(1)}, u32[]{:S(2)}, u32[]{:S(2)}) collective-permute-start(bf16[1,1,512,512]{3,2,1,0:T(8,128)(2,1)} %get-tuple-element.271), channel_id=1, source_target_pairs={{0,8},{1,9},{2,10},{3,11},{4,12},{5,13},{6,14},{7,15},{8,0},{9,1},... | collective-permute-start | bytes 1572872 | tf_op jit(solution)/shard_map/ppermute | solution.py:593
  357.6 37.4 %collective-permute-start.39 = (bf16[1,2,128,2048]{3,2,1,0:T(8,128)(2,1)}, bf16[1,2,128,2048]{3,2,1,0:T(8,128)(2,1)S(1)}, u32[]{:S(2)}, u32[]{:S(2)}) collective-permute-start(bf16[1,2,128,2048]{3,2,1,0:T(8,128)(2,1)} %get-tuple-element.280), channel_id=1, source_target_pairs={{0,16},{1,17},{2,18},{3,19},{4,20},{5,21},{6,22},{7,23},{8,24},{9,... | collective-permute-start | bytes 3145736 | tf_op jit(solution)/shard_map/ppermute | solution.py:593
  358.3 36.7 %collective-permute-start.40 = (bf16[1,2,128,2048]{3,2,1,0:T(8,128)(2,1)}, bf16[1,2,128,2048]{3,2,1,0:T(8,128)(2,1)}, u32[]{:S(2)}, u32[]{:S(2)}) collective-permute-start(bf16[1,2,128,2048]{3,2,1,0:T(8,128)(2,1)} %get-tuple-element.281), channel_id=1, source_target_pairs={{0,8},{1,9},{2,10},{3,11},{4,12},{5,13},{6,14},{7,15},{8,0},{9,1},... | collective-permute-start | bytes 3145736 | tf_op jit(solution)/shard_map/ppermute | solution.py:593
  361.0 34.1 %collective-permute-start.41 = (bf16[2,2,128,512]{3,2,0,1:T(8,128)(2,1)}, bf16[2,2,128,512]{3,2,0,1:T(8,128)(2,1)}, u32[]{:S(2)}, u32[]{:S(2)}) collective-permute-start(bf16[2,2,128,512]{3,2,0,1:T(8,128)(2,1)} %fusion.1), channel_id=1, source_target_pairs={{0,1},{1,0},{2,3},{3,2},{4,5},{5,4},{6,7},{7,6},{8,9},{9,8},{10,11... | collective-permute-start | bytes 1572872 | tf_op jit(solution)/shard_map/ppermute | solution.py:593
  395.1 23.7 %collective-permute-start.42 = (bf16[4,512,1024]{2,1,0:T(8,128)(2,1)}, bf16[4,512,1024]{2,1,0:T(8,128)(2,1)}, u32[]{:S(2)}, u32[]{:S(2)}) collective-permute-start(bf16[4,512,1024]{2,1,0:T(8,128)(2,1)} %get-tuple-element.295), channel_id=1, source_target_pairs={{0,4},{1,5},{2,6},{3,7},{4,0},{5,1},{6,2},{7,3},{8,12},{9,13},{10,... | collective-permute-start | bytes 12582920 | tf_op jit(solution)/shard_map/ppermute | solution.py:593
  425.0 24.3 %collective-permute-start.46 = (bf16[2,2,128,1024]{3,2,1,0:T(8,128)(2,1)}, bf16[2,2,128,1024]{3,2,1,0:T(8,128)(2,1)S(1)}, u32[]{:S(2)}, u32[]{:S(2)}) collective-permute-start(bf16[2,2,128,1024]{3,2,1,0:T(8,128)(2,1)} %get-tuple-element.310), channel_id=1, source_target_pairs={{0,16},{1,17},{2,18},{3,19},{4,20},{5,21},{6,22},{7,23},{8,24},{9,... | collective-permute-start | bytes 3145736 | tf_op jit(solution)/shard_map/ppermute | solution.py:593
  425.8 24.0 %collective-permute-start.47 = (bf16[2,2,128,1024]{3,2,1,0:T(8,128)(2,1)}, bf16[2,2,128,1024]{3,2,1,0:T(8,128)(2,1)}, u32[]{:S(2)}, u32[]{:S(2)}) collective-permute-start(bf16[2,2,128,1024]{3,2,1,0:T(8,128)(2,1)} %get-tuple-element.311), channel_id=1, source_target_pairs={{0,8},{1,9},{2,10},{3,11},{4,12},{5,13},{6,14},{7,15},{8,0},{9,1},... | collective-permute-start | bytes 3145736 | tf_op jit(solution)/shard_map/ppermute | solution.py:593
  449.8 27.7 %collective-permute-start.51 = (bf16[4,512,1024]{2,1,0:T(8,128)(2,1)}, bf16[4,512,1024]{2,1,0:T(8,128)(2,1)}, u32[]{:S(2)}, u32[]{:S(2)}) collective-permute-start(bf16[4,512,1024]{2,1,0:T(8,128)(2,1)} %get-tuple-element.330), channel_id=1, source_target_pairs={{0,4},{1,5},{2,6},{3,7},{4,0},{5,1},{6,2},{7,3},{8,12},{9,13},{10,... | collective-permute-start | bytes 12582920 | tf_op jit(solution)/shard_map/ppermute | solution.py:593
  485.7 24.4 %collective-permute-start.53 = (bf16[2,2,128,1024]{3,2,1,0:T(8,128)(2,1)}, bf16[2,2,128,1024]{3,2,1,0:T(8,128)(2,1)S(1)}, u32[]{:S(2)}, u32[]{:S(2)}) collective-permute-start(bf16[2,2,128,1024]{3,2,1,0:T(8,128)(2,1)} %get-tuple-element.340), channel_id=1, source_target_pairs={{0,16},{1,17},{2,18},{3,19},{4,20},{5,21},{6,22},{7,23},{8,24},{9,... | collective-permute-start | bytes 3145736 | tf_op jit(solution)/shard_map/ppermute | solution.py:593
  486.4 24.2 %collective-permute-start.54 = (bf16[2,2,128,1024]{3,2,1,0:T(8,128)(2,1)}, bf16[2,2,128,1024]{3,2,1,0:T(8,128)(2,1)}, u32[]{:S(2)}, u32[]{:S(2)}) collective-permute-start(bf16[2,2,128,1024]{3,2,1,0:T(8,128)(2,1)} %get-tuple-element.341), channel_id=1, source_target_pairs={{0,8},{1,9},{2,10},{3,11},{4,12},{5,13},{6,14},{7,15},{8,0},{9,1},... | collective-permute-start | bytes 3145736 | tf_op jit(solution)/shard_map/ppermute | solution.py:593
  (106 other events, 824.1 us)

commit v5 on v4

--- a/solution.py
+++ b/solution.py
@@ -238,6 +238,10 @@
     )(place, qkv, qkv, qkv, lse, d_out)
 
 
+def row_of(row):
+    return pl.BlockSpec((None, 1, row[0].shape[2]), lambda *_: (row[1], 0, 0))
+
+
 def stacked(array, i, **kw):
     return pl.BlockSpec((None,) + array.shape[1:], lambda *_: (i, 0, 0), **kw)
 
@@ -253,6 +257,7 @@
 
 def stack_project(rows, weights, first, bias, scales, dtype):
     near, far = weights
+    bias, start = bias
     m, h = rows[0].shape
     n = near.shape[2]
     count = len(scales)
@@ -261,7 +266,7 @@
     return pl.pallas_call(
         functools.partial(project_kernel, scales),
         grid=(count,),
-        in_specs=[whole, whole, weight, weight, pl.BlockSpec((None, 1, n), lambda j: (j, 0, 0))],
+        in_specs=[whole, whole, weight, weight, pl.BlockSpec((None, 1, n), lambda j: (start + j, 0, 0))],
         out_specs=pl.BlockSpec((None, m, n), lambda j: (j, 0, 0)),
         out_shape=jax.ShapeDtypeStruct((count, m, n), dtype),
         name="stack_project",
@@ -358,13 +363,12 @@
     rows = m // 2
     full = pl.BlockSpec((rows, n), lambda i, *_: (i, 0))
     halves = pl.BlockSpec((rows, n // 2), lambda i, *_: (i, 0))
-    row = pl.BlockSpec((1, n), lambda i, *_: (0, 0))
     pre, out, rel0, rel1 = pl.pallas_call(
         norm_kernel,
         grid_spec=pltpu.PrefetchScalarGridSpec(
             num_scalar_prefetch=1,
             grid=(2,),
-            in_specs=[full, full, row, row],
+            in_specs=[full, full, row_of(gain), row_of(shift)],
             out_specs=[full, full, halves, halves],
         ),
         out_shape=[
@@ -374,7 +378,7 @@
             jax.ShapeDtypeStruct((m, n // 2), BF),
         ],
         name="norm",
-    )(blocks, branch, residual, gain, shift)
+    )(blocks, branch, residual, gain[0], shift[0])
     return pre, out, (rel0, rel1)
 
 
@@ -410,8 +414,7 @@
     m, n = pre.shape
     rows = m // 2
     full = pl.BlockSpec((rows, n), lambda i: (i, 0))
-    row = pl.BlockSpec((1, n), lambda i: (0, 0))
-    extra = [] if shift is None else [shift]
+    extra = [gain] if shift is None else [gain, shift]
     out_specs = [full, full, pl.BlockSpec((8, n), lambda i: (0, 0))]
     out_shape = [
         jax.ShapeDtypeStruct((m, n), F32),
@@ -423,11 +426,11 @@
     return pl.pallas_call(
         functools.partial(norm_back_kernel, len(cotangents)),
         grid=(2,),
-        in_specs=[full] * (len(cotangents) + 1) + [row] * (1 + len(extra)),
+        in_specs=[full] * (len(cotangents) + 1) + [row_of(row) for row in extra],
         out_specs=out_specs,
         out_shape=out_shape,
         name="norm_back",
-    )(*cotangents, pre, gain, *extra)
+    )(*cotangents, pre, *[row[0] for row in extra])
 
 
 def gelu_parts(u):
@@ -518,11 +521,11 @@
         in_specs=[pl.BlockSpec((block, h), lambda i: (i, 0))] * 2
         + [stacked(near, key_pick, pipeline_mode=once)] * 2
         + [stacked(near, value_pick, pipeline_mode=once)] * 2
-        + [pl.BlockSpec((1, n), lambda i: (0, 0))],
+        + [row_of(bias)],
         out_specs=[pl.BlockSpec((block, n), lambda i: (i, 0))] * 2,
         out_shape=[jax.ShapeDtypeStruct((m, n), BF)] * 2,
         name="memory_project",
-    )(*rows, near, far, near, far, bias)
+    )(*rows, near, far, near, far, bias[0])
 
 
 def add_split_kernel(*refs):
@@ -681,21 +684,24 @@
         for mask in self.zs:
             axis = len(acc.shape) - 3
             place = self.bit(self.z, mask)
+            if mask != self.zs[0]:
+                acc = acc + got.astype(F32)
             send = lax.dynamic_index_in_dim(acc, 1 - place, axis, keepdims=False).astype(BF)
             acc = lax.dynamic_index_in_dim(acc, place, axis, keepdims=False)
             (got,) = yield [(send, mask)]
-            acc = acc + got.astype(F32)
-        return acc
+        return acc, got
 
     def gather_small(self, vector):
         n = vector.shape[0]
-        have = vector.reshape(1, n // 128, 128)
-        for mask in [1 << b for b in range(self.count.bit_length() - 1)]:
+        have = vector.reshape(n // 128, 128)
+        masks = [*self.across, self.core, *reversed(self.zs)]
+        for mask in masks:
             (other,) = yield [(have, mask)]
             low = self.bit(self.me, mask) == 0
-            have = jnp.concatenate(
-                [jnp.where(low, have, other), jnp.where(low, other, have)], axis=0
-            )
+            have = jnp.stack([jnp.where(low, have, other), jnp.where(low, other, have)])
+        count = len(masks)
+        axes = [list(reversed(masks)).index(mask) for mask in sorted(masks, reverse=True)]
+        have = jnp.transpose(have, [*axes, count, count + 1])
         return have.reshape(self.count, n)
 
     def scatter_small(self, table):
@@ -789,9 +795,9 @@
 
     def add_norm(branch, residual, gain, shift):
         if (model_width // plan.wide) % 128 == 0:
-            return norm(branch, residual, gain[None], shift[None], plan.blocks())
+            return norm(branch, residual, gain, shift, plan.blocks())
         pre = residual.astype(F32) + branch
-        out = layer_norm(pre, gain, shift)
+        out = layer_norm(pre, gain[0][gain[1], 0], shift[0][shift[1], 0])
         return pre, out, plan.relative(out.astype(BF))
 
 
@@ -828,61 +834,55 @@
     )
     fins = Stream(plan.gather(ffn_in[None], columns, one))
     fouts = Stream(plan.gather(ffn_out[None], columns, one))
-    after = plan.step(small)
-    for _ in plan.zs:
-        after = (plan.step(selfs, after), plan.step(small))
-    after = (after, plan.step(small))
+    x_rel = plan.relative(inputs)
+    mem_rel = plan.relative(memory.reshape(item_count * mem_slots, model_width))
+    after = plan.step(selfs)
+    small_last = plan.step(small, after)
+    for _ in plan.across:
+        small_last = plan.step(small)
+    for _ in plan.zs[1:]:
+        after = plan.step(selfs, after)
     for _ in plan.across[2:]:
         after = plan.step(selfs, after)
-    last = plan.step(selfs, after)
+    last, (x_rel, _) = plan.step(selfs, after, (x_rel, small_last))
     plan.finish(small)
     cross_z = plan.step(crosses, after)
-    last = plan.step(selfs, (last, cross_z, small.result))
+    last, (mem_rel, small_sum) = plan.step(selfs, (last, cross_z), (mem_rel, small.result))
+    table = small_sum.astype(F32)
+    vectors = table[:, : vector_count * share].reshape(plan.count, vector_count, share)
+    vectors = jnp.swapaxes(vectors, 0, 1).reshape(vector_count, 1, model_width)
+    first_bias = jnp.stack([vectors[0], jnp.zeros_like(vectors[0]), vectors[1]])
+    fbin = table[:, vector_count * share :][:, :hidden_share].reshape(-1)
     for _ in plan.zs[1:]:
         cross_z = plan.step(crosses, cross_z)
     self_core = plan.step(selfs, cross_z)
     fin_z = plan.step(fins, cross_z)
     last, fin_z = plan.step(crosses, last, fin_z)
-    table = small.result.astype(F32)
-    vectors = table[:, : vector_count * share].reshape(plan.count, vector_count, share)
-    vectors = jnp.swapaxes(vectors, 0, 1).reshape(vector_count, model_width)
-    sbias, sgain, cbias, cgain, fbout, fgain = (
-        vectors[:4],
-        vectors[4],
-        vectors[5:9],
-        vectors[9],
-        vectors[10:12],
-        vectors[12],
-    )
-    fbin = table[:, vector_count * share :][:, :hidden_share].reshape(-1)
-
-    x_rel = plan.relative(inputs)
-    no_bias = jnp.zeros((model_width,), F32)
+
     qkv = stack_project(
         x_rel,
         selfs.result,
         0,
-        jnp.stack([sbias[0], no_bias, sbias[1]])[:, None],
+        (first_bias, 0),
         (scaling, 1.0, 1.0),
         BF,
     )
     self_ctx, self_lse = self_attend(qkv, item_count, place)
     self_rel = to_relative(self_ctx)
-    branch = stack_project(self_rel, selfs.result, 3, sbias[None, 2:3], (1.0,), F32)[0]
+    branch = stack_project(self_rel, selfs.result, 3, (vectors, 2), (1.0,), F32)[0]
     after = (last, self_core, fin_z)
     for _ in plan.zs[1:]:
         fin_z = plan.step(fins, fin_z)
-    fout_z = plan.step(fouts, fin_z)
+    fout_z = plan.step(fouts, (fin_z, self_ctx))
     last, (branch, fout_z) = plan.across_steps(crosses, after, (branch, fout_z))
-    first_pre, first, first_rel = add_norm(branch, inputs, sgain, sbias[3])
+    first_pre, first, first_rel = add_norm(branch, inputs, (vectors, 4), (vectors, 3))
     cross_core = plan.step(crosses)
     for _ in plan.zs[1:]:
         fout_z = plan.step(fouts, fout_z)
     last, _ = plan.step(fins, last, (cross_core, fout_z))
 
-    queries_two = stack_project(first_rel, crosses.result, 0, cbias[None, 0:1], (scaling,), BF)[0]
-    mem_rel = plan.relative(memory.reshape(item_count * mem_slots, model_width))
-    mem_keys, mem_values = memory_project(mem_rel, crosses.result, 1, 2, cbias[1:2], 512)
+    queries_two = stack_project(first_rel, crosses.result, 0, (vectors, 5), (scaling,), BF)[0]
+    mem_keys, mem_values = memory_project(mem_rel, crosses.result, 1, 2, (vectors, 6), 512)
     cross_out = ()
     for item in range(item_count):
         cross_out = cross_attend(
@@ -895,8 +895,8 @@
     cross_ctx, cross_lse = cross_out
     fin = fins.result
     cross_rel = to_relative(cross_ctx)
-    branch = stack_project(cross_rel, crosses.result, 3, cbias[None, 2:3], (1.0,), F32)[0]
-    second_pre, second, second_rel = add_norm(branch, first, cgain, cbias[3])
+    branch = stack_project(cross_rel, crosses.result, 3, (vectors, 7), (1.0,), F32)[0]
+    second_pre, second, second_rel = add_norm(branch, first, (vectors, 9), (vectors, 8))
 
     places = plan.places()
     hidden, slope = ffn_up(second_rel, fin, fbin[None], places)
@@ -905,10 +905,10 @@
     hidden_rel = (hidden[:, :half], hidden[:, half:])
     plan.step(fouts)
     fout = fouts.result
-    third_pre = second + (forward(hidden_rel, fout) + fbout[0])
+    third_pre = second + (forward(hidden_rel, fout) + vectors[10, 0])
 
     layer_out, d_third, e_three, third_sums = norm_back(
-        [out_grad], third_pre, fgain[None], fbout[1:2]
+        [out_grad], third_pre, (vectors, 12), (vectors, 11)
     )
     half = model_width // 2
     to_fout = Stream(
@@ -923,7 +923,7 @@
     to_fin.replace(fin_sends)
     fin_core = plan.step(to_fin)
 
-    d_second_pre, e_two, second_sums = norm_back([d_third, d_hidden], second_pre, cgain[None])
+    d_second_pre, e_two, second_sums = norm_back([d_third, d_hidden], second_pre, (vectors, 9))
     d_cross_ctx = context_back(e_two, crosses.result)
     cross_back = ()
     for item in range(item_count):
@@ -951,7 +951,7 @@
     cross_core = plan.step(to_cross)
     fout_last = plan.step(to_fout)
 
-    d_first_pre, e_one, first_sums = norm_back([d_second_pre, d_queries], first_pre, sgain[None])
+    d_first_pre, e_one, first_sums = norm_back([d_second_pre, d_queries], first_pre, (vectors, 4))
     d_self_ctx = context_back(e_one, selfs.result)
     last, (d_self_ctx, *_) = plan.across_steps(
         to_fin, last, (d_self_ctx, cross_core, fout_last)
@@ -1017,9 +1017,13 @@
     small_sums = to_small.result
     found = small_sums[: vector_count * share].reshape(vector_count, share)
     g_hidden = small_sums[vector_count * share :][:hidden_share]
-    g_self, g_cross = to_self.result, to_cross.result
-    g_fout = jnp.concatenate([to_fout.result[0], to_fout.result[1]], axis=1)
-    g_fin = jnp.concatenate([to_fin.result[0], to_fin.result[1]], axis=1)
+    early = [stream.result for stream in (to_cross, to_fin, to_fout)]
+    early, _ = lax.optimization_barrier((early, last))
+    g_self, g_cross, g_fin, g_fout = [
+        keep + got.astype(F32) for keep, got in (to_self.result, *early)
+    ]
+    g_fout = jnp.concatenate([g_fout[0], g_fout[1]], axis=1)
+    g_fin = jnp.concatenate([g_fin[0], g_fin[1]], axis=1)
     return (
         layer_out,
         input_grad,

time: 582 us -> 580 us (level)
  Pallas kernels: 243 us -> 253 us
    pallas_call x3, Pallas kernels: 9.72 us -> 20.6 us  [norm_back(): pl.pallas_call(functools.partial(norm_back_kernel, len(cotangents)), grid...]
    unnamed x129 -> x144, local copies, waits for them, and re-layouts: 8.78 us -> 17.7 us
    slice x10 -> x3, local copies, waits for them, and re-layouts: 7.93 us -> 0.3 us  [the longest x2 0.16 us: local(): first_bias = jnp.stack([vectors[0], jnp.zeros_like(vectors[0]), vectors[1]])]
    another operation x9 -> x10, other arithmetic: 10.6 us -> 12.9 us  [gather(): sets = [jnp.stack([s, g]) for s, g in zip(sets, got)]]
  transfers between devices with their start and end apart: 66 -> 66, of which waited for: 32 -> 35; matrix products, arithmetic and copies ran while one was open for 11% -> 10% of each run, Pallas kernels for 36% -> 36%
where the time goes in v5:
time: 580 us; the launch traced here: 574 us
  Pallas kernels  253 us (44%)
  waiting for transfers between devices  149 us (26%)
  starting transfers between devices  60.6 us (10%)
  local copies, waits for them, and re-layouts  52.7 us (9%)
  other arithmetic  51.9 us (9%)
    ppermute x66, waiting for transfers between devices, step(): lax.ppermute(v, AXES, [(i, i ^ m) for i in range(self.count)])  149 us
    ppermute x66, starting transfers between devices, step(): lax.ppermute(v, AXES, [(i, i ^ m) for i in range(self.count)])  60.6 us
    pallas_call x4, Pallas kernels, cross_call(): pl.pallas_call(kernel, grid_spec=pltpu.PrefetchScalarGridSpec(num_scalar_...  47.1 us
    pallas_call x6, Pallas kernels, back_natural(): pl.pallas_call(back_kernel, grid_spec=pltpu.PrefetchScalarGridSpec(num_sc...  42.4 us
    pallas_call x4, Pallas kernels, stack_grads(): pl.pallas_call(functools.partial(grads_kernel, table), grid=(len(products...  37.2 us
    pallas_call x8, Pallas kernels, add_split(): pl.pallas_call(add_split_kernel, grid=shapes[0].shape[:2], in_specs=in_sp...  36.2 us
    pallas_call x3, Pallas kernels, norm_back(): pl.pallas_call(functools.partial(norm_back_kernel, len(cotangents)), grid...  20.6 us
    unnamed x144, local copies, waits for them, and re-layouts  17.7 us
  transfers between devices with their start and end apart: 66, of which 35 were waited for; matrix products, arithmetic and copies ran while one was open for 10% of the time, Pallas kernels for 36%

profile of v5, /device:TPU:0, one launch (start us, length us, event | category | flops | bytes accessed | tf_op | source)
XLA Modules:
  0.0 574.4 jit_solution(5777680563006627617)
XLA Ops:
  26.2 8.2 %collective-permute-done.1 = bf16[4,2,32,1024]{3,2,1,0:T(8,128)(2,1)S(1)} collective-permute-done((bf16[4,2,32,1024]{3,2,1,0:T(8,128)(2,1)S(1)}, bf16[4,2,32,1024]{3,2,1,0:T(8,128)(2,1)S(1)}, u32[]{:S(2)}, u32[]{:S(2)}) %collective-permute-start.1) | collective-permute-done | bytes 524320 | tf_op jit(solution)/shard_map/ppermute | solution.py:596
  61.1 17.4 %collective-permute-done.10 = bf16[2,2,128,1024]{3,2,1,0:T(8,128)(2,1)} collective-permute-done((bf16[2,2,128,1024]{3,2,1,0:T(8,128)(2,1)}, bf16[2,2,128,1024]{3,2,1,0:T(8,128)(2,1)}, u32[]{:S(2)}, u32[]{:S(2)}) %collective-permute-start.10) | collective-permute-done | bytes 1048608 | tf_op jit(solution)/shard_map/ppermute | solution.py:596
  87.4 10.1 %collective-permute-done.4 = bf16[1,1,32,4096]{3,2,1,0:T(8,128)(2,1)S(1)} collective-permute-done((bf16[1,1,32,4096]{3,2,1,0:T(8,128)(2,1)S(1)}, bf16[1,1,32,4096]{3,2,1,0:T(8,128)(2,1)S(1)}, u32[]{:S(2)}, u32[]{:S(2)}) %collective-permute-start.4) | collective-permute-done | bytes 262176 | tf_op jit(solution)/shard_map/ppermute | solution.py:596
  127.9 6.4 %collective-permute-done.18 = bf16[1,1,128,1024]{3,2,1,0:T(8,128)(2,1)} collective-permute-done((bf16[1,1,128,1024]{3,2,1,0:T(8,128)(2,1)}, bf16[1,1,128,1024]{3,2,1,0:T(8,128)(2,1)}, u32[]{:S(2)}, u32[]{:S(2)}) %collective-permute-start.18) | collective-permute-done | bytes 262176 | tf_op jit(solution)/shard_map/ppermute | solution.py:596
  143.8 11.9 %collective-permute-done.19 = bf16[1,2,128,1024]{3,2,1,0:T(8,128)(2,1)S(1)} collective-permute-done((bf16[1,2,128,1024]{3,2,1,0:T(8,128)(2,1)S(1)}, bf16[1,2,128,1024]{3,2,1,0:T(8,128)(2,1)S(1)}, u32[]{:S(2)}, u32[]{:S(2)}) %collective-permute-start.19) | collective-permute-done | bytes 524320 | tf_op jit(solution)/shard_map/ppermute | solution.py:596
  170.1 13.2 %memory_project.1 = (bf16[2048,1024]{1,0:T(8,128)(2,1)}, bf16[2048,1024]{1,0:T(8,128)(2,1)}) custom-call(bf16[2048,512]{1,0:T(8,128)(2,1)} %get-tuple-element.243.x0.refs_2_, bf16[2048,512]{1,0:T(8,128)(2,1)} %get-tuple-element.244.x1.refs_3_, bf16[4,512,1024]{2,1,0:T(8,128)(2,1)} %copy-done, bf16[4,512,1024]{2,1,0:T(8,128)(2,1)} %copy-done.1, ...), custom_call_target="tpu_custom_call" | custom-call | tf_op jit(solution)/shard_map/memory_project/pallas_call | solution.py:518
  183.3 11.4 %cross_attend.4 = (bf16[256,1024]{1,0:T(8,128)(2,1)}, f32[2,8,1,256]{3,2,1,0:T(1,128)}) custom-call(s32[8]{0:T(128)} %fusion.17.place.places, s32[1]{0:T(128)} %get-tuple-element.483.length, bf16[256,1024]{1,0:T(8,128)(2,1)} %bitcast.285, bf16[2048,1024]{1,0:T(8,128)(2,1)} %get-tuple-element.245.k, bf16[2048,1024]{1,0:T(8,128)(2,1)} %get-tuple-element.246.v), custom_call_target="tpu_custom_call" | custom-call | tf_op jit(solution)/shard_map/cross_attend/pallas_call | solution.py:128
  205.6 11.4 %cross_attend.5 = (bf16[256,1024]{1,0:T(8,128)(2,1)}, f32[2,8,1,256]{3,2,1,0:T(1,128)}) custom-call(s32[8]{0:T(128)} %fusion.17.place.places, s32[1]{0:T(128)} %get-tuple-element.482.length, bf16[256,1024]{1,0:T(8,128)(2,1)} %bitcast.286, bf16[2048,1024]{1,0:T(8,128)(2,1)} %get-tuple-element.245.k, ...), custom_call_target="tpu_custom_call", output_to_operand_aliasing={{0}: (5, {}), {1}: (6, {})} | custom-call | tf_op jit(solution)/shard_map/cross_attend/pallas_call | solution.py:128
  231.0 10.9 %ffn_up.1 = (bf16[256,4096]{1,0:T(8,128)(2,1)}, f32[256,4096]{1,0:T(8,128)}) custom-call(s32[8]{0:T(128)} %fusion.17.place.places, bf16[256,512]{1,0:T(8,128)(2,1)} %get-tuple-element.264.x0.refs_0_, bf16[256,512]{1,0:T(8,128)(2,1)} %get-tuple-element.265.x1.refs_1_, bf16[512,4096]{1,0:T(8,128)(2,1)} %get-tuple-element.398.near, ...), custom_call_target="tpu_custom_call" | custom-call | tf_op jit(solution)/shard_map/ffn_up/pallas_call | solution.py:454
  265.3 14.2 %norm_back.3 = (bf16[256,1024]{1,0:T(8,128)(2,1)}, f32[256,1024]{1,0:T(8,128)}, bf16[256,1024]{1,0:T(8,128)(2,1)}, f32[8,1024]{1,0:T(8,128)}) custom-call(bf16[256,1024]{1,0:T(8,128)(2,1)} %refs_0_.1, f32[256,1024]{1,0:T(8,128)} %add.267.refs_1_, f32[13,1,1024]{2,1,0:T(1,128)} %reshape.193.bias.gain.shift.refs_2_.refs_3_, ...), custom_call_target="tpu_custom_call" | custom-call | tf_op jit(solution)/shard_map/norm_back/pallas_call | solution.py:426
  285.9 10.5 %ffn_down_back.1.refs_0_.refs_2_ = bf16[256,4096]{1,0:T(8,128)(2,1)} custom-call(s32[8]{0:T(128)} %broadcast_xor_fusion.blocks, bf16[256,1024]{1,0:T(8,128)(2,1)} %get-tuple-element.273.refs_2_.cotangent, bf16[2048,1024]{1,0:T(8,128)(2,1)} %pad_maximum_fusion.3.near, bf16[2048,1024]{1,0:T(8,128)(2,1)} %collective-permute-done.32.far, ...), custom_call_target="tpu_custom_call" | custom-call | tf_op jit(solution)/shard_map/ffn_down_back/pallas_call | solution.py:489
  309.9 8.2 %back_natural.6.refs_1_ = f32[256,1024]{1,0:T(8,128)} custom-call(s32[8]{0:T(128)} %broadcast_xor_fusion.blocks, bf16[256,4096]{1,0:T(8,128)(2,1)} %ffn_down_back.1.refs_0_.refs_2_, bf16[1,512,4096]{2,1,0:T(8,128)(2,1)} %get-tuple-element.397.refs_1_, bf16[1,512,4096]{2,1,0:T(8,128)(2,1)} %bitcast.110.refs_2_), custom_call_target="tpu_custom_call" | custom-call | tf_op jit(solution)/shard_map/back_natural/pallas_call | solution.py:331
  318.0 9.2 %collective-permute-done.34.refs_1_.refs_3_ = bf16[1,2,512,512]{3,2,1,0:T(8,128)(2,1)S(1)} collective-permute-done((bf16[1,2,512,512]{3,2,1,0:T(8,128)(2,1)}, bf16[1,2,512,512]{3,2,1,0:T(8,128)(2,1)S(1)}, u32[]{:S(2)}, u32[]{:S(2)}) %collective-permute-start.34) | collective-permute-done | bytes 1048608 | tf_op jit(solution)/shard_map/ppermute | solution.py:596
  342.1 12.2 %cross_attend.6 = (bf16[256,1024]{1,0:T(8,128)(2,1)}, bf16[2048,1024]{1,0:T(8,128)(2,1)}, bf16[2048,1024]{1,0:T(8,128)(2,1)}) custom-call(s32[8]{0:T(128)} %fusion.17.place.places, s32[1]{0:T(128)} %get-tuple-element.483.length, bf16[256,1024]{1,0:T(8,128)(2,1)} %bitcast.287, bf16[2048,1024]{1,0:T(8,128)(2,1)} %get-tuple-element.245.k, ...), custom_call_target="tpu_custom_call" | custom-call | tf_op jit(solution)/shard_map/cross_attend/pallas_call | solution.py:128
  365.1 12.2 %cross_attend.7 = (bf16[256,1024]{1,0:T(8,128)(2,1)}, bf16[2048,1024]{1,0:T(8,128)(2,1)}, bf16[2048,1024]{1,0:T(8,128)(2,1)}) custom-call(s32[8]{0:T(128)} %fusion.17.place.places, s32[1]{0:T(128)} %get-tuple-element.482.length, bf16[256,1024]{1,0:T(8,128)(2,1)} %bitcast.288, ...), custom_call_target="tpu_custom_call", output_to_operand_aliasing={{0}: (7, {}), {1}: (8, {}), {2}: (9, {})} | custom-call | tf_op jit(solution)/shard_map/cross_attend/pallas_call | solution.py:128
  377.3 17.7 %stack_grads.6 = (bf16[4,512,1024]{2,1,0:T(8,128)(2,1)}, bf16[4,512,1024]{2,1,0:T(8,128)(2,1)}) custom-call(bf16[256,512]{1,0:T(8,128)(2,1)} %get-tuple-element.241.x0.refs_0_, bf16[256,512]{1,0:T(8,128)(2,1)} %get-tuple-element.242.x1.refs_1_, bf16[2048,512]{1,0:T(8,128)(2,1)} %get-tuple-element.243.x0.refs_2_, ...), custom_call_target="tpu_custom_call" | custom-call | tf_op jit(solution)/shard_map/stack_grads/pallas_call | solution.py:294
  431.8 7.9 %self_attend_back.1 = (bf16[256,1024]{1,0:T(8,128)(2,1)}, bf16[256,1024]{1,0:T(8,128)(2,1)}, bf16[256,1024]{1,0:T(8,128)(2,1)}) custom-call(s32[8]{0:T(128)} %fusion.17.place.places, bf16[3,256,1024]{2,1,0:T(8,128)(2,1)} %stack_project.4.q.k.v, bf16[3,256,1024]{2,1,0:T(8,128)(2,1)} %stack_project.4.q.k.v, bf16[3,256,1024]{2,1,0:T(8,128)(2,1)} %stack_project.4.q.k.v, ...), custom_call_target="tpu_custom_call" | custom-call | tf_op jit(solution)/shard_map/self_attend_back/pallas_call | solution.py:228
  439.6 6.8 %stack_grads.7 = (bf16[4,512,1024]{2,1,0:T(8,128)(2,1)}, bf16[4,512,1024]{2,1,0:T(8,128)(2,1)}) custom-call(bf16[256,512]{1,0:T(8,128)(2,1)} %get-tuple-element.222.x0.refs_0_, bf16[256,512]{1,0:T(8,128)(2,1)} %get-tuple-element.223.x1.refs_1_, bf16[256,512]{1,0:T(8,128)(2,1)} %get-tuple-element.452.x0.refs_2_, ...), custom_call_target="tpu_custom_call" | custom-call | tf_op jit(solution)/shard_map/stack_grads/pallas_call | solution.py:294
  446.5 6.9 %collective-permute-done.46.refs_1_.refs_3_ = bf16[2,2,128,1024]{3,2,1,0:T(8,128)(2,1)S(1)} collective-permute-done((bf16[2,2,128,1024]{3,2,1,0:T(8,128)(2,1)}, bf16[2,2,128,1024]{3,2,1,0:T(8,128)(2,1)S(1)}, u32[]{:S(2)}, u32[]{:S(2)}) %collective-permute-start.46) | collective-permute-done | bytes 1048608 | tf_op jit(solution)/shard_map/ppermute | solution.py:596
  462.4 6.8 %back_natural.10 = f32[256,1024]{1,0:T(8,128)} custom-call(s32[8]{0:T(128)} %broadcast_xor_fusion.blocks, bf16[256,1024]{1,0:T(8,128)(2,1)} %get-tuple-element.379.refs_4_.refs_0_, bf16[256,1024]{1,0:T(8,128)(2,1)} %get-tuple-element.352.refs_5_.refs_1_, bf16[256,1024]{1,0:T(8,128)(2,1)} %get-tuple-element.380.refs_6_.refs_2_, ...), custom_call_target="tpu_custom_call" | custom-call | tf_op jit(solution)/shard_map/back_natural/pallas_call | solution.py:331
  488.5 15.2 %back_natural.11 = f32[2048,1024]{1,0:T(8,128)} custom-call(s32[8]{0:T(128)} %broadcast_xor_fusion.blocks, bf16[2048,1024]{1,0:T(8,128)(2,1)} %get-tuple-element.358.refs_7_.refs_0_, bf16[2048,1024]{1,0:T(8,128)(2,1)} %get-tuple-element.383.refs_8_.refs_1_, bf16[4,512,1024]{2,1,0:T(8,128)(2,1)} %copy-done, bf16[4,512,1024]{2,1,0:T(8,128)(2,1)} %copy-done.1, ...), custom_call_target="tpu_custom_call" | custom-call | tf_op jit(solution)/shard_map/back_natural/pallas_call | solution.py:331
  516.9 11.9 %collective-permute-done.58 = bf16[4,32,1024]{2,1,0:T(8,128)(2,1)S(1)} collective-permute-done((bf16[4,32,1024]{2,1,0:T(8,128)(2,1)S(1)}, bf16[4,32,1024]{2,1,0:T(8,128)(2,1)S(1)}, u32[]{:S(2)}, u32[]{:S(2)}) %collective-permute-start.58) | collective-permute-done | bytes 262176 | tf_op jit(solution)/shard_map/ppermute | solution.py:596
  543.1 9.1 %collective-permute-done.59 = bf16[4,2,32,1024]{3,2,0,1:T(8,128)(2,1)S(1)} collective-permute-done((bf16[4,2,32,1024]{3,2,0,1:T(8,128)(2,1)S(1)}, bf16[4,2,32,1024]{3,2,0,1:T(8,128)(2,1)S(1)}, u32[]{:S(2)}, u32[]{:S(2)}) %collective-permute-start.59) | collective-permute-done | bytes 524320 | tf_op jit(solution)/shard_map/ppermute | solution.py:596
  565.5 7.1 %collective-permute-done.60 = bf16[4,32,1024]{2,1,0:T(8,128)(2,1)S(1)} collective-permute-done((bf16[4,32,1024]{2,1,0:T(8,128)(2,1)S(1)}, bf16[4,32,1024]{2,1,0:T(8,128)(2,1)S(1)}, u32[]{:S(2)}, u32[]{:S(2)}) %collective-permute-start.60) | collective-permute-done | bytes 262176 | tf_op jit(solution)/shard_map/ppermute | solution.py:596
  (453 shorter events, 315.2 us)
Async XLA Ops:
  55.0 23.6 %collective-permute-start.10 = (bf16[2,2,128,1024]{3,2,1,0:T(8,128)(2,1)}, bf16[2,2,128,1024]{3,2,1,0:T(8,128)(2,1)}, u32[]{:S(2)}, u32[]{:S(2)}) collective-permute-start(bf16[2,2,128,1024]{3,2,1,0:T(8,128)(2,1)} %get-tuple-element.214), channel_id=1, source_target_pairs={{0,16},{1,17},{2,18},{3,19},{4,20},{5,21},{6,22},{7,23},{8,24},{9,... | collective-permute-start | bytes 3145736 | tf_op jit(solution)/shard_map/ppermute | solution.py:596
  55.5 23.3 %collective-permute-start.11 = (bf16[2,2,128,1024]{3,2,1,0:T(8,128)(2,1)}, bf16[2,2,128,1024]{3,2,1,0:T(8,128)(2,1)}, u32[]{:S(2)}, u32[]{:S(2)}) collective-permute-start(bf16[2,2,128,1024]{3,2,1,0:T(8,128)(2,1)} %get-tuple-element.215), channel_id=1, source_target_pairs={{0,8},{1,9},{2,10},{3,11},{4,12},{5,13},{6,14},{7,15},{8,0},{9,1},... | collective-permute-start | bytes 3145736 | tf_op jit(solution)/shard_map/ppermute | solution.py:596
  61.1 21.3 %collective-permute-start.3 = (bf16[4,2,32,1024]{3,2,1,0:T(8,128)(2,1)S(1)}, bf16[4,2,32,1024]{3,2,1,0:T(8,128)(2,1)S(1)}, u32[]{:S(2)}, u32[]{:S(2)}) collective-permute-start(bf16[4,2,32,1024]{3,2,1,0:T(8,128)(2,1)S(1)} %copy_bitcast_fusion), channel_id=1, source_target_pairs={{0,1},{1,0},{2,3},{3,2},{4,5},{5,4},{6,7},{7,6},{8,9},{9,8},{10,11... | collective-permute-start | bytes 1572872 | tf_op jit(solution)/shard_map/ppermute | solution.py:596
  102.8 31.6 %collective-permute-start.20 = (bf16[2,2,128,1024]{3,2,1,0:T(8,128)(2,1)}, bf16[2,2,128,1024]{3,2,1,0:T(8,128)(2,1)}, u32[]{:S(2)}, u32[]{:S(2)}) collective-permute-start(bf16[2,2,128,1024]{3,2,1,0:T(8,128)(2,1)} %get-tuple-element.230), channel_id=1, source_target_pairs={{0,16},{1,17},{2,18},{3,19},{4,20},{5,21},{6,22},{7,23},{8,24},{9,... | collective-permute-start | bytes 3145736 | tf_op jit(solution)/shard_map/ppermute | solution.py:596
  104.3 30.1 %collective-permute-start.21 = (bf16[2,2,128,1024]{3,2,1,0:T(8,128)(2,1)}, bf16[2,2,128,1024]{3,2,1,0:T(8,128)(2,1)}, u32[]{:S(2)}, u32[]{:S(2)}) collective-permute-start(bf16[2,2,128,1024]{3,2,1,0:T(8,128)(2,1)} %get-tuple-element.231), channel_id=1, source_target_pairs={{0,8},{1,9},{2,10},{3,11},{4,12},{5,13},{6,14},{7,15},{8,0},{9,1},... | collective-permute-start | bytes 3145736 | tf_op jit(solution)/shard_map/ppermute | solution.py:596
  138.0 18.9 %collective-permute-start.24 = (bf16[4,512,1024]{2,1,0:T(8,128)(2,1)S(1)}, bf16[4,512,1024]{2,1,0:T(8,128)(2,1)S(1)}, u32[]{:S(2)}, u32[]{:S(2)}) collective-permute-start(bf16[4,512,1024]{2,1,0:T(8,128)(2,1)S(1)} %pad_maximum_fusion.1.near.k0.v0.refs_1_.refs_2_.refs_4_), channel_id=1, source_target_pairs={{0,4},{1,5},{2,6},{3,7},{4,0},{5,1},{6,2},{7,3},{8,12},{9,13},{10,... | collective-permute-start | bytes 12582920 | tf_op jit(solution)/shard_map/ppermute | solution.py:596
  161.2 33.5 %collective-permute-start.25 = (bf16[2,1,128,2048]{3,2,1,0:T(8,128)(2,1)}, bf16[2,1,128,2048]{3,2,1,0:T(8,128)(2,1)}, u32[]{:S(2)}, u32[]{:S(2)}) collective-permute-start(bf16[2,1,128,2048]{3,2,1,0:T(8,128)(2,1)} %get-tuple-element.238), channel_id=1, source_target_pairs={{0,16},{1,17},{2,18},{3,19},{4,20},{5,21},{6,22},{7,23},{8,24},{9,... | collective-permute-start | bytes 3145736 | tf_op jit(solution)/shard_map/ppermute | solution.py:596
  161.7 33.0 %collective-permute-start.26 = (bf16[2,1,128,2048]{3,2,1,0:T(8,128)(2,1)}, bf16[2,1,128,2048]{3,2,1,0:T(8,128)(2,1)}, u32[]{:S(2)}, u32[]{:S(2)}) collective-permute-start(bf16[2,1,128,2048]{3,2,1,0:T(8,128)(2,1)} %get-tuple-element.239), channel_id=1, source_target_pairs={{0,8},{1,9},{2,10},{3,11},{4,12},{5,13},{6,14},{7,15},{8,0},{9,1},... | collective-permute-start | bytes 3145736 | tf_op jit(solution)/shard_map/ppermute | solution.py:596
  220.4 24.6 %collective-permute-start.30 = (bf16[2,1,512,512]{3,2,1,0:T(8,128)(2,1)}, bf16[2,1,512,512]{3,2,1,0:T(8,128)(2,1)S(1)}, u32[]{:S(2)}, u32[]{:S(2)}) collective-permute-start(bf16[2,1,512,512]{3,2,1,0:T(8,128)(2,1)} %get-tuple-element.262), channel_id=1, source_target_pairs={{0,16},{1,17},{2,18},{3,19},{4,20},{5,21},{6,22},{7,23},{8,24},{9,... | collective-permute-start | bytes 3145736 | tf_op jit(solution)/shard_map/ppermute | solution.py:596
  221.9 24.5 %collective-permute-start.31 = (bf16[2,1,512,512]{3,2,1,0:T(8,128)(2,1)}, bf16[2,1,512,512]{3,2,1,0:T(8,128)(2,1)}, u32[]{:S(2)}, u32[]{:S(2)}) collective-permute-start(bf16[2,1,512,512]{3,2,1,0:T(8,128)(2,1)} %get-tuple-element.263), channel_id=1, source_target_pairs={{0,8},{1,9},{2,10},{3,11},{4,12},{5,13},{6,14},{7,15},{8,0},{9,1},... | collective-permute-start | bytes 3145736 | tf_op jit(solution)/shard_map/ppermute | solution.py:596
  301.6 25.7 %collective-permute-start.34 = (bf16[1,2,512,512]{3,2,1,0:T(8,128)(2,1)}, bf16[1,2,512,512]{3,2,1,0:T(8,128)(2,1)S(1)}, u32[]{:S(2)}, u32[]{:S(2)}) collective-permute-start(bf16[1,2,512,512]{3,2,1,0:T(8,128)(2,1)} %get-tuple-element.278), channel_id=1, source_target_pairs={{0,16},{1,17},{2,18},{3,19},{4,20},{5,21},{6,22},{7,23},{8,24},{9,... | collective-permute-start | bytes 3145736 | tf_op jit(solution)/shard_map/ppermute | solution.py:596
  302.8 25.4 %collective-permute-start.35 = (bf16[1,2,512,512]{3,2,1,0:T(8,128)(2,1)}, bf16[1,2,512,512]{3,2,1,0:T(8,128)(2,1)S(1)}, u32[]{:S(2)}, u32[]{:S(2)}) collective-permute-start(bf16[1,2,512,512]{3,2,1,0:T(8,128)(2,1)} %get-tuple-element.279), channel_id=1, source_target_pairs={{0,8},{1,9},{2,10},{3,11},{4,12},{5,13},{6,14},{7,15},{8,0},{9,1},... | collective-permute-start | bytes 3145736 | tf_op jit(solution)/shard_map/ppermute | solution.py:596
  328.2 26.2 %collective-permute-start.36 = (bf16[2,512,2048]{2,1,0:T(8,128)(2,1)}, bf16[2,512,2048]{2,1,0:T(8,128)(2,1)}, u32[]{:S(2)}, u32[]{:S(2)}) collective-permute-start(bf16[2,512,2048]{2,1,0:T(8,128)(2,1)} %get-tuple-element.286), channel_id=1, source_target_pairs={{0,4},{1,5},{2,6},{3,7},{4,0},{5,1},{6,2},{7,3},{8,12},{9,13},{10,... | collective-permute-start | bytes 12582920 | tf_op jit(solution)/shard_map/ppermute | solution.py:596
  332.8 21.6 %collective-permute-start.37 = (bf16[1,1,512,512]{3,2,1,0:T(8,128)(2,1)}, bf16[1,1,512,512]{3,2,1,0:T(8,128)(2,1)S(1)}, u32[]{:S(2)}, u32[]{:S(2)}) collective-permute-start(bf16[1,1,512,512]{3,2,1,0:T(8,128)(2,1)} %get-tuple-element.295), channel_id=1, source_target_pairs={{0,8},{1,9},{2,10},{3,11},{4,12},{5,13},{6,14},{7,15},{8,0},{9,1},... | collective-permute-start | bytes 1572872 | tf_op jit(solution)/shard_map/ppermute | solution.py:596
  333.6 20.8 %collective-permute-start.38 = (bf16[1,1,512,512]{3,2,1,0:T(8,128)(2,1)}, bf16[1,1,512,512]{3,2,1,0:T(8,128)(2,1)S(1)}, u32[]{:S(2)}, u32[]{:S(2)}) collective-permute-start(bf16[1,1,512,512]{3,2,1,0:T(8,128)(2,1)} %get-tuple-element.296), channel_id=1, source_target_pairs={{0,16},{1,17},{2,18},{3,19},{4,20},{5,21},{6,22},{7,23},{8,24},{9,... | collective-permute-start | bytes 1572872 | tf_op jit(solution)/shard_map/ppermute | solution.py:596
  359.8 39.4 %collective-permute-start.39 = (bf16[1,2,128,2048]{3,2,1,0:T(8,128)(2,1)}, bf16[1,2,128,2048]{3,2,1,0:T(8,128)(2,1)S(1)}, u32[]{:S(2)}, u32[]{:S(2)}) collective-permute-start(bf16[1,2,128,2048]{3,2,1,0:T(8,128)(2,1)} %get-tuple-element.304), channel_id=1, source_target_pairs={{0,16},{1,17},{2,18},{3,19},{4,20},{5,21},{6,22},{7,23},{8,24},{9,... | collective-permute-start | bytes 3145736 | tf_op jit(solution)/shard_map/ppermute | solution.py:596
  361.0 38.2 %collective-permute-start.40 = (bf16[1,2,128,2048]{3,2,1,0:T(8,128)(2,1)}, bf16[1,2,128,2048]{3,2,1,0:T(8,128)(2,1)}, u32[]{:S(2)}, u32[]{:S(2)}) collective-permute-start(bf16[1,2,128,2048]{3,2,1,0:T(8,128)(2,1)} %get-tuple-element.305), channel_id=1, source_target_pairs={{0,8},{1,9},{2,10},{3,11},{4,12},{5,13},{6,14},{7,15},{8,0},{9,1},... | collective-permute-start | bytes 3145736 | tf_op jit(solution)/shard_map/ppermute | solution.py:596
  363.5 35.7 %collective-permute-start.41 = (bf16[2,2,128,512]{3,2,0,1:T(8,128)(2,1)}, bf16[2,2,128,512]{3,2,0,1:T(8,128)(2,1)}, u32[]{:S(2)}, u32[]{:S(2)}) collective-permute-start(bf16[2,2,128,512]{3,2,0,1:T(8,128)(2,1)} %fusion.1), channel_id=1, source_target_pairs={{0,1},{1,0},{2,3},{3,2},{4,5},{5,4},{6,7},{7,6},{8,9},{9,8},{10,11... | collective-permute-start | bytes 1572872 | tf_op jit(solution)/shard_map/ppermute | solution.py:596
  399.2 22.1 %collective-permute-start.42 = (bf16[4,512,1024]{2,1,0:T(8,128)(2,1)}, bf16[4,512,1024]{2,1,0:T(8,128)(2,1)}, u32[]{:S(2)}, u32[]{:S(2)}) collective-permute-start(bf16[4,512,1024]{2,1,0:T(8,128)(2,1)} %get-tuple-element.319), channel_id=1, source_target_pairs={{0,4},{1,5},{2,6},{3,7},{4,0},{5,1},{6,2},{7,3},{8,12},{9,13},{10,... | collective-permute-start | bytes 12582920 | tf_op jit(solution)/shard_map/ppermute | solution.py:596
  428.1 25.4 %collective-permute-start.46 = (bf16[2,2,128,1024]{3,2,1,0:T(8,128)(2,1)}, bf16[2,2,128,1024]{3,2,1,0:T(8,128)(2,1)S(1)}, u32[]{:S(2)}, u32[]{:S(2)}) collective-permute-start(bf16[2,2,128,1024]{3,2,1,0:T(8,128)(2,1)} %get-tuple-element.334), channel_id=1, source_target_pairs={{0,16},{1,17},{2,18},{3,19},{4,20},{5,21},{6,22},{7,23},{8,24},{9,... | collective-permute-start | bytes 3145736 | tf_op jit(solution)/shard_map/ppermute | solution.py:596
  429.3 25.1 %collective-permute-start.47 = (bf16[2,2,128,1024]{3,2,1,0:T(8,128)(2,1)}, bf16[2,2,128,1024]{3,2,1,0:T(8,128)(2,1)}, u32[]{:S(2)}, u32[]{:S(2)}) collective-permute-start(bf16[2,2,128,1024]{3,2,1,0:T(8,128)(2,1)} %get-tuple-element.335), channel_id=1, source_target_pairs={{0,8},{1,9},{2,10},{3,11},{4,12},{5,13},{6,14},{7,15},{8,0},{9,1},... | collective-permute-start | bytes 3145736 | tf_op jit(solution)/shard_map/ppermute | solution.py:596
  454.4 21.1 %collective-permute-start.51 = (bf16[4,512,1024]{2,1,0:T(8,128)(2,1)}, bf16[4,512,1024]{2,1,0:T(8,128)(2,1)}, u32[]{:S(2)}, u32[]{:S(2)}) collective-permute-start(bf16[4,512,1024]{2,1,0:T(8,128)(2,1)} %get-tuple-element.354), channel_id=1, source_target_pairs={{0,4},{1,5},{2,6},{3,7},{4,0},{5,1},{6,2},{7,3},{8,12},{9,13},{10,... | collective-permute-start | bytes 12582920 | tf_op jit(solution)/shard_map/ppermute | solution.py:596
  482.3 25.4 %collective-permute-start.53 = (bf16[2,2,128,1024]{3,2,1,0:T(8,128)(2,1)}, bf16[2,2,128,1024]{3,2,1,0:T(8,128)(2,1)S(1)}, u32[]{:S(2)}, u32[]{:S(2)}) collective-permute-start(bf16[2,2,128,1024]{3,2,1,0:T(8,128)(2,1)} %get-tuple-element.364), channel_id=1, source_target_pairs={{0,16},{1,17},{2,18},{3,19},{4,20},{5,21},{6,22},{7,23},{8,24},{9,... | collective-permute-start | bytes 3145736 | tf_op jit(solution)/shard_map/ppermute | solution.py:596
  483.5 25.1 %collective-permute-start.54 = (bf16[2,2,128,1024]{3,2,1,0:T(8,128)(2,1)}, bf16[2,2,128,1024]{3,2,1,0:T(8,128)(2,1)}, u32[]{:S(2)}, u32[]{:S(2)}) collective-permute-start(bf16[2,2,128,1024]{3,2,1,0:T(8,128)(2,1)} %get-tuple-element.365), channel_id=1, source_target_pairs={{0,8},{1,9},{2,10},{3,11},{4,12},{5,13},{6,14},{7,15},{8,0},{9,1},... | collective-permute-start | bytes 3145736 | tf_op jit(solution)/shard_map/ppermute | solution.py:596
  (113 other events, 772.7 us)

commit v6 on v5

--- a/solution.py
+++ b/solution.py
@@ -879,7 +879,7 @@
     cross_core = plan.step(crosses)
     for _ in plan.zs[1:]:
         fout_z = plan.step(fouts, fout_z)
-    last, _ = plan.step(fins, last, (cross_core, fout_z))
+    last, (_, _, first_rel) = plan.step(fins, last, (cross_core, fout_z, first_rel))
 
     queries_two = stack_project(first_rel, crosses.result, 0, (vectors, 5), (scaling,), BF)[0]
     mem_keys, mem_values = memory_project(mem_rel, crosses.result, 1, 2, (vectors, 6), 512)
@@ -941,12 +941,12 @@
             [(0, 0, 0, model_width), (1, 1, 0, model_width), (1, 2, 0, model_width), (2, 3, 0, model_width)],
         )
     )
-    d_queries = back([dq_scaled], crosses.result, [0], row_count)
     for _ in plan.zs[1:]:
         fout_last = plan.step(to_fout)
-    last, (d_queries, _, cross_sends) = plan.step(
-        to_fin, last, (d_queries, fout_last, to_cross.values())
-    )
+    last, (dq_late, _, cross_sends) = plan.step(
+        to_fin, last, (dq_scaled, fout_last, to_cross.values())
+    )
+    d_queries = back([dq_late], crosses.result, [0], row_count)
     to_cross.replace(cross_sends)
     cross_core = plan.step(to_cross)
     fout_last = plan.step(to_fout)

time: 580 us -> 572 us (0.986)
  waiting for transfers between devices: 149 us -> 141 us
    ppermute x66, waiting for transfers between devices: 149 us -> 141 us  [step(): lax.ppermute(v, AXES, [(i, i ^ m) for i in range(self.count)])]
  transfers between devices with their start and end apart: 66 -> 66, of which waited for: 35 -> 35; matrix products, arithmetic and copies ran while one was open for 10% -> 10% of each run, Pallas kernels for 36% -> 37%
where the time goes in v6:
time: 572 us; the launch traced here: 567 us
  Pallas kernels  253 us (44%)
  waiting for transfers between devices  141 us (25%)
  starting transfers between devices  61 us (11%)
  other arithmetic  56 us (10%)
  local copies, waits for them, and re-layouts  49 us (9%)
    ppermute x66, waiting for transfers between devices, step(): lax.ppermute(v, AXES, [(i, i ^ m) for i in range(self.count)])  141 us
    ppermute x66, starting transfers between devices, step(): lax.ppermute(v, AXES, [(i, i ^ m) for i in range(self.count)])  61 us
    pallas_call x4, Pallas kernels, cross_call(): pl.pallas_call(kernel, grid_spec=pltpu.PrefetchScalarGridSpec(num_scalar_...  47.1 us
    pallas_call x6, Pallas kernels, back_natural(): pl.pallas_call(back_kernel, grid_spec=pltpu.PrefetchScalarGridSpec(num_sc...  42.4 us
    pallas_call x4, Pallas kernels, stack_grads(): pl.pallas_call(functools.partial(grads_kernel, table), grid=(len(products...  37.1 us
    pallas_call x8, Pallas kernels, add_split(): pl.pallas_call(add_split_kernel, grid=shapes[0].shape[:2], in_specs=in_sp...  36.1 us
    pallas_call x3, Pallas kernels, norm_back(): pl.pallas_call(functools.partial(norm_back_kernel, len(cotangents)), grid...  20.6 us
    pallas_call x4, Pallas kernels, stack_project(): pl.pallas_call(functools.partial(project_kernel, scales), grid=(count,),...  16.1 us
  transfers between devices with their start and end apart: 66, of which 35 were waited for; matrix products, arithmetic and copies ran while one was open for 10% of the time, Pallas kernels for 37%

profile of v6, /device:TPU:0, one launch (start us, length us, event | category | flops | bytes accessed | tf_op | source)
XLA Modules:
  0.0 567.3 jit_solution(8616744926819100222)
XLA Ops:
  26.2 8.2 %collective-permute-done.1 = bf16[4,2,32,1024]{3,2,1,0:T(8,128)(2,1)S(1)} collective-permute-done((bf16[4,2,32,1024]{3,2,1,0:T(8,128)(2,1)S(1)}, bf16[4,2,32,1024]{3,2,1,0:T(8,128)(2,1)S(1)}, u32[]{:S(2)}, u32[]{:S(2)}) %collective-permute-start.1) | collective-permute-done | bytes 524320 | tf_op jit(solution)/shard_map/ppermute | solution.py:596
  61.1 17.4 %collective-permute-done.10 = bf16[2,2,128,1024]{3,2,1,0:T(8,128)(2,1)} collective-permute-done((bf16[2,2,128,1024]{3,2,1,0:T(8,128)(2,1)}, bf16[2,2,128,1024]{3,2,1,0:T(8,128)(2,1)}, u32[]{:S(2)}, u32[]{:S(2)}) %collective-permute-start.10) | collective-permute-done | bytes 1048608 | tf_op jit(solution)/shard_map/ppermute | solution.py:596
  87.4 10.1 %collective-permute-done.4 = bf16[1,1,32,4096]{3,2,1,0:T(8,128)(2,1)S(1)} collective-permute-done((bf16[1,1,32,4096]{3,2,1,0:T(8,128)(2,1)S(1)}, bf16[1,1,32,4096]{3,2,1,0:T(8,128)(2,1)S(1)}, u32[]{:S(2)}, u32[]{:S(2)}) %collective-permute-start.4) | collective-permute-done | bytes 262176 | tf_op jit(solution)/shard_map/ppermute | solution.py:596
  127.9 6.4 %collective-permute-done.18 = bf16[1,1,128,1024]{3,2,1,0:T(8,128)(2,1)} collective-permute-done((bf16[1,1,128,1024]{3,2,1,0:T(8,128)(2,1)}, bf16[1,1,128,1024]{3,2,1,0:T(8,128)(2,1)}, u32[]{:S(2)}, u32[]{:S(2)}) %collective-permute-start.18) | collective-permute-done | bytes 262176 | tf_op jit(solution)/shard_map/ppermute | solution.py:596
  148.0 8.7 %collective-permute-done.19 = bf16[1,2,128,1024]{3,2,1,0:T(8,128)(2,1)S(1)} collective-permute-done((bf16[1,2,128,1024]{3,2,1,0:T(8,128)(2,1)S(1)}, bf16[1,2,128,1024]{3,2,1,0:T(8,128)(2,1)S(1)}, u32[]{:S(2)}, u32[]{:S(2)}) %collective-permute-start.19) | collective-permute-done | bytes 524320 | tf_op jit(solution)/shard_map/ppermute | solution.py:596
  167.3 13.2 %memory_project.1 = (bf16[2048,1024]{1,0:T(8,128)(2,1)}, bf16[2048,1024]{1,0:T(8,128)(2,1)}) custom-call(bf16[2048,512]{1,0:T(8,128)(2,1)} %get-tuple-element.247.x0.refs_2_, bf16[2048,512]{1,0:T(8,128)(2,1)} %get-tuple-element.248.x1.refs_3_, bf16[4,512,1024]{2,1,0:T(8,128)(2,1)} %pad_maximum_fusion.1.near.k0.v0.refs_1_.refs_2_.refs_4_, ...), custom_call_target="tpu_custom_call" | custom-call | tf_op jit(solution)/shard_map/memory_project/pallas_call | solution.py:518
  180.5 11.4 %cross_attend.4 = (bf16[256,1024]{1,0:T(8,128)(2,1)}, f32[2,8,1,256]{3,2,1,0:T(1,128)}) custom-call(s32[8]{0:T(128)} %fusion.17.place.places, s32[1]{0:T(128)} %get-tuple-element.487.length, bf16[256,1024]{1,0:T(8,128)(2,1)} %bitcast.285, bf16[2048,1024]{1,0:T(8,128)(2,1)} %get-tuple-element.249.k, bf16[2048,1024]{1,0:T(8,128)(2,1)} %get-tuple-element.250.v), custom_call_target="tpu_custom_call" | custom-call | tf_op jit(solution)/shard_map/cross_attend/pallas_call | solution.py:128
  202.6 11.4 %cross_attend.5 = (bf16[256,1024]{1,0:T(8,128)(2,1)}, f32[2,8,1,256]{3,2,1,0:T(1,128)}) custom-call(s32[8]{0:T(128)} %fusion.17.place.places, s32[1]{0:T(128)} %get-tuple-element.486.length, bf16[256,1024]{1,0:T(8,128)(2,1)} %bitcast.286, bf16[2048,1024]{1,0:T(8,128)(2,1)} %get-tuple-element.249.k, ...), custom_call_target="tpu_custom_call", output_to_operand_aliasing={{0}: (5, {}), {1}: (6, {})} | custom-call | tf_op jit(solution)/shard_map/cross_attend/pallas_call | solution.py:128
  228.2 10.9 %ffn_up.1 = (bf16[256,4096]{1,0:T(8,128)(2,1)}, f32[256,4096]{1,0:T(8,128)}) custom-call(s32[8]{0:T(128)} %fusion.17.place.places, bf16[256,512]{1,0:T(8,128)(2,1)} %get-tuple-element.268.x0.refs_0_, bf16[256,512]{1,0:T(8,128)(2,1)} %get-tuple-element.269.x1.refs_1_, bf16[512,4096]{1,0:T(8,128)(2,1)} %get-tuple-element.402.near, ...), custom_call_target="tpu_custom_call" | custom-call | tf_op jit(solution)/shard_map/ffn_up/pallas_call | solution.py:454
  262.3 14.2 %norm_back.3 = (bf16[256,1024]{1,0:T(8,128)(2,1)}, f32[256,1024]{1,0:T(8,128)}, bf16[256,1024]{1,0:T(8,128)(2,1)}, f32[8,1024]{1,0:T(8,128)}) custom-call(bf16[256,1024]{1,0:T(8,128)(2,1)} %refs_0_.1, f32[256,1024]{1,0:T(8,128)} %add.267.refs_1_, f32[13,1,1024]{2,1,0:T(1,128)} %reshape.193.bias.gain.shift.refs_2_.refs_3_, ...), custom_call_target="tpu_custom_call" | custom-call | tf_op jit(solution)/shard_map/norm_back/pallas_call | solution.py:426
  282.9 10.5 %ffn_down_back.1.refs_0_.refs_2_ = bf16[256,4096]{1,0:T(8,128)(2,1)} custom-call(s32[8]{0:T(128)} %broadcast_xor_fusion.blocks, bf16[256,1024]{1,0:T(8,128)(2,1)} %get-tuple-element.277.refs_2_.cotangent, bf16[2048,1024]{1,0:T(8,128)(2,1)} %pad_maximum_fusion.3.near, bf16[2048,1024]{1,0:T(8,128)(2,1)} %collective-permute-done.32.far, ...), custom_call_target="tpu_custom_call" | custom-call | tf_op jit(solution)/shard_map/ffn_down_back/pallas_call | solution.py:489
  307.0 8.2 %back_natural.6.refs_1_ = f32[256,1024]{1,0:T(8,128)} custom-call(s32[8]{0:T(128)} %broadcast_xor_fusion.blocks, bf16[256,4096]{1,0:T(8,128)(2,1)} %ffn_down_back.1.refs_0_.refs_2_, bf16[1,512,4096]{2,1,0:T(8,128)(2,1)} %get-tuple-element.401.refs_1_, bf16[1,512,4096]{2,1,0:T(8,128)(2,1)} %bitcast.110.refs_2_), custom_call_target="tpu_custom_call" | custom-call | tf_op jit(solution)/shard_map/back_natural/pallas_call | solution.py:331
  315.1 9.2 %collective-permute-done.34.refs_1_.refs_3_ = bf16[1,2,512,512]{3,2,1,0:T(8,128)(2,1)S(1)} collective-permute-done((bf16[1,2,512,512]{3,2,1,0:T(8,128)(2,1)}, bf16[1,2,512,512]{3,2,1,0:T(8,128)(2,1)S(1)}, u32[]{:S(2)}, u32[]{:S(2)}) %collective-permute-start.34) | collective-permute-done | bytes 1048608 | tf_op jit(solution)/shard_map/ppermute | solution.py:596
  339.3 12.2 %cross_attend.6 = (bf16[256,1024]{1,0:T(8,128)(2,1)}, bf16[2048,1024]{1,0:T(8,128)(2,1)}, bf16[2048,1024]{1,0:T(8,128)(2,1)}) custom-call(s32[8]{0:T(128)} %fusion.17.place.places, s32[1]{0:T(128)} %get-tuple-element.487.length, bf16[256,1024]{1,0:T(8,128)(2,1)} %bitcast.287, bf16[2048,1024]{1,0:T(8,128)(2,1)} %get-tuple-element.249.k, ...), custom_call_target="tpu_custom_call" | custom-call | tf_op jit(solution)/shard_map/cross_attend/pallas_call | solution.py:128
  362.2 12.2 %cross_attend.7 = (bf16[256,1024]{1,0:T(8,128)(2,1)}, bf16[2048,1024]{1,0:T(8,128)(2,1)}, bf16[2048,1024]{1,0:T(8,128)(2,1)}) custom-call(s32[8]{0:T(128)} %fusion.17.place.places, s32[1]{0:T(128)} %get-tuple-element.486.length, bf16[256,1024]{1,0:T(8,128)(2,1)} %bitcast.288, ...), custom_call_target="tpu_custom_call", output_to_operand_aliasing={{0}: (7, {}), {1}: (8, {}), {2}: (9, {})} | custom-call | tf_op jit(solution)/shard_map/cross_attend/pallas_call | solution.py:128
  374.3 17.7 %stack_grads.6 = (bf16[4,512,1024]{2,1,0:T(8,128)(2,1)}, bf16[4,512,1024]{2,1,0:T(8,128)(2,1)}) custom-call(bf16[256,512]{1,0:T(8,128)(2,1)} %get-tuple-element.245.x0.refs_0_, bf16[256,512]{1,0:T(8,128)(2,1)} %get-tuple-element.246.x1.refs_1_, bf16[2048,512]{1,0:T(8,128)(2,1)} %get-tuple-element.247.x0.refs_2_, ...), custom_call_target="tpu_custom_call" | custom-call | tf_op jit(solution)/shard_map/stack_grads/pallas_call | solution.py:294
  424.9 7.9 %self_attend_back.1 = (bf16[256,1024]{1,0:T(8,128)(2,1)}, bf16[256,1024]{1,0:T(8,128)(2,1)}, bf16[256,1024]{1,0:T(8,128)(2,1)}) custom-call(s32[8]{0:T(128)} %fusion.17.place.places, bf16[3,256,1024]{2,1,0:T(8,128)(2,1)} %stack_project.4.q.k.v, bf16[3,256,1024]{2,1,0:T(8,128)(2,1)} %stack_project.4.q.k.v, bf16[3,256,1024]{2,1,0:T(8,128)(2,1)} %stack_project.4.q.k.v, ...), custom_call_target="tpu_custom_call" | custom-call | tf_op jit(solution)/shard_map/self_attend_back/pallas_call | solution.py:228
  432.8 6.8 %stack_grads.7 = (bf16[4,512,1024]{2,1,0:T(8,128)(2,1)}, bf16[4,512,1024]{2,1,0:T(8,128)(2,1)}) custom-call(bf16[256,512]{1,0:T(8,128)(2,1)} %get-tuple-element.224.x0.refs_0_, bf16[256,512]{1,0:T(8,128)(2,1)} %get-tuple-element.225.x1.refs_1_, bf16[256,512]{1,0:T(8,128)(2,1)} %get-tuple-element.456.x0.refs_2_, ...), custom_call_target="tpu_custom_call" | custom-call | tf_op jit(solution)/shard_map/stack_grads/pallas_call | solution.py:294
  439.6 6.7 %collective-permute-done.46.refs_1_.refs_3_ = bf16[2,2,128,1024]{3,2,1,0:T(8,128)(2,1)S(1)} collective-permute-done((bf16[2,2,128,1024]{3,2,1,0:T(8,128)(2,1)}, bf16[2,2,128,1024]{3,2,1,0:T(8,128)(2,1)S(1)}, u32[]{:S(2)}, u32[]{:S(2)}) %collective-permute-start.46) | collective-permute-done | bytes 1048608 | tf_op jit(solution)/shard_map/ppermute | solution.py:596
  455.2 6.8 %back_natural.10 = f32[256,1024]{1,0:T(8,128)} custom-call(s32[8]{0:T(128)} %broadcast_xor_fusion.blocks, bf16[256,1024]{1,0:T(8,128)(2,1)} %get-tuple-element.383.refs_4_.refs_0_, bf16[256,1024]{1,0:T(8,128)(2,1)} %get-tuple-element.356.refs_5_.refs_1_, bf16[256,1024]{1,0:T(8,128)(2,1)} %get-tuple-element.384.refs_6_.refs_2_, ...), custom_call_target="tpu_custom_call" | custom-call | tf_op jit(solution)/shard_map/back_natural/pallas_call | solution.py:331
  481.4 15.2 %back_natural.11 = f32[2048,1024]{1,0:T(8,128)} custom-call(s32[8]{0:T(128)} %broadcast_xor_fusion.blocks, bf16[2048,1024]{1,0:T(8,128)(2,1)} %get-tuple-element.362.refs_7_.refs_0_, bf16[2048,1024]{1,0:T(8,128)(2,1)} %get-tuple-element.387.refs_8_.refs_1_, bf16[4,512,1024]{2,1,0:T(8,128)(2,1)} %pad_maximum_fusion.1.near.k0.v0.refs_1_.refs_2_.refs_4_, ...), custom_call_target="tpu_custom_call" | custom-call | tf_op jit(solution)/shard_map/back_natural/pallas_call | solution.py:331
  509.7 12.0 %collective-permute-done.58 = bf16[4,32,1024]{2,1,0:T(8,128)(2,1)S(1)} collective-permute-done((bf16[4,32,1024]{2,1,0:T(8,128)(2,1)S(1)}, bf16[4,32,1024]{2,1,0:T(8,128)(2,1)S(1)}, u32[]{:S(2)}, u32[]{:S(2)}) %collective-permute-start.58) | collective-permute-done | bytes 262176 | tf_op jit(solution)/shard_map/ppermute | solution.py:596
  536.0 9.1 %collective-permute-done.59 = bf16[4,2,32,1024]{3,2,0,1:T(8,128)(2,1)S(1)} collective-permute-done((bf16[4,2,32,1024]{3,2,0,1:T(8,128)(2,1)S(1)}, bf16[4,2,32,1024]{3,2,0,1:T(8,128)(2,1)S(1)}, u32[]{:S(2)}, u32[]{:S(2)}) %collective-permute-start.59) | collective-permute-done | bytes 524320 | tf_op jit(solution)/shard_map/ppermute | solution.py:596
  558.4 7.1 %collective-permute-done.60 = bf16[4,32,1024]{2,1,0:T(8,128)(2,1)S(1)} collective-permute-done((bf16[4,32,1024]{2,1,0:T(8,128)(2,1)S(1)}, bf16[4,32,1024]{2,1,0:T(8,128)(2,1)S(1)}, u32[]{:S(2)}, u32[]{:S(2)}) %collective-permute-start.60) | collective-permute-done | bytes 262176 | tf_op jit(solution)/shard_map/ppermute | solution.py:596
  (453 shorter events, 311.7 us)
Async XLA Ops:
  55.0 23.6 %collective-permute-start.10 = (bf16[2,2,128,1024]{3,2,1,0:T(8,128)(2,1)}, bf16[2,2,128,1024]{3,2,1,0:T(8,128)(2,1)}, u32[]{:S(2)}, u32[]{:S(2)}) collective-permute-start(bf16[2,2,128,1024]{3,2,1,0:T(8,128)(2,1)} %get-tuple-element.216), channel_id=1, source_target_pairs={{0,16},{1,17},{2,18},{3,19},{4,20},{5,21},{6,22},{7,23},{8,24},{9,... | collective-permute-start | bytes 3145736 | tf_op jit(solution)/shard_map/ppermute | solution.py:596
  55.5 23.3 %collective-permute-start.11 = (bf16[2,2,128,1024]{3,2,1,0:T(8,128)(2,1)}, bf16[2,2,128,1024]{3,2,1,0:T(8,128)(2,1)}, u32[]{:S(2)}, u32[]{:S(2)}) collective-permute-start(bf16[2,2,128,1024]{3,2,1,0:T(8,128)(2,1)} %get-tuple-element.217), channel_id=1, source_target_pairs={{0,8},{1,9},{2,10},{3,11},{4,12},{5,13},{6,14},{7,15},{8,0},{9,1},... | collective-permute-start | bytes 3145736 | tf_op jit(solution)/shard_map/ppermute | solution.py:596
  61.1 21.3 %collective-permute-start.3 = (bf16[4,2,32,1024]{3,2,1,0:T(8,128)(2,1)S(1)}, bf16[4,2,32,1024]{3,2,1,0:T(8,128)(2,1)S(1)}, u32[]{:S(2)}, u32[]{:S(2)}) collective-permute-start(bf16[4,2,32,1024]{3,2,1,0:T(8,128)(2,1)S(1)} %copy_bitcast_fusion), channel_id=1, source_target_pairs={{0,1},{1,0},{2,3},{3,2},{4,5},{5,4},{6,7},{7,6},{8,9},{9,8},{10,11... | collective-permute-start | bytes 1572872 | tf_op jit(solution)/shard_map/ppermute | solution.py:596
  82.4 18.4 %collective-permute-start.17 = (bf16[4,512,1024]{2,1,0:T(8,128)(2,1)S(1)}, bf16[4,512,1024]{2,1,0:T(8,128)(2,1)S(1)}, u32[]{:S(2)}, u32[]{:S(2)}) collective-permute-start(bf16[4,512,1024]{2,1,0:T(8,128)(2,1)S(1)} %pad_maximum_fusion.near.refs_1_.refs_3_.refs_5_.refs_7_), channel_id=1, source_target_pairs={{0,4},{1,5},{2,6},{3,7},{4,0},{5,1},{6,2},{7,3},{8,12},{9,13},{10,... | collective-permute-start | bytes 12582920 | tf_op jit(solution)/shard_map/ppermute | solution.py:596
  102.8 31.6 %collective-permute-start.20 = (bf16[2,2,128,1024]{3,2,1,0:T(8,128)(2,1)}, bf16[2,2,128,1024]{3,2,1,0:T(8,128)(2,1)}, u32[]{:S(2)}, u32[]{:S(2)}) collective-permute-start(bf16[2,2,128,1024]{3,2,1,0:T(8,128)(2,1)} %get-tuple-element.232), channel_id=1, source_target_pairs={{0,16},{1,17},{2,18},{3,19},{4,20},{5,21},{6,22},{7,23},{8,24},{9,... | collective-permute-start | bytes 3145736 | tf_op jit(solution)/shard_map/ppermute | solution.py:596
  104.3 30.1 %collective-permute-start.21 = (bf16[2,2,128,1024]{3,2,1,0:T(8,128)(2,1)}, bf16[2,2,128,1024]{3,2,1,0:T(8,128)(2,1)}, u32[]{:S(2)}, u32[]{:S(2)}) collective-permute-start(bf16[2,2,128,1024]{3,2,1,0:T(8,128)(2,1)} %get-tuple-element.233), channel_id=1, source_target_pairs={{0,8},{1,9},{2,10},{3,11},{4,12},{5,13},{6,14},{7,15},{8,0},{9,1},... | collective-permute-start | bytes 3145736 | tf_op jit(solution)/shard_map/ppermute | solution.py:596
  162.1 29.7 %collective-permute-start.25 = (bf16[2,1,128,2048]{3,2,1,0:T(8,128)(2,1)}, bf16[2,1,128,2048]{3,2,1,0:T(8,128)(2,1)}, u32[]{:S(2)}, u32[]{:S(2)}) collective-permute-start(bf16[2,1,128,2048]{3,2,1,0:T(8,128)(2,1)} %get-tuple-element.243), channel_id=1, source_target_pairs={{0,16},{1,17},{2,18},{3,19},{4,20},{5,21},{6,22},{7,23},{8,24},{9,... | collective-permute-start | bytes 3145736 | tf_op jit(solution)/shard_map/ppermute | solution.py:596
  162.6 29.2 %collective-permute-start.26 = (bf16[2,1,128,2048]{3,2,1,0:T(8,128)(2,1)}, bf16[2,1,128,2048]{3,2,1,0:T(8,128)(2,1)}, u32[]{:S(2)}, u32[]{:S(2)}) collective-permute-start(bf16[2,1,128,2048]{3,2,1,0:T(8,128)(2,1)} %get-tuple-element.244), channel_id=1, source_target_pairs={{0,8},{1,9},{2,10},{3,11},{4,12},{5,13},{6,14},{7,15},{8,0},{9,1},... | collective-permute-start | bytes 3145736 | tf_op jit(solution)/shard_map/ppermute | solution.py:596
  217.4 24.6 %collective-permute-start.30 = (bf16[2,1,512,512]{3,2,1,0:T(8,128)(2,1)}, bf16[2,1,512,512]{3,2,1,0:T(8,128)(2,1)S(1)}, u32[]{:S(2)}, u32[]{:S(2)}) collective-permute-start(bf16[2,1,512,512]{3,2,1,0:T(8,128)(2,1)} %get-tuple-element.266), channel_id=1, source_target_pairs={{0,16},{1,17},{2,18},{3,19},{4,20},{5,21},{6,22},{7,23},{8,24},{9,... | collective-permute-start | bytes 3145736 | tf_op jit(solution)/shard_map/ppermute | solution.py:596
  218.9 24.5 %collective-permute-start.31 = (bf16[2,1,512,512]{3,2,1,0:T(8,128)(2,1)}, bf16[2,1,512,512]{3,2,1,0:T(8,128)(2,1)}, u32[]{:S(2)}, u32[]{:S(2)}) collective-permute-start(bf16[2,1,512,512]{3,2,1,0:T(8,128)(2,1)} %get-tuple-element.267), channel_id=1, source_target_pairs={{0,8},{1,9},{2,10},{3,11},{4,12},{5,13},{6,14},{7,15},{8,0},{9,1},... | collective-permute-start | bytes 3145736 | tf_op jit(solution)/shard_map/ppermute | solution.py:596
  298.6 25.7 %collective-permute-start.34 = (bf16[1,2,512,512]{3,2,1,0:T(8,128)(2,1)}, bf16[1,2,512,512]{3,2,1,0:T(8,128)(2,1)S(1)}, u32[]{:S(2)}, u32[]{:S(2)}) collective-permute-start(bf16[1,2,512,512]{3,2,1,0:T(8,128)(2,1)} %get-tuple-element.282), channel_id=1, source_target_pairs={{0,16},{1,17},{2,18},{3,19},{4,20},{5,21},{6,22},{7,23},{8,24},{9,... | collective-permute-start | bytes 3145736 | tf_op jit(solution)/shard_map/ppermute | solution.py:596
  299.8 25.4 %collective-permute-start.35 = (bf16[1,2,512,512]{3,2,1,0:T(8,128)(2,1)}, bf16[1,2,512,512]{3,2,1,0:T(8,128)(2,1)S(1)}, u32[]{:S(2)}, u32[]{:S(2)}) collective-permute-start(bf16[1,2,512,512]{3,2,1,0:T(8,128)(2,1)} %get-tuple-element.283), channel_id=1, source_target_pairs={{0,8},{1,9},{2,10},{3,11},{4,12},{5,13},{6,14},{7,15},{8,0},{9,1},... | collective-permute-start | bytes 3145736 | tf_op jit(solution)/shard_map/ppermute | solution.py:596
  325.2 26.3 %collective-permute-start.36 = (bf16[2,512,2048]{2,1,0:T(8,128)(2,1)}, bf16[2,512,2048]{2,1,0:T(8,128)(2,1)}, u32[]{:S(2)}, u32[]{:S(2)}) collective-permute-start(bf16[2,512,2048]{2,1,0:T(8,128)(2,1)} %get-tuple-element.290), channel_id=1, source_target_pairs={{0,4},{1,5},{2,6},{3,7},{4,0},{5,1},{6,2},{7,3},{8,12},{9,13},{10,... | collective-permute-start | bytes 12582920 | tf_op jit(solution)/shard_map/ppermute | solution.py:596
  329.8 21.6 %collective-permute-start.37 = (bf16[1,1,512,512]{3,2,1,0:T(8,128)(2,1)}, bf16[1,1,512,512]{3,2,1,0:T(8,128)(2,1)S(1)}, u32[]{:S(2)}, u32[]{:S(2)}) collective-permute-start(bf16[1,1,512,512]{3,2,1,0:T(8,128)(2,1)} %get-tuple-element.299), channel_id=1, source_target_pairs={{0,8},{1,9},{2,10},{3,11},{4,12},{5,13},{6,14},{7,15},{8,0},{9,1},... | collective-permute-start | bytes 1572872 | tf_op jit(solution)/shard_map/ppermute | solution.py:596
  330.7 20.8 %collective-permute-start.38 = (bf16[1,1,512,512]{3,2,1,0:T(8,128)(2,1)}, bf16[1,1,512,512]{3,2,1,0:T(8,128)(2,1)S(1)}, u32[]{:S(2)}, u32[]{:S(2)}) collective-permute-start(bf16[1,1,512,512]{3,2,1,0:T(8,128)(2,1)} %get-tuple-element.300), channel_id=1, source_target_pairs={{0,16},{1,17},{2,18},{3,19},{4,20},{5,21},{6,22},{7,23},{8,24},{9,... | collective-permute-start | bytes 1572872 | tf_op jit(solution)/shard_map/ppermute | solution.py:596
  356.9 35.1 %collective-permute-start.39 = (bf16[1,2,128,2048]{3,2,1,0:T(8,128)(2,1)}, bf16[1,2,128,2048]{3,2,1,0:T(8,128)(2,1)S(1)}, u32[]{:S(2)}, u32[]{:S(2)}) collective-permute-start(bf16[1,2,128,2048]{3,2,1,0:T(8,128)(2,1)} %get-tuple-element.308), channel_id=1, source_target_pairs={{0,16},{1,17},{2,18},{3,19},{4,20},{5,21},{6,22},{7,23},{8,24},{9,... | collective-permute-start | bytes 3145736 | tf_op jit(solution)/shard_map/ppermute | solution.py:596
  358.1 33.9 %collective-permute-start.40 = (bf16[1,2,128,2048]{3,2,1,0:T(8,128)(2,1)}, bf16[1,2,128,2048]{3,2,1,0:T(8,128)(2,1)}, u32[]{:S(2)}, u32[]{:S(2)}) collective-permute-start(bf16[1,2,128,2048]{3,2,1,0:T(8,128)(2,1)} %get-tuple-element.309), channel_id=1, source_target_pairs={{0,8},{1,9},{2,10},{3,11},{4,12},{5,13},{6,14},{7,15},{8,0},{9,1},... | collective-permute-start | bytes 3145736 | tf_op jit(solution)/shard_map/ppermute | solution.py:596
  360.5 31.5 %collective-permute-start.41 = (bf16[2,2,128,512]{3,2,0,1:T(8,128)(2,1)}, bf16[2,2,128,512]{3,2,0,1:T(8,128)(2,1)}, u32[]{:S(2)}, u32[]{:S(2)}) collective-permute-start(bf16[2,2,128,512]{3,2,0,1:T(8,128)(2,1)} %fusion.1), channel_id=1, source_target_pairs={{0,1},{1,0},{2,3},{3,2},{4,5},{5,4},{6,7},{7,6},{8,9},{9,8},{10,11... | collective-permute-start | bytes 1572872 | tf_op jit(solution)/shard_map/ppermute | solution.py:596
  392.0 22.2 %collective-permute-start.42 = (bf16[4,512,1024]{2,1,0:T(8,128)(2,1)}, bf16[4,512,1024]{2,1,0:T(8,128)(2,1)}, u32[]{:S(2)}, u32[]{:S(2)}) collective-permute-start(bf16[4,512,1024]{2,1,0:T(8,128)(2,1)} %get-tuple-element.323), channel_id=1, source_target_pairs={{0,4},{1,5},{2,6},{3,7},{4,0},{5,1},{6,2},{7,3},{8,12},{9,13},{10,... | collective-permute-start | bytes 12582920 | tf_op jit(solution)/shard_map/ppermute | solution.py:596
  421.0 25.4 %collective-permute-start.46 = (bf16[2,2,128,1024]{3,2,1,0:T(8,128)(2,1)}, bf16[2,2,128,1024]{3,2,1,0:T(8,128)(2,1)S(1)}, u32[]{:S(2)}, u32[]{:S(2)}) collective-permute-start(bf16[2,2,128,1024]{3,2,1,0:T(8,128)(2,1)} %get-tuple-element.338), channel_id=1, source_target_pairs={{0,16},{1,17},{2,18},{3,19},{4,20},{5,21},{6,22},{7,23},{8,24},{9,... | collective-permute-start | bytes 3145736 | tf_op jit(solution)/shard_map/ppermute | solution.py:596
  422.2 25.1 %collective-permute-start.47 = (bf16[2,2,128,1024]{3,2,1,0:T(8,128)(2,1)}, bf16[2,2,128,1024]{3,2,1,0:T(8,128)(2,1)}, u32[]{:S(2)}, u32[]{:S(2)}) collective-permute-start(bf16[2,2,128,1024]{3,2,1,0:T(8,128)(2,1)} %get-tuple-element.339), channel_id=1, source_target_pairs={{0,8},{1,9},{2,10},{3,11},{4,12},{5,13},{6,14},{7,15},{8,0},{9,1},... | collective-permute-start | bytes 3145736 | tf_op jit(solution)/shard_map/ppermute | solution.py:596
  447.3 21.2 %collective-permute-start.51 = (bf16[4,512,1024]{2,1,0:T(8,128)(2,1)}, bf16[4,512,1024]{2,1,0:T(8,128)(2,1)}, u32[]{:S(2)}, u32[]{:S(2)}) collective-permute-start(bf16[4,512,1024]{2,1,0:T(8,128)(2,1)} %get-tuple-element.358), channel_id=1, source_target_pairs={{0,4},{1,5},{2,6},{3,7},{4,0},{5,1},{6,2},{7,3},{8,12},{9,13},{10,... | collective-permute-start | bytes 12582920 | tf_op jit(solution)/shard_map/ppermute | solution.py:596
  475.2 25.4 %collective-permute-start.53 = (bf16[2,2,128,1024]{3,2,1,0:T(8,128)(2,1)}, bf16[2,2,128,1024]{3,2,1,0:T(8,128)(2,1)S(1)}, u32[]{:S(2)}, u32[]{:S(2)}) collective-permute-start(bf16[2,2,128,1024]{3,2,1,0:T(8,128)(2,1)} %get-tuple-element.368), channel_id=1, source_target_pairs={{0,16},{1,17},{2,18},{3,19},{4,20},{5,21},{6,22},{7,23},{8,24},{9,... | collective-permute-start | bytes 3145736 | tf_op jit(solution)/shard_map/ppermute | solution.py:596
  476.4 25.1 %collective-permute-start.54 = (bf16[2,2,128,1024]{3,2,1,0:T(8,128)(2,1)}, bf16[2,2,128,1024]{3,2,1,0:T(8,128)(2,1)}, u32[]{:S(2)}, u32[]{:S(2)}) collective-permute-start(bf16[2,2,128,1024]{3,2,1,0:T(8,128)(2,1)} %get-tuple-element.369), channel_id=1, source_target_pairs={{0,8},{1,9},{2,10},{3,11},{4,12},{5,13},{6,14},{7,15},{8,0},{9,1},... | collective-permute-start | bytes 3145736 | tf_op jit(solution)/shard_map/ppermute | solution.py:596
  (113 other events, 781.6 us)
